TPU v7x, 128 devices: a whole 4x4x4 slice. The times are simulated.
128 devices in a mesh: req: 32 (over x, z, core), mlp: 4 (over y).
Axes of the slice: x: 4, y: 4, z: 4, core: 2. Of those that a mesh axis runs over, the one named last changes fastest.
Arguments:
- queries: bfloat16 [16896, 2048], P('req', 'mlp'), may hold values from -6 to 6
- key_cache: bfloat16 [2560, 128, 1024], P('req', None, 'mlp'), may hold values from -6 to 6
- value_cache: bfloat16 [2560, 128, 1024], P('req', None, 'mlp'), may hold values from -6 to 6
- decode_len: int32 [512], P('req'), may hold values from 1 to 4096, as said below
- stretch_start: int32 [32], P('req'), may hold values from 0 to 3584, as said below
- page_table: int32 [544, 32], P('req'), may hold values from 0 to 79, as said below
- hidden_in: bfloat16 [16896, 2304], P('req')
- o_weight: bfloat16 [2048, 2304], P('mlp'), may hold values from -0.125 to 0.125
- attn_gain: float32 [2304], replicated, may hold values from 0.1 to 1.9
- ffn_in_gain: float32 [2304], replicated, may hold values from 0.1 to 1.9
- ffn_out_gain: float32 [2304], replicated, may hold values from 0.1 to 1.9
- w_gate: bfloat16 [2304, 9216], P('req', 'mlp'), may hold values from -0.125 to 0.125
- w_up: bfloat16 [2304, 9216], P('req', 'mlp'), may hold values from -0.125 to 0.125
- w_down: bfloat16 [2304, 9216], P('req', 'mlp')
Outputs:
- layer_out: bfloat16 [16896, 2304], P('req', 'mlp')
Inputs may be any that keep to these rules, and one draw needn't show every extreme that they name: `decode_len`: each decode request's tokens fill its first pages; request 1 of req index 1 holds 4096 tokens. `stretch_start`: req index 0 starts at 3584, req index 1 at 0. `page_table`: row j of req index r's block of 17 rows names request j's pages by slot in that index's own pool of 80 pages; the slots holding a req index's tokens are all distinct; entries past a request's last page are valid slots that hold none of its tokens.
All inputs are finite; a program needn't handle non-finite values.
Results may differ from a plain program's by a relative error of at most 0.014.
Values may be sent and summed in bfloat16 or wider, within the bound.
A program may use at most 128 MiB of HBM per device.

v0:
```python
import math

import jax
import jax.numpy as jnp
from jax import lax
from jax.sharding import PartitionSpec as P

H = 8
KVH = 4
HD = 256
PRE_DEV = 512
DEC_DEV = 16


EPS = 1e-06
CAP = 50.0


def rms(values, gain):
    return values * lax.rsqrt(jnp.mean(values * values, axis=-1, keepdims=True) + EPS) * gain


def capped_weight(scores, visible):
    capped = CAP * jnp.tanh(scores / (16.0 * CAP))
    return jnp.where(visible, jnp.exp(capped), jnp.float32(0.0))


def attend(queries, key_cache, value_cache, decode_len, stretch_start, page_table):
    rows = queries.shape[0]
    local_kv = key_cache.shape[2] // HD
    rep = H // KVH
    page_len = key_cache.shape[1]
    max_pages = page_table.shape[1]
    requests = page_table.shape[0]
    block = math.gcd(max_pages, max(1, 512 // page_len))
    span = block * page_len
    query = queries.reshape(rows, local_kv, rep, HD)
    pre_q = query[:PRE_DEV]
    dec_q = query[PRE_DEV:]
    start = stretch_start[0]
    limit = start + jnp.arange(PRE_DEV, dtype=jnp.int32) + 1
    need = jnp.maximum(
        (start + PRE_DEV + page_len - 1) // page_len,
        jnp.max((decode_len + page_len - 1) // page_len),
    )
    blocks = (need + block - 1) // block

    def step(index, carry):
        pre_num, pre_den, dec_num, dec_den = carry
        slots = lax.dynamic_slice_in_dim(page_table, index * block, block, 1)
        keys = key_cache[slots].reshape(requests, span, local_kv, HD)
        vals = value_cache[slots].reshape(requests, span, local_kv, HD)
        position = index * span + jnp.arange(span, dtype=jnp.int32)
        pre_scores = jnp.einsum(
            "rghd,tgd->rght", pre_q, keys[0], preferred_element_type=jnp.float32
        )
        pre_weight = capped_weight(
            pre_scores, position[None, None, None, :] < limit[:, None, None, None]
        )
        pre_num = pre_num + jnp.einsum(
            "rght,tgd->rghd",
            pre_weight.astype(jnp.bfloat16),
            vals[0],
            preferred_element_type=jnp.float32,
        )
        pre_den = pre_den + jnp.sum(pre_weight, axis=-1)
        dec_scores = jnp.einsum(
            "rghd,rtgd->rght", dec_q, keys[1:], preferred_element_type=jnp.float32
        )
        dec_weight = capped_weight(
            dec_scores, position[None, None, None, :] < decode_len[:, None, None, None]
        )
        dec_num = dec_num + jnp.einsum(
            "rght,rtgd->rghd",
            dec_weight.astype(jnp.bfloat16),
            vals[1:],
            preferred_element_type=jnp.float32,
        )
        dec_den = dec_den + jnp.sum(dec_weight, axis=-1)
        return (pre_num, pre_den, dec_num, dec_den)

    start_carry = (
        jnp.zeros((PRE_DEV, local_kv, rep, HD), jnp.float32),
        jnp.zeros((PRE_DEV, local_kv, rep), jnp.float32),
        jnp.zeros((DEC_DEV, local_kv, rep, HD), jnp.float32),
        jnp.zeros((DEC_DEV, local_kv, rep), jnp.float32),
    )
    pre_num, pre_den, dec_num, dec_den = lax.fori_loop(0, blocks, step, start_carry)
    pre_out = (pre_num / pre_den[..., None]).astype(jnp.bfloat16)
    dec_out = (dec_num / dec_den[..., None]).astype(jnp.bfloat16)
    return jnp.concatenate([pre_out, dec_out], axis=0).reshape(rows, local_kv * rep * HD)


def per_device(
    queries,
    key_cache,
    value_cache,
    decode_len,
    stretch_start,
    page_table,
    hidden_in,
    o_weight,
    attn_gain,
    ffn_in_gain,
    ffn_out_gain,
    w_gate,
    w_up,
    w_down,
):
    attended = attend(queries, key_cache, value_cache, decode_len, stretch_start, page_table)
    projected = lax.psum(
        jnp.dot(attended, o_weight, preferred_element_type=jnp.float32).astype(jnp.bfloat16), "mlp"
    ).astype(jnp.float32)
    resid = hidden_in.astype(jnp.float32) + rms(projected, attn_gain)
    normed = rms(resid, ffn_in_gain).astype(jnp.bfloat16)
    gate = jnp.dot(
        normed,
        lax.all_gather(w_gate, "req", axis=0, tiled=True),
        preferred_element_type=jnp.float32,
    )
    up_part = jnp.dot(
        normed, lax.all_gather(w_up, "req", axis=0, tiled=True), preferred_element_type=jnp.float32
    )
    act = (jax.nn.gelu(gate, approximate=True) * up_part).astype(jnp.bfloat16)
    partial_out = lax.dot_general(
        act,
        lax.all_gather(w_down, "req", axis=0, tiled=True),
        (((1,), (1,)), ((), ())),
        preferred_element_type=jnp.float32,
    )
    width = hidden_in.shape[1] // lax.axis_size("mlp")
    first = lax.axis_index("mlp") * width
    total = lax.psum(partial_out.astype(jnp.bfloat16), "mlp").astype(jnp.float32)
    combined = resid + rms(total, ffn_out_gain)
    result = lax.dynamic_slice_in_dim(combined, first, width, 1)
    return result.astype(jnp.bfloat16)


def solution(mesh):
    return jax.shard_map(
        per_device,
        mesh=mesh,
        in_specs=(
            P("req", "mlp"),
            P("req", None, "mlp"),
            P("req", None, "mlp"),
            P("req"),
            P("req"),
            P("req", None),
            P("req", None),
            P("mlp", None),
            P(),
            P(),
            P(),
            P("req", "mlp"),
            P("req", "mlp"),
            P("req", "mlp"),
        ),
        out_specs=P("req", "mlp"),
        check_vma=False,
    )
```

profile of v0, /device:TPU:1, one launch (start us, length us, event | category | flops | bytes accessed | tf_op | source)
XLA Modules:
  0.0 543.3 jit_solution(7240394064184673819)
XLA Ops:
  13.4 251.4 %while.17 = (s32[]{:T(128)}, f32[512,1,2,256]{0,3,2,1:T(8,128)S(1)}, f32[512,1,2]{0,2,1:T(2,128)S(1)}, f32[16,1,2,256]{3,2,0,1:T(2,128)S(1)}, f32[16,1,2]{0,2,1:...) while((s32[]{:T(128)}, ...), condition=%wide.region_4.5_spmd.clone, body=%wide.region_1.4_spmd.clone.sunk | while | flops 556894976 | bytes 58393828 | solution.py:88
  14.3 7.8 %gather_fusion.1 = bf16[68,128,256]{2,1,0:T(8,128)(2,1)} fusion(bf16[80,128,256]{2,1,0:T(8,128)(2,1)} %get-tuple-element.310, s32[1024]{0:T(1024)S(1)} %pad_clamp_fusion.2), kind=kCustom, calls=%fused_computation.1.clone.clone.1 | custom fusion | bytes 8913168 | tf_op jit(solution)/shard_map/while/body/gather | solution.py:51
  24.7 3.0 fusion.59
  27.7 7.9 %gather_fusion = bf16[68,128,256]{2,1,0:T(8,128)(2,1)} fusion(bf16[80,128,256]{2,1,0:T(8,128)(2,1)} %get-tuple-element.309, s32[1024]{0:T(1024)S(1)} %pad_clamp_fusion.2), kind=kCustom, calls=%fused_computation.clone.clone.1 | custom fusion | bytes 8913168 | tf_op jit(solution)/shard_map/while/body/gather | solution.py:52
  41.8 2.2 slice-done.1
  45.7 7.8 %gather_fusion.1 = bf16[68,128,256]{2,1,0:T(8,128)(2,1)} fusion(bf16[80,128,256]{2,1,0:T(8,128)(2,1)} %get-tuple-element.310, s32[1024]{0:T(1024)S(1)} %pad_clamp_fusion.2), kind=kCustom, calls=%fused_computation.1.clone.clone.1 | custom fusion | bytes 8913168 | tf_op jit(solution)/shard_map/while/body/gather | solution.py:51
  56.1 3.0 fusion.59
  59.1 7.9 %gather_fusion = bf16[68,128,256]{2,1,0:T(8,128)(2,1)} fusion(bf16[80,128,256]{2,1,0:T(8,128)(2,1)} %get-tuple-element.309, s32[1024]{0:T(1024)S(1)} %pad_clamp_fusion.2), kind=kCustom, calls=%fused_computation.clone.clone.1 | custom fusion | bytes 8913168 | tf_op jit(solution)/shard_map/while/body/gather | solution.py:52
  68.0 1.7 fusion.60
  73.2 2.2 slice-done.1
  77.1 7.8 %gather_fusion.1 = bf16[68,128,256]{2,1,0:T(8,128)(2,1)} fusion(bf16[80,128,256]{2,1,0:T(8,128)(2,1)} %get-tuple-element.310, s32[1024]{0:T(1024)S(1)} %pad_clamp_fusion.2), kind=kCustom, calls=%fused_computation.1.clone.clone.1 | custom fusion | bytes 8913168 | tf_op jit(solution)/shard_map/while/body/gather | solution.py:51
  87.5 3.0 fusion.59
  90.5 7.9 %gather_fusion = bf16[68,128,256]{2,1,0:T(8,128)(2,1)} fusion(bf16[80,128,256]{2,1,0:T(8,128)(2,1)} %get-tuple-element.309, s32[1024]{0:T(1024)S(1)} %pad_clamp_fusion.2), kind=kCustom, calls=%fused_computation.clone.clone.1 | custom fusion | bytes 8913168 | tf_op jit(solution)/shard_map/while/body/gather | solution.py:52
  104.6 2.2 slice-done.1
  108.5 7.9 %gather_fusion.1 = bf16[68,128,256]{2,1,0:T(8,128)(2,1)} fusion(bf16[80,128,256]{2,1,0:T(8,128)(2,1)} %get-tuple-element.310, s32[1024]{0:T(1024)S(1)} %pad_clamp_fusion.2), kind=kCustom, calls=%fused_computation.1.clone.clone.1 | custom fusion | bytes 8913168 | tf_op jit(solution)/shard_map/while/body/gather | solution.py:51
  118.9 3.0 fusion.59
  121.9 7.9 %gather_fusion = bf16[68,128,256]{2,1,0:T(8,128)(2,1)} fusion(bf16[80,128,256]{2,1,0:T(8,128)(2,1)} %get-tuple-element.309, s32[1024]{0:T(1024)S(1)} %pad_clamp_fusion.2), kind=kCustom, calls=%fused_computation.clone.clone.1 | custom fusion | bytes 8913168 | tf_op jit(solution)/shard_map/while/body/gather | solution.py:52
  136.0 2.2 slice-done.1
  139.9 7.9 %gather_fusion.1 = bf16[68,128,256]{2,1,0:T(8,128)(2,1)} fusion(bf16[80,128,256]{2,1,0:T(8,128)(2,1)} %get-tuple-element.310, s32[1024]{0:T(1024)S(1)} %pad_clamp_fusion.2), kind=kCustom, calls=%fused_computation.1.clone.clone.1 | custom fusion | bytes 8913168 | tf_op jit(solution)/shard_map/while/body/gather | solution.py:51
  150.3 3.1 fusion.59
  153.4 7.9 %gather_fusion = bf16[68,128,256]{2,1,0:T(8,128)(2,1)} fusion(bf16[80,128,256]{2,1,0:T(8,128)(2,1)} %get-tuple-element.309, s32[1024]{0:T(1024)S(1)} %pad_clamp_fusion.2), kind=kCustom, calls=%fused_computation.clone.clone.1 | custom fusion | bytes 8913168 | tf_op jit(solution)/shard_map/while/body/gather | solution.py:52
  167.5 2.2 slice-done.1
  171.3 7.9 %gather_fusion.1 = bf16[68,128,256]{2,1,0:T(8,128)(2,1)} fusion(bf16[80,128,256]{2,1,0:T(8,128)(2,1)} %get-tuple-element.310, s32[1024]{0:T(1024)S(1)} %pad_clamp_fusion.2), kind=kCustom, calls=%fused_computation.1.clone.clone.1 | custom fusion | bytes 8913168 | tf_op jit(solution)/shard_map/while/body/gather | solution.py:51
  181.8 3.0 fusion.59
  184.8 7.9 %gather_fusion = bf16[68,128,256]{2,1,0:T(8,128)(2,1)} fusion(bf16[80,128,256]{2,1,0:T(8,128)(2,1)} %get-tuple-element.309, s32[1024]{0:T(1024)S(1)} %pad_clamp_fusion.2), kind=kCustom, calls=%fused_computation.clone.clone.1 | custom fusion | bytes 8913168 | tf_op jit(solution)/shard_map/while/body/gather | solution.py:52
  193.7 1.7 fusion.60
  198.9 2.2 slice-done.1
  202.8 7.9 %gather_fusion.1 = bf16[68,128,256]{2,1,0:T(8,128)(2,1)} fusion(bf16[80,128,256]{2,1,0:T(8,128)(2,1)} %get-tuple-element.310, s32[1024]{0:T(1024)S(1)} %pad_clamp_fusion.2), kind=kCustom, calls=%fused_computation.1.clone.clone.1 | custom fusion | bytes 8913168 | tf_op jit(solution)/shard_map/while/body/gather | solution.py:51
  213.2 3.0 fusion.59
  216.3 7.9 %gather_fusion = bf16[68,128,256]{2,1,0:T(8,128)(2,1)} fusion(bf16[80,128,256]{2,1,0:T(8,128)(2,1)} %get-tuple-element.309, s32[1024]{0:T(1024)S(1)} %pad_clamp_fusion.2), kind=kCustom, calls=%fused_computation.clone.clone.1 | custom fusion | bytes 8913168 | tf_op jit(solution)/shard_map/while/body/gather | solution.py:52
  230.4 2.2 slice-done.1
  234.2 7.9 %gather_fusion.1 = bf16[68,128,256]{2,1,0:T(8,128)(2,1)} fusion(bf16[80,128,256]{2,1,0:T(8,128)(2,1)} %get-tuple-element.310, s32[1024]{0:T(1024)S(1)} %pad_clamp_fusion.2), kind=kCustom, calls=%fused_computation.1.clone.clone.1 | custom fusion | bytes 8913168 | tf_op jit(solution)/shard_map/while/body/gather | solution.py:51
  244.6 3.0 fusion.59
  247.7 7.9 %gather_fusion = bf16[68,128,256]{2,1,0:T(8,128)(2,1)} fusion(bf16[80,128,256]{2,1,0:T(8,128)(2,1)} %get-tuple-element.309, s32[1024]{0:T(1024)S(1)} %pad_clamp_fusion.2), kind=kCustom, calls=%fused_computation.clone.clone.1 | custom fusion | bytes 8913168 | tf_op jit(solution)/shard_map/while/body/gather | solution.py:52
  261.8 2.2 slice-done.1
  266.6 2.9 convolution_convert_fusion.1
  271.5 65.2 %all-reduce.3.cloned.1.call-done = bf16[528,2304]{1,0:T(8,128)(2,1)} async-done(((bf16[528,2304]{1,0:T(8,128)(2,1)}), bf16[528,2304]{1,0:T(8,128)(2,1)}) %all-reduce.3.cloned.1.call-update) | async-done | bytes 2433040 | tf_op jit(solution)/shard_map/psum | solution.py:111
  336.7 2.2 fusion.14
  338.9 5.8 %multiply_reduce_fusion.1 = (f32[528]{0:T(1024)S(1)}, f32[528,2304]{1,0:T(8,128)}) fusion(f32[2304]{0:T(1024)S(1)} %copy-done.3, f32[528]{0:T(1024)S(1)} %add_rsqrt_fusion.2, bf16[528,2304]{1,0:T(8,128)(2,1)} %all-reduce.3.cloned.1.call-done, bf16[528,2304]{1,0:T(8,128)(2,1)} %param.22), kind=kLoop, calls=%fused_computation.43 | loop fusion | flops 8515056 | bytes 9745536 | tf_op jit(solution)/shard_map/reduce_sum | solution.py:20
  344.7 12.5 %fusion.28 = f32[528,2304]{1,0:T(8,128)} fusion(bf16[2304,2304]{1,0:T(8,128)(2,1)} %all-gather.4.cloned.1.call-done, f32[528,2304]{1,0:T(8,128)} %get-tuple-element.163, f32[2304]{0:T(1024)S(1)} %copy-done.4, f32[528]{0:T(1024)S(1)} %add_rsqrt_fusion.1), kind=kOutput, calls=%fused_computation.62 | convolution fusion | flops 5609336832 | bytes 20360256 | tf_op jit(solution)/shard_map/dot_general | solution.py:116
  357.2 36.2 %all-gather.6.cloned.1.call-done = bf16[2304,2304]{1,0:T(8,128)(2,1)} async-done(((bf16[72,2304]{1,0:T(8,128)(2,1)}), bf16[2304,2304]{1,0:T(8,128)(2,1)}) %all-gather.6.cloned.1.call-update) | async-done | bytes 10616848 | tf_op jit(solution)/shard_map/all_gather | solution.py:122
  393.4 12.9 %fusion.24 = bf16[528,2304]{1,0:T(8,128)(2,1)} fusion(bf16[2304,2304]{1,0:T(8,128)(2,1)} %all-gather.6.cloned.1.call-done, f32[528,2304]{1,0:T(8,128)} %fusion.28, f32[528,2304]{1,0:T(8,128)} %get-tuple-element.163, f32[2304]{0:T(1024)S(1)} %copy-done.4, f32[528]{0:T(1024)S(1)} %add_rsqrt_fusion.1), kind=kOutput, calls=%fused_computation.44 | convolution fusion | flops 5621501952 | bytes 22793280 | tf_op jit(solution)/shard_map/dot_general | solution.py:121
  406.3 46.8 %all-gather.8.cloned.1.call-done = bf16[2304,2304]{1,0:T(8,128)(2,1)} async-done(((bf16[72,2304]{1,0:T(8,128)(2,1)}), bf16[2304,2304]{1,0:T(8,128)(2,1)}) %all-gather.8.cloned.1.call-update) | async-done | bytes 10616848 | tf_op jit(solution)/shard_map/all_gather | solution.py:127
  453.1 11.6 %convolution_convert_fusion = bf16[528,2304]{1,0:T(8,128)(2,1)} fusion(bf16[528,2304]{1,0:T(8,128)(2,1)} %fusion.24, bf16[2304,2304]{1,0:T(8,128)(2,1)} %all-gather.8.cloned.1.call-done), kind=kOutput, calls=%fused_computation.45 | convolution fusion | flops 5606903808 | bytes 15482880 | tf_op jit(solution)/shard_map/dot_general | solution.py:125
  465.5 62.5 %all-reduce.5.cloned.1.call-done = bf16[528,2304]{1,0:T(8,128)(2,1)} async-done(((bf16[528,2304]{1,0:T(8,128)(2,1)}), bf16[528,2304]{1,0:T(8,128)(2,1)}) %all-reduce.5.cloned.1.call-update) | async-done | bytes 2433040 | tf_op jit(solution)/shard_map/psum | solution.py:133
  528.0 2.2 multiply_reduce_fusion
  530.3 2.2 convert_element_type.45
  532.5 3.2 fusion.25
  (188 shorter events, 88.3 us)
Async XLA Ops:
  7.4 259.2 %copy-start = (bf16[512,2304]{1,0:T(8,128)(2,1)S(1)}, bf16[512,2304]{1,0:T(8,128)(2,1)}, u32[]{:S(2)}) copy-start(bf16[512,2304]{1,0:T(8,128)(2,1)} %param.23) | copy-start | bytes 7077892
  7.4 329.3 %all-reduce.3.cloned.1.call-start = ((), (), s32[]{:S(2)}) async-start(), calls=%async_computation | async-start | bytes 4866048 | tf_op jit(solution)/shard_map/psum | solution.py:111
  38.3 0.7 copy-start.2
  38.3 2.2 slice-start
  41.8 2.2 slice-start.1
  69.7 0.7 copy-start.2
  69.7 2.2 slice-start
  73.2 2.2 slice-start.1
  101.1 0.7 copy-start.2
  101.1 2.2 slice-start
  104.6 2.2 slice-start.1
  132.5 0.7 copy-start.2
  132.6 2.2 slice-start
  136.0 2.2 slice-start.1
  164.0 0.7 copy-start.2
  164.0 2.2 slice-start
  167.5 2.2 slice-start.1
  195.4 0.7 copy-start.2
  195.4 2.2 slice-start
  198.9 2.2 slice-start.1
  226.9 0.7 copy-start.2
  226.9 2.2 slice-start
  230.4 2.2 slice-start.1
  258.3 0.7 copy-start.2
  258.3 2.2 slice-start
  261.8 2.2 slice-start.1
  269.5 69.4 %copy-start.3 = (f32[2304]{0:T(1024)S(1)}, f32[2304]{0:T(1024)}, u32[]{:S(2)}) copy-start(f32[2304]{0:T(1024)} %param.24) | copy-start | bytes 27652
  269.5 75.2 %all-gather.4.cloned.1.call-start = ((), (), s32[]{:S(2)}) async-start(), calls=%async_computation.1 | async-start | bytes 10948608 | tf_op jit(solution)/shard_map/all_gather | solution.py:118
  270.1 123.3 %all-gather.6.cloned.1.call-start = ((), (), s32[]{:S(2)}) async-start(), calls=%async_computation.2 | async-start | bytes 10948608 | tf_op jit(solution)/shard_map/all_gather | solution.py:122
  270.7 182.4 %all-gather.8.cloned.1.call-start = ((), (), s32[]{:S(2)}) async-start(), calls=%async_computation.3 | async-start | bytes 10948608 | tf_op jit(solution)/shard_map/all_gather | solution.py:127
  271.3 256.8 %all-reduce.5.cloned.1.call-start = ((), (), s32[]{:S(2)}) async-start(), calls=%async_computation.4 | async-start | bytes 4866048 | tf_op jit(solution)/shard_map/psum | solution.py:133
  338.9 5.8 %copy-start.4 = (f32[2304]{0:T(1024)S(1)}, f32[2304]{0:T(1024)}, u32[]{:S(2)}) copy-start(f32[2304]{0:T(1024)} %param.25) | copy-start | bytes 27652
  530.3 5.4 copy-start.1
Sparse Core Ops, SparseCore 0:
  269.7 66.9 all-reduce.2
  464.8 63.1 all-reduce.4
Sparse Core Ops, SparseCore 1:
  272.4 61.3 all-gather.3
  335.9 57.5 all-gather.5
  395.6 57.4 all-gather.7
where the time goes:
time: 546 us; the launch traced here: 543 us
  waiting for transfers between devices  212 us (39%)
  local copies, waits for them, and re-layouts  188 us (34%)
  matrix products  93.3 us (17%)
  other arithmetic  31.8 us (6%)
  between operations  16.6 us (3%)
    psum x1, waiting for transfers between devices, per_device(): lax.psum(jnp.dot(attended, o_weight, preferred_element_type=jnp.float32)....  65.2 us
    gather x8, local copies, waits for them, and re-layouts, step(): vals = value_cache[slots].reshape(requests, span, local_kv, HD)  63.5 us
    gather x8, local copies, waits for them, and re-layouts, step(): keys = key_cache[slots].reshape(requests, span, local_kv, HD)  62.9 us
    psum x1, waiting for transfers between devices, per_device(): lax.psum(partial_out.astype(jnp.bfloat16), 'mlp').astype(jnp.float32)  62.5 us
    all_gather x1, waiting for transfers between devices, per_device(): lax.all_gather(w_down, 'req', axis=0, tiled=True)  46.8 us
    all_gather x1, waiting for transfers between devices, per_device(): lax.all_gather(w_up, 'req', axis=0, tiled=True)  36.2 us
    dot_general x8, matrix products, step(): jnp.einsum('rghd,tgd->rght', pre_q, keys[0], preferred_element_type=jnp.f...  24.4 us
    slice x16, local copies, waits for them, and re-layouts, step(): vals[1:]  17.6 us
  transfers between devices with their start and end apart: 5, of which 4 were waited for; matrix products, arithmetic and copies ran while one was open for 6% of the time, Pallas kernels for 0%

commit v1 on v0

--- a/solution.py
+++ b/solution.py
@@ -29,63 +29,58 @@
     rows = queries.shape[0]
     local_kv = key_cache.shape[2] // HD
     rep = H // KVH
+    pool = key_cache.shape[0]
     page_len = key_cache.shape[1]
     max_pages = page_table.shape[1]
-    requests = page_table.shape[0]
-    block = math.gcd(max_pages, max(1, 512 // page_len))
-    span = block * page_len
     query = queries.reshape(rows, local_kv, rep, HD)
     pre_q = query[:PRE_DEV]
     dec_q = query[PRE_DEV:]
     start = stretch_start[0]
+
+    pre_keys = key_cache[page_table[0]].reshape(max_pages * page_len, local_kv, HD)
+    pre_vals = value_cache[page_table[0]].reshape(max_pages * page_len, local_kv, HD)
+    position = jnp.arange(max_pages * page_len, dtype=jnp.int32)
     limit = start + jnp.arange(PRE_DEV, dtype=jnp.int32) + 1
-    need = jnp.maximum(
-        (start + PRE_DEV + page_len - 1) // page_len,
-        jnp.max((decode_len + page_len - 1) // page_len),
+    pre_scores = jnp.einsum(
+        "rghd,tgd->rght", pre_q, pre_keys, preferred_element_type=jnp.float32
     )
-    blocks = (need + block - 1) // block
+    pre_weight = capped_weight(
+        pre_scores, position[None, None, None, :] < limit[:, None, None, None]
+    )
+    pre_num = jnp.einsum(
+        "rght,tgd->rghd",
+        pre_weight.astype(jnp.bfloat16),
+        pre_vals,
+        preferred_element_type=jnp.float32,
+    )
+    pre_den = jnp.sum(pre_weight, axis=-1)
 
-    def step(index, carry):
-        pre_num, pre_den, dec_num, dec_den = carry
-        slots = lax.dynamic_slice_in_dim(page_table, index * block, block, 1)
-        keys = key_cache[slots].reshape(requests, span, local_kv, HD)
-        vals = value_cache[slots].reshape(requests, span, local_kv, HD)
-        position = index * span + jnp.arange(span, dtype=jnp.int32)
-        pre_scores = jnp.einsum(
-            "rghd,tgd->rght", pre_q, keys[0], preferred_element_type=jnp.float32
-        )
-        pre_weight = capped_weight(
-            pre_scores, position[None, None, None, :] < limit[:, None, None, None]
-        )
-        pre_num = pre_num + jnp.einsum(
-            "rght,tgd->rghd",
-            pre_weight.astype(jnp.bfloat16),
-            vals[0],
-            preferred_element_type=jnp.float32,
-        )
-        pre_den = pre_den + jnp.sum(pre_weight, axis=-1)
-        dec_scores = jnp.einsum(
-            "rghd,rtgd->rght", dec_q, keys[1:], preferred_element_type=jnp.float32
-        )
-        dec_weight = capped_weight(
-            dec_scores, position[None, None, None, :] < decode_len[:, None, None, None]
-        )
-        dec_num = dec_num + jnp.einsum(
-            "rght,rtgd->rghd",
-            dec_weight.astype(jnp.bfloat16),
-            vals[1:],
-            preferred_element_type=jnp.float32,
-        )
-        dec_den = dec_den + jnp.sum(dec_weight, axis=-1)
-        return (pre_num, pre_den, dec_num, dec_den)
+    table = page_table[1:]
+    page_idx = jnp.arange(max_pages, dtype=jnp.int32)
+    used = page_idx[None, :] * page_len < decode_len[:, None]
+    owned = (table[:, :, None] == jnp.arange(pool, dtype=jnp.int32)[None, None, :]) & used[
+        :, :, None
+    ]
+    base = jnp.min(
+        jnp.where(owned, page_idx[None, :, None] * page_len, jnp.int32(1 << 30)), axis=1
+    )
+    dec_pos = (base[:, :, None] + jnp.arange(page_len, dtype=jnp.int32)[None, None, :]).reshape(
+        DEC_DEV, pool * page_len
+    )
+    all_keys = key_cache.reshape(pool * page_len, local_kv, HD)
+    all_vals = value_cache.reshape(pool * page_len, local_kv, HD)
+    dec_scores = jnp.einsum(
+        "rghd,tgd->rght", dec_q, all_keys, preferred_element_type=jnp.float32
+    )
+    dec_weight = capped_weight(dec_scores, (dec_pos < decode_len[:, None])[:, None, None, :])
+    dec_num = jnp.einsum(
+        "rght,tgd->rghd",
+        dec_weight.astype(jnp.bfloat16),
+        all_vals,
+        preferred_element_type=jnp.float32,
+    )
+    dec_den = jnp.sum(dec_weight, axis=-1)
 
-    start_carry = (
-        jnp.zeros((PRE_DEV, local_kv, rep, HD), jnp.float32),
-        jnp.zeros((PRE_DEV, local_kv, rep), jnp.float32),
-        jnp.zeros((DEC_DEV, local_kv, rep, HD), jnp.float32),
-        jnp.zeros((DEC_DEV, local_kv, rep), jnp.float32),
-    )
-    pre_num, pre_den, dec_num, dec_den = lax.fori_loop(0, blocks, step, start_carry)
     pre_out = (pre_num / pre_den[..., None]).astype(jnp.bfloat16)
     dec_out = (dec_num / dec_den[..., None]).astype(jnp.bfloat16)
     return jnp.concatenate([pre_out, dec_out], axis=0).reshape(rows, local_kv * rep * HD)

time: 546 us -> 325 us (0.60)
  local copies, waits for them, and re-layouts: 188 us -> 12 us
  matrix products: 93.3 us -> 63.9 us
  other arithmetic: 31.8 us -> 20.2 us
    gather x16 -> x2, local copies, waits for them, and re-layouts: 126 us -> 8.98 us  [the longest x1 4.49 us: attend(): key_cache[page_table[0]].reshape(max_pages * page_len, local_kv, HD)]
    slice x48 -> x1, local copies, waits for them, and re-layouts: 50.6 us -> 0.71 us  [attend(): table = page_table[1:]]
    dot_general x32 -> x4, matrix products: 53.5 us -> 23.9 us  [the longest x1 10.4 us: attend(): jnp.einsum('rghd,tgd->rght', pre_q, pre_keys, preferred_element_type=jnp....]
  transfers between devices with their start and end apart: 5 -> 5, of which waited for: 4 -> 4; matrix products, arithmetic and copies ran while one was open for 6% -> 11% of each run, Pallas kernels for 0% -> 0%
where the time goes in v1:
time: 325 us
  waiting for transfers between devices  213 us (66%)
  matrix products  63.9 us (20%)
  other arithmetic  20.2 us (6%)
  between operations  15.9 us (5%)
  local copies, waits for them, and re-layouts  12 us (4%)
    psum x1, waiting for transfers between devices, per_device(): lax.psum(jnp.dot(attended, o_weight, preferred_element_type=jnp.float32)....  65.7 us
    psum x1, waiting for transfers between devices, per_device(): lax.psum(partial_out.astype(jnp.bfloat16), 'mlp').astype(jnp.float32)  62.5 us
    all_gather x1, waiting for transfers between devices, per_device(): lax.all_gather(w_down, 'req', axis=0, tiled=True)  46.8 us
    all_gather x1, waiting for transfers between devices, per_device(): lax.all_gather(w_up, 'req', axis=0, tiled=True)  36 us
    dot_general x1, matrix products, per_device(): jnp.dot(normed, lax.all_gather(w_up, 'req', axis=0, tiled=True), preferre...  12.9 us
    dot_general x1, matrix products, per_device(): jnp.dot(normed, lax.all_gather(w_gate, 'req', axis=0, tiled=True), prefer...  12.7 us
    dot_general x1, matrix products, per_device(): lax.dot_general(act, lax.all_gather(w_down, 'req', axis=0, tiled=True), (...  11.6 us
    dot_general x1, matrix products, attend(): jnp.einsum('rghd,tgd->rght', pre_q, pre_keys, preferred_element_type=jnp....  10.4 us
  transfers between devices with their start and end apart: 5, of which 4 were waited for; matrix products, arithmetic and copies ran while one was open for 11% of the time, Pallas kernels for 0%

profile of v1, /device:TPU:1, one launch (start us, length us, event | category | flops | bytes accessed | tf_op | source)
XLA Modules:
  0.0 324.8 jit_solution(14163465529039394121)
XLA Ops:
  7.4 0.8 fusion.41
  8.2 0.7 slice.17
  8.9 1.1 slice.16
  10.7 3.0 iota_compare_fusion
  13.7 0.2 copy.35
  13.9 4.5 %gather_fusion.1 = bf16[32,128,256]{2,1,0:T(8,128)(2,1)} fusion(bf16[80,128,256]{2,1,0:T(8,128)(2,1)} %param.15, s32[1024]{0:T(1024)S(1)} %pad_clamp_fusion), kind=kCustom, calls=%fused_computation.1 | custom fusion | bytes 4194432 | tf_op jit(solution)/shard_map/gather | solution.py:40
  18.4 4.5 %gather_fusion = bf16[32,128,256]{2,1,0:T(8,128)(2,1)} fusion(bf16[80,128,256]{2,1,0:T(8,128)(2,1)} %param.16, s32[1024]{0:T(1024)S(1)} %pad_clamp_fusion), kind=kCustom, calls=%fused_computation | custom fusion | bytes 4194432 | tf_op jit(solution)/shard_map/gather | solution.py:41
  22.9 0.1 broadcast_compare_fusion
  23.0 0.2 select_reduce_fusion
  23.2 0.2 add.106
  23.5 0.3 fusion.35
  23.8 0.0 slice-start
  23.8 0.0 slice-start.2
  23.8 10.4 %fusion = (f32[512,2]{0,1:T(2,128)S(1)}, f32[4096,512,2]{1,0,2:T(8,128)}) fusion(pred[512,4096]{0,1:T(8,128)(4,1)} %iota_compare_fusion, bf16[4096,256,1]{1,0,2:T(8,128)(2,1)} %bitcast.101, bf16[512,2,256]{0,2,1:T(8,128)(2,1)S(1)} %bitcast.110), kind=kOutput, calls=%fused_computation.3 | convolution fusion | flops 2164259840 | bytes 21499904 | tf_op jit(solution)/shard_map/rghd,tgd->rght/dot_general | solution.py:44
  34.2 0.0 copy-done.3
  34.2 0.0 slice-start.1
  34.2 0.0 slice-start.4
  34.3 0.0 slice-start.3
  34.3 9.5 %fusion.32 = bf16[512,1,2,256]{0,3,2,1:T(8,128)(2,1)S(1)} fusion(bf16[4096,256,1]{1,0,2:T(8,128)(2,1)S(1)} %bitcast.100, f32[4096,512,2]{1,0,2:T(8,128)} %get-tuple-element.10, pred[512,4096]{0,1:T(8,128)(4,1)S(1)} %copy-done.2, f32[512,2]{0,1:T(2,128)S(1)} %get-tuple-element.9), kind=kOutput, calls=%fused_computation.45 | convolution fusion | flops 2164785152 | bytes 21499904 | tf_op jit(solution)/shard_map/rght,tgd->rghd/dot_general | solution.py:50
  43.9 1.8 fusion.47
  45.6 2.1 fusion.29
  47.8 0.1 pad_maximum_fusion
  47.9 2.9 convolution_convert_fusion.1
  50.7 0.0 all-reduce.3.cloned.1.call-update
  50.8 0.0 all-gather.4.cloned.1.call-start
  50.8 0.5 all-gather.4.cloned.1.call-update
  51.4 0.0 all-gather.6.cloned.1.call-start
  51.4 0.5 all-gather.6.cloned.1.call-update
  51.9 0.0 all-gather.8.cloned.1.call-start
  52.0 0.5 all-gather.8.cloned.1.call-update
  52.5 0.0 all-reduce.5.cloned.1.call-start
  52.6 65.7 %all-reduce.3.cloned.1.call-done = bf16[528,2304]{1,0:T(8,128)(2,1)} async-done(((bf16[528,2304]{1,0:T(8,128)(2,1)}), bf16[528,2304]{1,0:T(8,128)(2,1)}) %all-reduce.3.cloned.1.call-update) | async-done | bytes 2433040 | tf_op jit(solution)/shard_map/psum | solution.py:106
  118.2 2.2 fusion.11
  120.5 0.0 copy-start.6
  120.5 5.8 %multiply_reduce_fusion.1 = (f32[528]{0:T(1024)S(1)}, f32[528,2304]{1,0:T(8,128)}) fusion(f32[2304]{0:T(1024)S(1)} %copy-done.4, f32[528]{0:T(1024)S(1)} %add_rsqrt_fusion.2, bf16[528,2304]{1,0:T(8,128)(2,1)} %all-reduce.3.cloned.1.call-done, bf16[528,2304]{1,0:T(8,128)(2,1)} %param.20), kind=kLoop, calls=%fused_computation.31 | loop fusion | flops 8515056 | bytes 9745536 | tf_op jit(solution)/shard_map/reduce_sum | solution.py:20
  126.3 0.0 copy-done.6
  126.3 12.7 %fusion.45 = f32[528,2304]{1,0:T(8,128)} fusion(bf16[2304,2304]{1,0:T(8,128)(2,1)} %all-gather.4.cloned.1.call-done, f32[528,2304]{1,0:T(8,128)} %get-tuple-element.6, f32[2304]{0:T(1024)S(1)} %copy-done.6, f32[528]{0:T(1024)S(1)} %add_rsqrt_fusion.1), kind=kOutput, calls=%fused_computation.69 | convolution fusion | flops 5609336832 | bytes 20360256 | tf_op jit(solution)/shard_map/dot_general | solution.py:111
  139.0 36.0 %all-gather.6.cloned.1.call-done = bf16[2304,2304]{1,0:T(8,128)(2,1)} async-done(((bf16[72,2304]{1,0:T(8,128)(2,1)}), bf16[2304,2304]{1,0:T(8,128)(2,1)}) %all-gather.6.cloned.1.call-update) | async-done | bytes 10616848 | tf_op jit(solution)/shard_map/all_gather | solution.py:117
  175.0 12.9 %fusion.21 = bf16[528,2304]{1,0:T(8,128)(2,1)} fusion(bf16[2304,2304]{1,0:T(8,128)(2,1)} %all-gather.6.cloned.1.call-done, f32[528,2304]{1,0:T(8,128)} %fusion.45, f32[528,2304]{1,0:T(8,128)} %get-tuple-element.6, f32[2304]{0:T(1024)S(1)} %copy-done.6, f32[528]{0:T(1024)S(1)} %add_rsqrt_fusion.1), kind=kOutput, calls=%fused_computation.32 | convolution fusion | flops 5621501952 | bytes 22793280 | tf_op jit(solution)/shard_map/dot_general | solution.py:116
  187.8 46.8 %all-gather.8.cloned.1.call-done = bf16[2304,2304]{1,0:T(8,128)(2,1)} async-done(((bf16[72,2304]{1,0:T(8,128)(2,1)}), bf16[2304,2304]{1,0:T(8,128)(2,1)}) %all-gather.8.cloned.1.call-update) | async-done | bytes 10616848 | tf_op jit(solution)/shard_map/all_gather | solution.py:122
  234.7 11.6 %convolution_convert_fusion = bf16[528,2304]{1,0:T(8,128)(2,1)} fusion(bf16[528,2304]{1,0:T(8,128)(2,1)} %fusion.21, bf16[2304,2304]{1,0:T(8,128)(2,1)} %all-gather.8.cloned.1.call-done), kind=kOutput, calls=%fused_computation.33 | convolution fusion | flops 5606903808 | bytes 15482880 | tf_op jit(solution)/shard_map/dot_general | solution.py:120
  246.3 0.0 all-reduce.5.cloned.1.call-update
  246.3 0.8 dynamic-slice
  247.1 62.5 %all-reduce.5.cloned.1.call-done = bf16[528,2304]{1,0:T(8,128)(2,1)} async-done(((bf16[528,2304]{1,0:T(8,128)(2,1)}), bf16[528,2304]{1,0:T(8,128)(2,1)}) %all-reduce.5.cloned.1.call-update) | async-done | bytes 2433040 | tf_op jit(solution)/shard_map/psum | solution.py:128
  309.6 2.2 multiply_reduce_fusion
  311.8 0.0 copy-start.1
  311.9 2.2 convert_element_type.54
  314.1 3.2 fusion.25
  (26 shorter events, 0.1 us)
Async XLA Ops:
  7.4 40.5 %copy-start = (bf16[512,2304]{1,0:T(8,128)(2,1)S(1)}, bf16[512,2304]{1,0:T(8,128)(2,1)}, u32[]{:S(2)}) copy-start(bf16[512,2304]{1,0:T(8,128)(2,1)} %param.21) | copy-start | bytes 7077892
  7.4 110.9 %all-reduce.3.cloned.1.call-start = ((), (), s32[]{:S(2)}) async-start(), calls=%async_computation | async-start | bytes 4866048 | tf_op jit(solution)/shard_map/psum | solution.py:106
  13.7 9.2 %copy-start.5 = (s32[16]{0:T(128)S(1)}, s32[16]{0:T(128)}, u32[]{:S(2)}) copy-start(s32[16]{0:T(128)} %param.17) | copy-start | bytes 196
  23.7 10.5 %copy-start.2 = (pred[512,4096]{0,1:T(8,128)(4,1)S(1)}, pred[512,4096]{0,1:T(8,128)(4,1)}, u32[]{:S(2)}) copy-start(pred[512,4096]{0,1:T(8,128)(4,1)} %iota_compare_fusion) | copy-start | bytes 6291460
  23.7 10.5 %copy-start.3 = (bf16[32,128,256]{2,1,0:T(8,128)(2,1)S(1)}, bf16[32,128,256]{2,1,0:T(8,128)(2,1)}, u32[]{:S(2)}) copy-start(bf16[32,128,256]{2,1,0:T(8,128)(2,1)} %gather_fusion) | copy-start | bytes 6291460
  23.8 20.1 %slice-start = ((s8[5242880]{0:T(1024)(128)(4,1)}), s8[4194304]{0:T(1024)(128)(4,1)S(1)}, s32[]{:S(2)}) async-start(s8[5242880]{0:T(1024)(128)(4,1)} %bitcast.102), calls=%async_computation.5 | async-start | bytes 8388608
  23.8 21.8 %slice-start.2 = ((s8[5242880]{0:T(1024)(128)(4,1)}), s8[4194304]{0:T(1024)(128)(4,1)S(1)}, s32[]{:S(2)}) async-start(s8[5242880]{0:T(1024)(128)(4,1)} %bitcast.105), calls=%async_computation.7 | async-start | bytes 8388608
  34.2 9.6 %slice-start.1 = ((s8[5242880]{0:T(1024)(128)(4,1)}), s8[1048576]{0:T(1024)(128)(4,1)S(1)}, s32[]{:S(2)}) async-start(s8[5242880]{0:T(1024)(128)(4,1)} %bitcast.102), calls=%async_computation.6 | async-start | bytes 2097152
  34.2 9.6 %slice-start.4 = ((bf16[528,512]{1,0:T(8,128)(2,1)}), bf16[16,512]{1,0:T(8,128)(2,1)S(1)}, s32[]{:S(2)}) async-start(bf16[528,512]{1,0:T(8,128)(2,1)} %param.14), calls=%async_computation.9 | async-start | bytes 32768 | tf_op jit(solution)/shard_map/slice | solution.py:37
  34.3 11.4 %slice-start.3 = ((s8[5242880]{0:T(1024)(128)(4,1)}), s8[1048576]{0:T(1024)(128)(4,1)S(1)}, s32[]{:S(2)}) async-start(s8[5242880]{0:T(1024)(128)(4,1)} %bitcast.105), calls=%async_computation.8 | async-start | bytes 2097152
  50.7 69.7 %copy-start.4 = (f32[2304]{0:T(1024)S(1)}, f32[2304]{0:T(1024)}, u32[]{:S(2)}) copy-start(f32[2304]{0:T(1024)} %param.22) | copy-start | bytes 27652
  50.8 75.5 %all-gather.4.cloned.1.call-start = ((), (), s32[]{:S(2)}) async-start(), calls=%async_computation.1 | async-start | bytes 10948608 | tf_op jit(solution)/shard_map/all_gather | solution.py:113
  51.4 123.6 %all-gather.6.cloned.1.call-start = ((), (), s32[]{:S(2)}) async-start(), calls=%async_computation.2 | async-start | bytes 10948608 | tf_op jit(solution)/shard_map/all_gather | solution.py:117
  51.9 182.7 %all-gather.8.cloned.1.call-start = ((), (), s32[]{:S(2)}) async-start(), calls=%async_computation.3 | async-start | bytes 10948608 | tf_op jit(solution)/shard_map/all_gather | solution.py:122
  52.5 257.1 %all-reduce.5.cloned.1.call-start = ((), (), s32[]{:S(2)}) async-start(), calls=%async_computation.4 | async-start | bytes 4866048 | tf_op jit(solution)/shard_map/psum | solution.py:128
  120.5 5.8 %copy-start.6 = (f32[2304]{0:T(1024)S(1)}, f32[2304]{0:T(1024)}, u32[]{:S(2)}) copy-start(f32[2304]{0:T(1024)} %param.23) | copy-start | bytes 27652
  311.8 5.4 %copy-start.1 = (bf16[512,2304]{1,0:T(8,128)(2,1)S(1)}, bf16[512,2304]{1,0:T(8,128)(2,1)}, u32[]{:S(2)}) copy-start(bf16[512,2304]{1,0:T(8,128)(2,1)} %param.21) | copy-start | bytes 7077892
Sparse Core Ops, SparseCore 0:
  50.9 67.3 all-reduce.2
  246.4 63.1 all-reduce.4
Sparse Core Ops, SparseCore 1:
  53.6 61.6 all-gather.3
  117.4 57.5 all-gather.5
  177.2 57.4 all-gather.7

commit v2 on v1

--- a/solution.py
+++ b/solution.py
@@ -1,5 +1,3 @@
-import math
-
 import jax
 import jax.numpy as jnp
 from jax import lax
@@ -41,9 +39,7 @@
     pre_vals = value_cache[page_table[0]].reshape(max_pages * page_len, local_kv, HD)
     position = jnp.arange(max_pages * page_len, dtype=jnp.int32)
     limit = start + jnp.arange(PRE_DEV, dtype=jnp.int32) + 1
-    pre_scores = jnp.einsum(
-        "rghd,tgd->rght", pre_q, pre_keys, preferred_element_type=jnp.float32
-    )
+    pre_scores = jnp.einsum("rghd,tgd->rght", pre_q, pre_keys, preferred_element_type=jnp.float32)
     pre_weight = capped_weight(
         pre_scores, position[None, None, None, :] < limit[:, None, None, None]
     )
@@ -86,6 +82,10 @@
     return jnp.concatenate([pre_out, dec_out], axis=0).reshape(rows, local_kv * rep * HD)
 
 
+def split_weight(weight):
+    return lax.all_to_all(weight, "core", 1, 0, tiled=True)
+
+
 def per_device(
     queries,
     key_cache,
@@ -102,55 +102,68 @@
     w_up,
     w_down,
 ):
+    gate_w = split_weight(w_gate)
+    up_w = split_weight(w_up)
+    down_w = split_weight(w_down)
+    queries, gate_w, up_w, down_w = lax.optimization_barrier((queries, gate_w, up_w, down_w))
+    gate_w = lax.all_gather(gate_w, "chip", axis=0, tiled=True)
+    up_w = lax.all_gather(up_w, "chip", axis=0, tiled=True)
+    down_w = lax.all_gather(down_w, "chip", axis=0, tiled=True)
     attended = attend(queries, key_cache, value_cache, decode_len, stretch_start, page_table)
     projected = lax.psum(
         jnp.dot(attended, o_weight, preferred_element_type=jnp.float32).astype(jnp.bfloat16), "mlp"
     ).astype(jnp.float32)
+    projected, gate_w, up_w, down_w = lax.optimization_barrier((projected, gate_w, up_w, down_w))
     resid = hidden_in.astype(jnp.float32) + rms(projected, attn_gain)
     normed = rms(resid, ffn_in_gain).astype(jnp.bfloat16)
-    gate = jnp.dot(
-        normed,
-        lax.all_gather(w_gate, "req", axis=0, tiled=True),
-        preferred_element_type=jnp.float32,
-    )
-    up_part = jnp.dot(
-        normed, lax.all_gather(w_up, "req", axis=0, tiled=True), preferred_element_type=jnp.float32
-    )
+    pair = lax.all_gather(normed, "core", axis=0, tiled=True)
+    gate = jnp.dot(pair, gate_w, preferred_element_type=jnp.float32)
+    up_part = jnp.dot(pair, up_w, preferred_element_type=jnp.float32)
     act = (jax.nn.gelu(gate, approximate=True) * up_part).astype(jnp.bfloat16)
     partial_out = lax.dot_general(
-        act,
-        lax.all_gather(w_down, "req", axis=0, tiled=True),
-        (((1,), (1,)), ((), ())),
-        preferred_element_type=jnp.float32,
+        act, down_w, (((1,), (1,)), ((), ())), preferred_element_type=jnp.float32
     )
-    width = hidden_in.shape[1] // lax.axis_size("mlp")
+    rows_part = lax.psum_scatter(
+        partial_out.astype(jnp.bfloat16), "core", scatter_dimension=0, tiled=True
+    )
+    total = lax.psum_scatter(rows_part, "mlp", scatter_dimension=1, tiled=True).astype(
+        jnp.float32
+    )
+    width = total.shape[1]
     first = lax.axis_index("mlp") * width
-    total = lax.psum(partial_out.astype(jnp.bfloat16), "mlp").astype(jnp.float32)
-    combined = resid + rms(total, ffn_out_gain)
-    result = lax.dynamic_slice_in_dim(combined, first, width, 1)
-    return result.astype(jnp.bfloat16)
+    square = lax.psum(jnp.sum(total * total, axis=-1, keepdims=True), "mlp")
+    scale = lax.rsqrt(square / hidden_in.shape[1] + EPS)
+    gain = lax.dynamic_slice_in_dim(ffn_out_gain, first, width, 0)
+    kept = lax.dynamic_slice_in_dim(resid, first, width, 1)
+    return (kept + total * scale * gain).astype(jnp.bfloat16)
 
 
 def solution(mesh):
+    devices = mesh.devices
+    chips = devices.shape[0] // 2
+    split = jax.sharding.Mesh(
+        devices.reshape(chips, 2, devices.shape[1]), ("chip", "core", "mlp")
+    )
+    req = ("chip", "core")
     return jax.shard_map(
         per_device,
-        mesh=mesh,
+        mesh=split,
         in_specs=(
-            P("req", "mlp"),
-            P("req", None, "mlp"),
-            P("req", None, "mlp"),
-            P("req"),
-            P("req"),
-            P("req", None),
-            P("req", None),
+            P(req, "mlp"),
+            P(req, None, "mlp"),
+            P(req, None, "mlp"),
+            P(req),
+            P(req),
+            P(req, None),
+            P(req, None),
             P("mlp", None),
             P(),
             P(),
             P(),
-            P("req", "mlp"),
-            P("req", "mlp"),
-            P("req", "mlp"),
+            P(req, "mlp"),
+            P(req, "mlp"),
+            P(req, "mlp"),
         ),
-        out_specs=P("req", "mlp"),
+        out_specs=P(req, "mlp"),
         check_vma=False,
     )

time: 325 us -> 386 us (1.19)
  waiting for transfers between devices: 213 us -> 245 us
  blocking collectives: 0 us -> 16.8 us
  local copies, waits for them, and re-layouts: 12 us -> 25.8 us
  matrix products: 63.9 us -> 55.9 us
  starting transfers between devices: 0.17 us -> 5.26 us
    psum x1 -> x0, waiting for transfers between devices: 62.5 us -> none  [per_device(): lax.psum(partial_out.astype(jnp.bfloat16), 'mlp').astype(jnp.float32)]
    all_gather x3 -> x4, waiting for transfers between devices: 82.8 us -> 125 us  [the longest x1 58.2 us: per_device(): down_w = lax.all_gather(down_w, 'chip', axis=0, tiled=True)]
    unnamed x5 -> x8, waiting for transfers between devices: 1.61 us -> 38.8 us
    reduce_scatter x0 -> x1, waiting for transfers between devices: none -> 16.7 us  [per_device(): lax.psum_scatter(partial_out.astype(jnp.bfloat16), 'core', scatter_dimens...]
    all_to_all x0 -> x2, blocking collectives: none -> 10.3 us  [split_weight(): return lax.all_to_all(weight, 'core', 1, 0, tiled=True)]
    unnamed x23 -> x26, local copies, waits for them, and re-layouts: 0.27 us -> 9.09 us
    psum x0 -> x1, blocking collectives: none -> 6.55 us  [per_device(): square = lax.psum(jnp.sum(total * total, axis=-1, keepdims=True), 'mlp')]
    dot_general x3 -> x2, matrix products: 37.1 us -> 31.7 us  [the longest x1 20.3 us: per_device(): lax.dot_general(act, down_w, (((1,), (1,)), ((), ())), preferred_element_...]
  transfers between devices with their start and end apart: 5 -> 8, of which waited for: 4 -> 6; matrix products, arithmetic and copies ran while one was open for 11% -> 2% of each run, Pallas kernels for 0% -> 0%
where the time goes in v2:
time: 386 us; the launch traced here: 383 us
  waiting for transfers between devices  245 us (63%)
  matrix products  55.9 us (14%)
  local copies, waits for them, and re-layouts  25.8 us (7%)
  other arithmetic  19.3 us (5%)
  blocking collectives  16.8 us (4%)
  between operations  15.8 us (4%)
  starting transfers between devices  5.26 us (1%)
    psum x1, waiting for transfers between devices, per_device(): lax.psum(jnp.dot(attended, o_weight, preferred_element_type=jnp.float32)....  64.4 us
    all_gather x1, waiting for transfers between devices, per_device(): down_w = lax.all_gather(down_w, 'chip', axis=0, tiled=True)  58.2 us
    all_gather x1, waiting for transfers between devices, per_device(): up_w = lax.all_gather(up_w, 'chip', axis=0, tiled=True)  48.8 us
    unnamed x8, waiting for transfers between devices  38.8 us
    dot_general x1, matrix products, per_device(): lax.dot_general(act, down_w, (((1,), (1,)), ((), ())), preferred_element_...  20.3 us
    all_gather x1, waiting for transfers between devices, per_device(): pair = lax.all_gather(normed, 'core', axis=0, tiled=True)  17.7 us
    reduce_scatter x1, waiting for transfers between devices, per_device(): lax.psum_scatter(partial_out.astype(jnp.bfloat16), 'core', scatter_dimens...  16.7 us
    dot_general x1, matrix products, per_device(): gate = jnp.dot(pair, gate_w, preferred_element_type=jnp.float32)  11.4 us
  transfers between devices with their start and end apart: 8, of which 6 were waited for; matrix products, arithmetic and copies ran while one was open for 2% of the time, Pallas kernels for 0%

profile of v2, /device:TPU:1, one launch (start us, length us, event | category | flops | bytes accessed | tf_op | source)
XLA Modules:
  0.0 383.5 jit_solution(13796225080021405128)
XLA Ops:
  7.4 1.9 copy.75
  9.3 4.8 %all-to-all-start = ((bf16[72,2,1152]{2,0,1:T(8,128)(2,1)}), bf16[72,2,1152]{2,0,1:T(8,128)(2,1)S(1)}, u32[]{:S(2)}, u32[]{:S(2)}) async-start(bf16[72,2,1152]{2,0,1:T(8,128)(2,1)} %bitcast.132), calls=%async_computation | async-start | bytes 663552 | tf_op jit(solution)/shard_map/all_to_all | solution.py:86
  14.1 0.7 slice.17
  14.8 0.7 fusion.40
  15.5 1.7 copy.74
  17.2 1.0 copy.73
  18.2 5.6 %all_to_all.57 = bf16[72,2,1152]{2,0,1:T(8,128)(2,1)} all-to-all(bf16[72,2,1152]{2,0,1:T(8,128)(2,1)} %bitcast.144), channel_id=1, replica_groups=mesh['chip'=16,'core'=2,'mlp'=4] {'core'}, dimensions={1} | all-to-all | bytes 663552 | tf_op jit(solution)/shard_map/all_to_all | solution.py:86
  23.8 4.7 %all_to_all.58 = bf16[72,2,1152]{2,0,1:T(8,128)(2,1)} all-to-all(bf16[72,2,1152]{2,0,1:T(8,128)(2,1)S(1)} %bitcast.143), channel_id=1, replica_groups=mesh['chip'=16,'core'=2,'mlp'=4] {'core'}, dimensions={1} | all-to-all | bytes 663552 | tf_op jit(solution)/shard_map/all_to_all | solution.py:86
  28.5 1.3 copy.45
  30.6 3.0 iota_compare_fusion
  33.6 4.5 %gather_fusion = bf16[32,128,256]{2,1,0:T(8,128)(2,1)} fusion(bf16[80,128,256]{2,1,0:T(8,128)(2,1)} %param.16, s32[1024]{0:T(1024)S(1)} %pad_clamp_fusion), kind=kCustom, calls=%fused_computation | custom fusion | bytes 4194432 | tf_op jit(solution)/shard_map/gather | solution.py:39
  38.1 4.5 %gather_fusion.1 = bf16[32,128,256]{2,1,0:T(8,128)(2,1)} fusion(bf16[80,128,256]{2,1,0:T(8,128)(2,1)} %param.15, s32[1024]{0:T(1024)S(1)} %pad_clamp_fusion), kind=kCustom, calls=%fused_computation.1 | custom fusion | bytes 4194432 | tf_op jit(solution)/shard_map/gather | solution.py:38
  42.6 0.1 broadcast_compare_fusion
  42.7 0.2 select_reduce_fusion
  43.0 0.2 add.106
  43.2 0.3 fusion.34
  43.5 4.2 %fusion.44 = (f32[16,2]{0,1:T(2,128)S(1)}, bf16[16,1,2,10240]{3,0,2,1:T(8,128)(2,1)S(1)}) fusion(bf16[10240,256,1]{1,0,2:T(8,128)(2,1)} %bitcast.135, bf16[2,2,8,256]{3,2,1,0:T(8,128)(2,1)S(1)} %bitcast.148, pred[16,10240]{1,0:T(8,128)(4,1)S(1)} %fusion.34), kind=kOutput, calls=%fused_computation.70 | convolution fusion | flops 169410528 | bytes 6078592 | tf_op jit(solution)/shard_map/rghd,tgd->rght/dot_general | solution.py:68
  47.7 4.2 %fusion.28 = bf16[16,1,2,256]{0,3,2,1:T(8,128)(2,1)S(1)} fusion(bf16[10240,256,1]{1,0,2:T(8,128)(2,1)} %bitcast.145, bf16[16,1,2,10240]{3,0,2,1:T(8,128)(2,1)S(1)} %get-tuple-element.24, f32[16,2]{0,1:T(2,128)S(1)} %get-tuple-element.23), kind=kOutput, calls=%fused_computation.41 | convolution fusion | flops 167788544 | bytes 5914752 | tf_op jit(solution)/shard_map/rght,tgd->rghd/dot_general | solution.py:72
  52.0 6.7 %fusion = (f32[512,2]{0,1:T(2,128)S(1)}, f32[4096,512,2]{1,0,2:T(8,128)S(1)}) fusion(pred[512,4096]{0,1:T(8,128)(4,1)S(1)} %copy-done.5, bf16[4096,256,1]{1,0,2:T(8,128)(2,1)S(1)} %bitcast.139, bf16[512,2,256]{0,2,1:T(8,128)(2,1)S(1)} %bitcast.137), kind=kOutput, calls=%fused_computation.3 | convolution fusion | flops 2164259840 | bytes 21499904 | tf_op jit(solution)/shard_map/rghd,tgd->rght/dot_general | solution.py:42
  58.7 6.2 %fusion.31 = bf16[512,1,2,256]{0,3,2,1:T(8,128)(2,1)S(1)} fusion(bf16[4096,256,1]{1,0,2:T(8,128)(2,1)S(1)} %bitcast.138, f32[4096,512,2]{1,0,2:T(8,128)S(1)} %get-tuple-element.26, pred[512,4096]{0,1:T(8,128)(4,1)S(1)} %copy-done.5, f32[512,2]{0,1:T(2,128)S(1)} %get-tuple-element.25), kind=kOutput, calls=%fused_computation.43 | convolution fusion | flops 2164785152 | bytes 21499904 | tf_op jit(solution)/shard_map/rght,tgd->rghd/dot_general | solution.py:46
  64.9 0.1 pad_maximum_fusion
  64.9 2.9 convolution_convert_fusion.1
  67.9 0.0 all-gather.5.cloned.1.call-start
  67.9 0.5 all-gather.5.cloned.1.call-update
  68.5 0.5 all-gather.7.cloned.1.call-update
  69.1 0.5 all-gather.9.cloned.1.call-update
  69.6 0.2 all-gather.11.cloned.1.call-start
  69.9 64.4 %all-reduce.2.cloned.1.call-done = bf16[528,2304]{1,0:T(8,128)(2,1)} async-done(((bf16[528,2304]{1,0:T(8,128)(2,1)}), bf16[528,2304]{1,0:T(8,128)(2,1)}) %all-reduce.2.cloned.1.call-update) | async-done | bytes 2433040 | tf_op jit(solution)/shard_map/psum | solution.py:113
  134.3 4.2 %convert_element_type.50 = f32[528,2304]{1,0:T(8,128)} convert(bf16[528,2304]{1,0:T(8,128)(2,1)} %all-reduce.2.cloned.1.call-done) | non-fusion elementwise | flops 1216512 | bytes 7299072 | tf_op jit(solution)/shard_map/convert_element_type | solution.py:115
  138.5 48.8 %all-gather.7.cloned.1.call-done = bf16[2304,1152]{1,0:T(8,128)(2,1)} async-done(((bf16[144,1152]{1,0:T(8,128)(2,1)}), bf16[2304,1152]{1,0:T(8,128)(2,1)}) %all-gather.7.cloned.1.call-update) | async-done | bytes 5308432 | tf_op jit(solution)/shard_map/all_gather | solution.py:110
  187.3 58.2 %all-gather.9.cloned.1.call-done = bf16[2304,1152]{1,0:T(8,128)(2,1)} async-done(((bf16[144,1152]{1,0:T(8,128)(2,1)}), bf16[2304,1152]{1,0:T(8,128)(2,1)}) %all-gather.9.cloned.1.call-update) | async-done | bytes 5308432 | tf_op jit(solution)/shard_map/all_gather | solution.py:111
  245.5 2.9 multiply_reduce_fusion.1
  248.5 0.9 copy-done.2
  249.4 2.8 multiply_reduce_fusion
  252.2 2.1 copy-done.3
  254.4 2.0 multiply_convert_fusion
  256.3 0.0 reduce-scatter.5.cloned.1.call-start
  256.4 17.7 %all-gather.11.cloned.1.call-done = bf16[1056,2304]{1,0:T(8,128)(2,1)} async-done(((bf16[528,2304]{1,0:T(8,128)(2,1)}), bf16[1056,2304]{1,0:T(8,128)(2,1)}) %all-gather.11.cloned.1.call-update) | async-done | bytes 4866064 | tf_op jit(solution)/shard_map/all_gather | solution.py:119
  274.1 11.4 %fusion.45 = f32[1056,1152]{1,0:T(8,128)} fusion(bf16[1056,2304]{1,0:T(8,128)(2,1)} %all-gather.11.cloned.1.call-done, bf16[2304,1152]{1,0:T(8,128)(2,1)} %all-gather.5.cloned.1.call-done), kind=kOutput, calls=%fused_computation.71 | convolution fusion | flops 5605687296 | bytes 15040512 | tf_op jit(solution)/shard_map/dot_general | solution.py:120
  285.5 20.3 %convolution_convert_fusion = bf16[1056,2304]{1,0:T(8,128)(2,1)} fusion(bf16[2304,1152]{1,0:T(8,128)(2,1)} %all-gather.9.cloned.1.call-done, bf16[1056,2304]{1,0:T(8,128)(2,1)} %all-gather.11.cloned.1.call-done, bf16[2304,1152]{1,0:T(8,128)(2,1)} %all-gather.7.cloned.1.call-done, f32[1056,1152]{1,0:T(8,128)} %fusion.45), kind=kOutput, calls=%fused_computation.10 | convolution fusion | flops 11225972736 | bytes 25214976 | tf_op jit(solution)/shard_map/dot_general | solution.py:123
  305.9 16.7 %reduce-scatter.5.cloned.1.call-done = bf16[528,2304]{1,0:T(8,128)(2,1)} async-done(((bf16[1056,2304]{1,0:T(8,128)(2,1)}), bf16[528,2304]{1,0:T(8,128)(2,1)}) %reduce-scatter.5.cloned.1.call-update) | async-done | bytes 2433040 | tf_op jit(solution)/shard_map/reduce_scatter | solution.py:126
  322.5 4.6 %copy.56 = bf16[528,2304]{0,1:T(8,128)(2,1)} copy(bf16[528,2304]{1,0:T(8,128)(2,1)} %reduce-scatter.5.cloned.1.call-done) | data formatting | bytes 4866048
  327.2 0.8 dynamic_slice.7
  328.0 37.1 %reduce-scatter.7.cloned.1.call-done = bf16[576,528]{1,0:T(8,128)(2,1)} async-done(((bf16[2304,528]{1,0:T(8,128)(2,1)}), bf16[576,528]{1,0:T(8,128)(2,1)}) %reduce-scatter.7.cloned.1.call-update) | async-done | bytes 608272
  365.1 1.4 copy.57
  366.5 0.2 fusion.22
  366.8 6.5 %psum.15 = f32[528,1]{0,1:T(1,128)S(1)} all-reduce(f32[528,1]{0,1:T(1,128)S(1)} %broadcast_in_dim.44), channel_id=1, replica_groups=mesh['chip'=16,'core'=2,'mlp'=4] {'mlp'}, use_global_device_ids=true, to_apply=%region_9.10 | all-reduce | flops 528 | bytes 4224 | tf_op jit(solution)/shard_map/psum | solution.py:134
  373.4 2.8 fusion.25
  (44 shorter events, 0.3 us)
Async XLA Ops:
  7.4 57.6 %copy-start = (bf16[512,2304]{1,0:T(8,128)(2,1)S(1)}, bf16[512,2304]{1,0:T(8,128)(2,1)}, u32[]{:S(2)}) copy-start(bf16[512,2304]{1,0:T(8,128)(2,1)} %param.21) | copy-start | bytes 7077892
  9.3 9.0 %all-to-all-start = ((bf16[72,2,1152]{2,0,1:T(8,128)(2,1)}), bf16[72,2,1152]{2,0,1:T(8,128)(2,1)S(1)}, u32[]{:S(2)}, u32[]{:S(2)}) async-start(bf16[72,2,1152]{2,0,1:T(8,128)(2,1)} %bitcast.132), calls=%async_computation | async-start | bytes 663552 | tf_op jit(solution)/shard_map/all_to_all | solution.py:86
  14.1 120.2 %all-reduce.2.cloned.1.call-start = ((), (), s32[]{:S(2)}) async-start(), calls=%async_computation.5 | async-start | bytes 4866048 | tf_op jit(solution)/shard_map/psum | solution.py:113
  18.2 24.4 %copy-start.8 = (bf16[72,2,1152]{2,0,1:T(8,128)(2,1)}, bf16[72,2,1152]{2,0,1:T(8,128)(2,1)S(1)}, u32[]{:S(2)}) copy-start(bf16[72,2,1152]{2,0,1:T(8,128)(2,1)S(1)} %all-to-all-done) | copy-start | bytes 995332
  29.9 12.8 %copy-start.4 = (bf16[528,512]{0,1:T(8,128)(2,1)}, bf16[528,512]{0,1:T(8,128)(2,1)S(1)}, u32[]{:S(2)}) copy-start(bf16[528,512]{0,1:T(8,128)(2,1)S(1)} %copy.45) | copy-start | bytes 1622020
  33.6 9.0 %copy-start.11 = (s32[16]{0:T(128)S(1)}, s32[16]{0:T(128)}, u32[]{:S(2)}) copy-start(s32[16]{0:T(128)} %param.17) | copy-start | bytes 196
  33.6 9.8 %slice-start.1 = ((bf16[528,512]{1,0:T(8,128)(2,1)}), bf16[16,512]{1,0:T(8,128)(2,1)S(1)}, s32[]{:S(2)}) async-start(bf16[528,512]{1,0:T(8,128)(2,1)} %param.14), calls=%async_computation.13 | async-start | bytes 32768 | tf_op jit(solution)/shard_map/slice | solution.py:35
  47.7 4.2 %slice-start = ((bf16[528,512]{0,1:T(8,128)(2,1)}), bf16[512,512]{0,1:T(8,128)(2,1)S(1)}, s32[]{:S(2)}) async-start(bf16[528,512]{0,1:T(8,128)(2,1)} %copy-done.4), calls=%async_computation.12 | async-start | bytes 1048576 | tf_op jit(solution)/shard_map/slice | solution.py:34
  47.7 4.3 %copy-start.5 = (pred[512,4096]{0,1:T(8,128)(4,1)S(1)}, pred[512,4096]{0,1:T(8,128)(4,1)}, u32[]{:S(2)}) copy-start(pred[512,4096]{0,1:T(8,128)(4,1)} %iota_compare_fusion) | copy-start | bytes 6291460
  47.7 4.3 %copy-start.7 = (bf16[32,128,256]{2,1,0:T(8,128)(2,1)S(1)}, bf16[32,128,256]{2,1,0:T(8,128)(2,1)}, u32[]{:S(2)}) copy-start(bf16[32,128,256]{2,1,0:T(8,128)(2,1)} %gather_fusion.1) | copy-start | bytes 6291460
  52.0 6.7 %copy-start.6 = (bf16[32,128,256]{2,1,0:T(8,128)(2,1)S(1)}, bf16[32,128,256]{2,1,0:T(8,128)(2,1)}, u32[]{:S(2)}) copy-start(bf16[32,128,256]{2,1,0:T(8,128)(2,1)} %gather_fusion) | copy-start | bytes 6291460
  67.9 70.6 %all-gather.5.cloned.1.call-start = ((), (), s32[]{:S(2)}) async-start(), calls=%async_computation.6 | async-start | bytes 5640192 | tf_op jit(solution)/shard_map/all_gather | solution.py:109
  68.4 118.9 %all-gather.7.cloned.1.call-start = ((), (), s32[]{:S(2)}) async-start(), calls=%async_computation.7 | async-start | bytes 5640192 | tf_op jit(solution)/shard_map/all_gather | solution.py:110
  69.0 176.5 %all-gather.9.cloned.1.call-start = ((), (), s32[]{:S(2)}) async-start(), calls=%async_computation.8 | async-start | bytes 5640192 | tf_op jit(solution)/shard_map/all_gather | solution.py:111
  69.6 178.9 %copy-start.9 = (f32[2304]{0:T(1024)S(1)}, f32[2304]{0:T(1024)}, u32[]{:S(2)}) copy-start(f32[2304]{0:T(1024)} %param.22) | copy-start | bytes 27652
  69.6 204.5 %all-gather.11.cloned.1.call-start = ((), (), s32[]{:S(2)}) async-start(), calls=%async_computation.9 | async-start | bytes 7299072 | tf_op jit(solution)/shard_map/all_gather | solution.py:119
  245.5 3.8 %copy-start.2 = (f32[528,2304]{1,0:T(8,128)S(1)}, f32[528,2304]{1,0:T(8,128)}, u32[]{:S(2)}) copy-start(f32[528,2304]{1,0:T(8,128)} %convert_element_type.50) | copy-start | bytes 14598148
  249.4 5.0 %copy-start.10 = (f32[2304]{0:T(1024)S(1)}, f32[2304]{0:T(1024)}, u32[]{:S(2)}) copy-start(f32[2304]{0:T(1024)} %param.23) | copy-start | bytes 27652
  252.2 2.1 copy-start.3
  256.3 66.2 %reduce-scatter.5.cloned.1.call-start = ((), (), s32[]{:S(2)}) async-start(), calls=%async_computation.10 | async-start | bytes 7299072 | tf_op jit(solution)/shard_map/reduce_scatter | solution.py:126
  305.8 59.3 %reduce-scatter.7.cloned.1.call-start = ((), (), s32[]{:S(2)}) async-start(), calls=%async_computation.11 | async-start | bytes 3686400
  322.5 53.6 %copy-start.1 = (bf16[512,2304]{1,0:T(8,128)(2,1)S(1)}, bf16[512,2304]{1,0:T(8,128)(2,1)}, u32[]{:S(2)}) copy-start(bf16[512,2304]{1,0:T(8,128)(2,1)} %param.21) | copy-start | bytes 7077892
Sparse Core Ops, SparseCore 0:
  68.0 66.2 all-reduce.1
  256.5 17.5 all-gather.10
  305.9 16.5 reduce-scatter.4
  327.3 37.7 reduce-scatter.6
Sparse Core Ops, SparseCore 1:
  70.5 58.5 all-gather.4
  131.1 56.1 all-gather.6
  189.4 56.1 all-gather.8

commit v3 on v1

--- a/solution.py
+++ b/solution.py
@@ -102,33 +102,31 @@
     w_up,
     w_down,
 ):
+    weights = lax.all_gather(
+        jnp.stack([w_gate, w_up, w_down]), "req", axis=1, tiled=True
+    )
     attended = attend(queries, key_cache, value_cache, decode_len, stretch_start, page_table)
     projected = lax.psum(
         jnp.dot(attended, o_weight, preferred_element_type=jnp.float32).astype(jnp.bfloat16), "mlp"
     ).astype(jnp.float32)
     resid = hidden_in.astype(jnp.float32) + rms(projected, attn_gain)
     normed = rms(resid, ffn_in_gain).astype(jnp.bfloat16)
-    gate = jnp.dot(
-        normed,
-        lax.all_gather(w_gate, "req", axis=0, tiled=True),
-        preferred_element_type=jnp.float32,
-    )
-    up_part = jnp.dot(
-        normed, lax.all_gather(w_up, "req", axis=0, tiled=True), preferred_element_type=jnp.float32
-    )
+    gate = jnp.dot(normed, weights[0], preferred_element_type=jnp.float32)
+    up_part = jnp.dot(normed, weights[1], preferred_element_type=jnp.float32)
     act = (jax.nn.gelu(gate, approximate=True) * up_part).astype(jnp.bfloat16)
     partial_out = lax.dot_general(
-        act,
-        lax.all_gather(w_down, "req", axis=0, tiled=True),
-        (((1,), (1,)), ((), ())),
-        preferred_element_type=jnp.float32,
+        act, weights[2], (((1,), (1,)), ((), ())), preferred_element_type=jnp.float32
     )
-    width = hidden_in.shape[1] // lax.axis_size("mlp")
+    total = lax.psum_scatter(
+        partial_out.astype(jnp.bfloat16), "mlp", scatter_dimension=1, tiled=True
+    ).astype(jnp.float32)
+    width = total.shape[1]
     first = lax.axis_index("mlp") * width
-    total = lax.psum(partial_out.astype(jnp.bfloat16), "mlp").astype(jnp.float32)
-    combined = resid + rms(total, ffn_out_gain)
-    result = lax.dynamic_slice_in_dim(combined, first, width, 1)
-    return result.astype(jnp.bfloat16)
+    square = lax.psum(jnp.sum(total * total, axis=-1, keepdims=True), "mlp")
+    scale = lax.rsqrt(square / hidden_in.shape[1] + EPS)
+    gain = lax.dynamic_slice_in_dim(ffn_out_gain, first, width, 0)
+    kept = lax.dynamic_slice_in_dim(resid, first, width, 1)
+    return (kept + total * scale * gain).astype(jnp.bfloat16)
 
 
 def solution(mesh):

time: 325 us -> 262 us (0.81)
  waiting for transfers between devices: 213 us -> 141 us
  blocking collectives: 0 us -> 6.56 us
  local copies, waits for them, and re-layouts: 12 us -> 18.1 us
    psum x1 -> x0, waiting for transfers between devices: 62.5 us -> none  [per_device(): lax.psum(partial_out.astype(jnp.bfloat16), 'mlp').astype(jnp.float32)]
    all_gather x3 -> x1, waiting for transfers between devices: 82.8 us -> 39.7 us  [per_device(): lax.all_gather(jnp.stack([w_gate, w_up, w_down]), 'req', axis=1, tiled=True)]
    unnamed x5 -> x4, waiting for transfers between devices: 1.61 us -> 34.9 us
    psum x0 -> x1, blocking collectives: none -> 6.56 us  [per_device(): square = lax.psum(jnp.sum(total * total, axis=-1, keepdims=True), 'mlp')]
    unnamed x23 -> x31, local copies, waits for them, and re-layouts: 0.27 us -> 6.31 us
    dot_general x3 -> x2, matrix products: 37.1 us -> 34.7 us  [the longest x1 22 us: per_device(): lax.dot_general(act, weights[2], (((1,), (1,)), ((), ())), preferred_elem...]
    reduce_sum x3 -> x2, other arithmetic: 10.2 us -> 8.53 us  [rms(): jnp.mean(values * values, axis=-1, keepdims=True) + EPS]
  transfers between devices with their start and end apart: 5 -> 3, of which waited for: 4 -> 3; matrix products, arithmetic and copies ran while one was open for 11% -> 4% of each run, Pallas kernels for 0% -> 0%
where the time goes in v3:
time: 262 us; the launch traced here: 260 us
  waiting for transfers between devices  141 us (54%)
  matrix products  61.5 us (23%)
  local copies, waits for them, and re-layouts  18.1 us (7%)
  other arithmetic  17.2 us (7%)
  between operations  15.8 us (6%)
  blocking collectives  6.56 us (3%)
    psum x1, waiting for transfers between devices, per_device(): lax.psum(jnp.dot(attended, o_weight, preferred_element_type=jnp.float32)....  66.2 us
    all_gather x1, waiting for transfers between devices, per_device(): lax.all_gather(jnp.stack([w_gate, w_up, w_down]), 'req', axis=1, tiled=True)  39.7 us
    unnamed x4, waiting for transfers between devices  34.9 us
    dot_general x1, matrix products, per_device(): lax.dot_general(act, weights[2], (((1,), (1,)), ((), ())), preferred_elem...  22 us
    dot_general x1, matrix products, per_device(): gate = jnp.dot(normed, weights[0], preferred_element_type=jnp.float32)  12.7 us
    dot_general x1, matrix products, attend(): jnp.einsum('rghd,tgd->rght', pre_q, pre_keys, preferred_element_type=jnp....  10.5 us
    dot_general x1, matrix products, attend(): jnp.einsum('rght,tgd->rghd', pre_weight.astype(jnp.bfloat16), pre_vals, p...  9.56 us
    reduce_sum x2, other arithmetic, rms(): jnp.mean(values * values, axis=-1, keepdims=True) + EPS  8.53 us
  transfers between devices with their start and end apart: 3, of which 3 were waited for; matrix products, arithmetic and copies ran while one was open for 4% of the time, Pallas kernels for 0%

profile of v3, /device:TPU:1, one launch (start us, length us, event | category | flops | bytes accessed | tf_op | source)
XLA Modules:
  0.0 260.0 jit_solution(16914655152772967113)
XLA Ops:
  7.4 0.8 fusion.48
  8.2 0.7 slice.26
  8.9 1.1 slice.25
  10.7 3.0 %iota_compare_fusion = pred[512,4096]{0,1:T(8,128)(4,1)} fusion(s32[512]{0:T(512)S(1)} %add_add_fusion), kind=kLoop, calls=%fused_computation.18 | loop fusion | flops 2097152 | bytes 2099200 | tf_op jit(solution)/shard_map/lt | solution.py:48
  13.7 0.2 copy.43
  13.9 4.5 %gather_fusion.1 = bf16[32,128,256]{2,1,0:T(8,128)(2,1)} fusion(bf16[80,128,256]{2,1,0:T(8,128)(2,1)} %param.15, s32[1024]{0:T(1024)S(1)} %pad_clamp_fusion), kind=kCustom, calls=%fused_computation.1 | custom fusion | bytes 4194432 | tf_op jit(solution)/shard_map/gather | solution.py:40
  18.4 4.5 %gather_fusion = bf16[32,128,256]{2,1,0:T(8,128)(2,1)} fusion(bf16[80,128,256]{2,1,0:T(8,128)(2,1)} %param.16, s32[1024]{0:T(1024)S(1)} %pad_clamp_fusion), kind=kCustom, calls=%fused_computation | custom fusion | bytes 4194432 | tf_op jit(solution)/shard_map/gather | solution.py:41
  22.9 0.1 broadcast_compare_fusion
  23.0 0.2 select_reduce_fusion
  23.2 0.2 add.104
  23.5 0.3 fusion.42
  23.7 0.0 copy-start.2
  23.7 0.0 copy-start.3
  23.7 0.0 slice-start
  23.7 0.0 slice-start.2
  23.8 10.5 %fusion = (f32[512,2]{0,1:T(2,128)S(1)}, f32[4096,512,2]{1,0,2:T(8,128)}) fusion(pred[512,4096]{0,1:T(8,128)(4,1)} %iota_compare_fusion, bf16[4096,256,1]{1,0,2:T(8,128)(2,1)} %bitcast.124, bf16[512,2,256]{0,2,1:T(8,128)(2,1)S(1)} %bitcast.134), kind=kOutput, calls=%fused_computation.3 | convolution fusion | flops 2164259840 | bytes 21499904 | tf_op jit(solution)/shard_map/rghd,tgd->rght/dot_general | solution.py:44
  34.2 0.0 copy-done.2
  34.2 0.0 slice-start.1
  34.2 0.0 slice-start.4
  34.2 0.0 slice-start.3
  34.3 9.6 %fusion.39 = bf16[512,1,2,256]{0,3,2,1:T(8,128)(2,1)S(1)} fusion(bf16[4096,256,1]{1,0,2:T(8,128)(2,1)S(1)} %bitcast.123, f32[4096,512,2]{1,0,2:T(8,128)} %get-tuple-element.10, pred[512,4096]{0,1:T(8,128)(4,1)S(1)} %copy-done.2, f32[512,2]{0,1:T(2,128)S(1)} %get-tuple-element.9), kind=kOutput, calls=%fused_computation.53 | convolution fusion | flops 2164785152 | bytes 21499904 | tf_op jit(solution)/shard_map/rght,tgd->rghd/dot_general | solution.py:50
  43.9 1.8 fusion.53
  45.6 2.1 fusion.36
  47.8 0.1 pad_maximum_fusion.1
  47.9 0.0 copy-start.4
  47.9 0.0 copy-start.5
  47.9 0.0 copy-start.6
  47.9 2.9 %convolution_convert_fusion = bf16[528,2304]{1,0:T(8,128)(2,1)} fusion(bf16[528,512]{0,1:T(8,128)(2,1)S(1)} %bitcast.132, bf16[512,2304]{1,0:T(8,128)(2,1)S(1)} %copy-done), kind=kOutput, calls=%fused_computation.39 | convolution fusion | flops 1246924800 | bytes 5332992 | tf_op jit(solution)/shard_map/dot_general | solution.py:110
  50.8 0.0 all-reduce.2.cloned.1.call-update
  50.8 0.0 all-gather.2.cloned.1.call-start
  50.9 1.1 pad_maximum_fusion
  52.0 0.0 all-gather.2.cloned.1.call-update
  52.0 0.0 reduce-scatter.4.cloned.1.call-start
  52.1 66.2 %all-reduce.2.cloned.1.call-done = bf16[528,2304]{1,0:T(8,128)(2,1)} async-done(((bf16[528,2304]{1,0:T(8,128)(2,1)}), bf16[528,2304]{1,0:T(8,128)(2,1)}) %all-reduce.2.cloned.1.call-update) | async-done | bytes 2433040 | tf_op jit(solution)/shard_map/psum | solution.py:109
  118.3 2.2 fusion.15
  120.5 0.0 copy-start.9
  120.5 6.3 %multiply_reduce_fusion = (f32[528]{0:T(1024)S(1)}, f32[528,2304]{1,0:T(8,128)}) fusion(f32[2304]{0:T(1024)S(1)} %copy-done.7, f32[528]{0:T(1024)S(1)} %add_rsqrt_fusion.1, bf16[528,2304]{1,0:T(8,128)(2,1)} %all-reduce.2.cloned.1.call-done, bf16[528,2304]{1,0:T(8,128)(2,1)} %param.20), kind=kLoop, calls=%fused_computation.36 | loop fusion | flops 8515056 | bytes 9745536 | tf_op jit(solution)/shard_map/reduce_sum | solution.py:20
  126.9 39.7 %all-gather.2.cloned.1.call-done = bf16[3,2304,2304]{2,1,0:T(8,128)(2,1)} async-done(((bf16[3,72,2304]{2,1,0:T(8,128)(2,1)}), bf16[3,2304,2304]{2,1,0:T(8,128)(2,1)}) %all-gather.2.cloned.1.call-update) | async-done | bytes 31850512 | tf_op jit(solution)/shard_map/all_gather | solution.py:105
  166.6 12.7 %fusion.24 = f32[528,2304]{1,0:T(8,128)} fusion(bf16[3,2304,2304]{2,1,0:T(8,128)(2,1)} %all-gather.2.cloned.1.call-done, f32[528,2304]{1,0:T(8,128)} %get-tuple-element.6, f32[2304]{0:T(1024)S(1)} %copy-done.9, f32[528]{0:T(1024)S(1)} %add_rsqrt_fusion), kind=kOutput, calls=%fused_computation.34 | convolution fusion | flops 5619068928 | bytes 20360256 | tf_op jit(solution)/shard_map/dot_general | solution.py:114
  179.2 22.0 %fusion.26 = bf16[528,2304]{1,0:T(8,128)(2,1)} fusion(bf16[3,2304,2304]{2,1,0:T(8,128)(2,1)} %all-gather.2.cloned.1.call-done, f32[528,2304]{1,0:T(8,128)} %fusion.24, f32[528,2304]{1,0:T(8,128)} %get-tuple-element.6, f32[2304]{0:T(1024)S(1)} %copy-done.9, f32[528]{0:T(1024)S(1)} %add_rsqrt_fusion), kind=kOutput, calls=%fused_computation.38 | convolution fusion | flops 11218673664 | bytes 33410112 | tf_op jit(solution)/shard_map/dot_general | solution.py:117
  201.3 4.6 %copy.41 = bf16[528,2304]{0,1:T(8,128)(2,1)} copy(bf16[528,2304]{1,0:T(8,128)(2,1)} %fusion.26) | data formatting | bytes 4866048
  205.9 0.0 reduce-scatter.4.cloned.1.call-update
  205.9 0.8 dynamic_slice.7
  206.7 34.8 %reduce-scatter.4.cloned.1.call-done = bf16[576,528]{1,0:T(8,128)(2,1)} async-done(((bf16[2304,528]{1,0:T(8,128)(2,1)}), bf16[576,528]{1,0:T(8,128)(2,1)}) %reduce-scatter.4.cloned.1.call-update) | async-done | bytes 608272
  241.5 1.4 copy.42
  242.9 0.2 fusion.30
  243.2 6.6 %psum.15 = f32[528,1]{0,1:T(1,128)S(1)} all-reduce(f32[528,1]{0,1:T(1,128)S(1)} %broadcast_in_dim.44), channel_id=1, replica_groups=mesh['req'=32,'mlp'=4] {'mlp'}, use_global_device_ids=true, to_apply=%region_8.9 | all-reduce | flops 528 | bytes 4224 | tf_op jit(solution)/shard_map/psum | solution.py:125
  249.8 2.8 %fusion.33 = bf16[528,576]{1,0:T(8,128)(2,1)} fusion(bf16[528,576]{1,0:T(8,128)(2,1)S(1)} %copy.42, f32[528,2304]{1,0:T(8,128)} %get-tuple-element.6, s32[]{:T(128)S(6)} %select_n.31, f32[576]{0:T(1024)S(1)} %dynamic_slice.7, f32[528]{0:T(1024)S(1)} %rsqrt_reduce_fusion), kind=kLoop, calls=%fused_computation.46 | loop fusion | flops 1520640 | bytes 2437444 | tf_op jit(solution)/shard_map/convert_element_type | solution.py:129
  (29 shorter events, 0.1 us)
Async XLA Ops:
  7.4 40.5 %copy-start = (bf16[512,2304]{1,0:T(8,128)(2,1)S(1)}, bf16[512,2304]{1,0:T(8,128)(2,1)}, u32[]{:S(2)}) copy-start(bf16[512,2304]{1,0:T(8,128)(2,1)} %param.21) | copy-start | bytes 7077892
  7.4 110.9 %all-reduce.2.cloned.1.call-start = ((), (), s32[]{:S(2)}) async-start(), calls=%async_computation.1 | async-start | bytes 4866048 | tf_op jit(solution)/shard_map/psum | solution.py:109
  13.7 9.2 %copy-start.8 = (s32[16]{0:T(128)S(1)}, s32[16]{0:T(128)}, u32[]{:S(2)}) copy-start(s32[16]{0:T(128)} %param.17) | copy-start | bytes 196
  23.7 10.5 %copy-start.2 = (pred[512,4096]{0,1:T(8,128)(4,1)S(1)}, pred[512,4096]{0,1:T(8,128)(4,1)}, u32[]{:S(2)}) copy-start(pred[512,4096]{0,1:T(8,128)(4,1)} %iota_compare_fusion) | copy-start | bytes 6291460
  23.7 10.5 %copy-start.3 = (bf16[32,128,256]{2,1,0:T(8,128)(2,1)S(1)}, bf16[32,128,256]{2,1,0:T(8,128)(2,1)}, u32[]{:S(2)}) copy-start(bf16[32,128,256]{2,1,0:T(8,128)(2,1)} %gather_fusion) | copy-start | bytes 6291460
  23.7 20.1 %slice-start = ((s8[5242880]{0:T(1024)(128)(4,1)}), s8[4194304]{0:T(1024)(128)(4,1)S(1)}, s32[]{:S(2)}) async-start(s8[5242880]{0:T(1024)(128)(4,1)} %bitcast.125), calls=%async_computation.4 | async-start | bytes 8388608
  23.7 21.9 %slice-start.2 = ((s8[5242880]{0:T(1024)(128)(4,1)}), s8[4194304]{0:T(1024)(128)(4,1)S(1)}, s32[]{:S(2)}) async-start(s8[5242880]{0:T(1024)(128)(4,1)} %bitcast.128), calls=%async_computation.6 | async-start | bytes 8388608
  34.2 9.6 %slice-start.1 = ((s8[5242880]{0:T(1024)(128)(4,1)}), s8[1048576]{0:T(1024)(128)(4,1)S(1)}, s32[]{:S(2)}) async-start(s8[5242880]{0:T(1024)(128)(4,1)} %bitcast.125), calls=%async_computation.5 | async-start | bytes 2097152
  34.2 9.6 %slice-start.4 = ((bf16[528,512]{1,0:T(8,128)(2,1)}), bf16[16,512]{1,0:T(8,128)(2,1)S(1)}, s32[]{:S(2)}) async-start(bf16[528,512]{1,0:T(8,128)(2,1)} %param.14), calls=%async_computation.8 | async-start | bytes 32768 | tf_op jit(solution)/shard_map/slice | solution.py:37
  34.2 11.4 %slice-start.3 = ((s8[5242880]{0:T(1024)(128)(4,1)}), s8[1048576]{0:T(1024)(128)(4,1)S(1)}, s32[]{:S(2)}) async-start(s8[5242880]{0:T(1024)(128)(4,1)} %bitcast.128), calls=%async_computation.7 | async-start | bytes 2097152
  47.9 3.0 %copy-start.4 = (bf16[72,2304]{1,0:T(8,128)(2,1)S(1)}, bf16[72,2304]{1,0:T(8,128)(2,1)}, u32[]{:S(2)}) copy-start(bf16[72,2304]{1,0:T(8,128)(2,1)} %param.27) | copy-start | bytes 995332
  47.9 3.0 %copy-start.5 = (bf16[72,2304]{1,0:T(8,128)(2,1)S(1)}, bf16[72,2304]{1,0:T(8,128)(2,1)}, u32[]{:S(2)}) copy-start(bf16[72,2304]{1,0:T(8,128)(2,1)} %param.26) | copy-start | bytes 995332
  47.9 3.0 %copy-start.6 = (bf16[72,2304]{1,0:T(8,128)(2,1)S(1)}, bf16[72,2304]{1,0:T(8,128)(2,1)}, u32[]{:S(2)}) copy-start(bf16[72,2304]{1,0:T(8,128)(2,1)} %param.25) | copy-start | bytes 995332
  50.8 69.7 %copy-start.7 = (f32[2304]{0:T(1024)S(1)}, f32[2304]{0:T(1024)}, u32[]{:S(2)}) copy-start(f32[2304]{0:T(1024)} %param.22) | copy-start | bytes 27652
  50.8 115.7 %all-gather.2.cloned.1.call-start = ((), (), s32[]{:S(2)}) async-start(), calls=%async_computation.2 | async-start | bytes 32845824 | tf_op jit(solution)/shard_map/all_gather | solution.py:105
  52.0 189.5 %reduce-scatter.4.cloned.1.call-start = ((), (), s32[]{:S(2)}) async-start(), calls=%async_computation.3 | async-start | bytes 3686400
  120.5 46.0 %copy-start.9 = (f32[2304]{0:T(1024)S(1)}, f32[2304]{0:T(1024)}, u32[]{:S(2)}) copy-start(f32[2304]{0:T(1024)} %param.23) | copy-start | bytes 27652
  201.3 51.3 %copy-start.1 = (bf16[512,2304]{1,0:T(8,128)(2,1)S(1)}, bf16[512,2304]{1,0:T(8,128)(2,1)}, u32[]{:S(2)}) copy-start(bf16[512,2304]{1,0:T(8,128)(2,1)} %param.21) | copy-start | bytes 7077892
Sparse Core Ops, SparseCore 0:
  51.0 67.2 all-reduce.1
  206.0 35.4 reduce-scatter.3
Sparse Core Ops, SparseCore 1:
  53.7 112.8 all-gather.1

commit v4 on v3

--- a/solution.py
+++ b/solution.py
@@ -1,9 +1,8 @@
-import math
-
 import jax
 import jax.numpy as jnp
 from jax import lax
 from jax.sharding import PartitionSpec as P
+
 
 H = 8
 KVH = 4
@@ -86,6 +85,25 @@
     return jnp.concatenate([pre_out, dec_out], axis=0).reshape(rows, local_kv * rep * HD)
 
 
+def ring_sum(partial, axis):
+    count = lax.axis_size(axis)
+    me = lax.axis_index(axis)
+    rows = partial.shape[0] // count
+    chunks = partial.reshape(count, rows, partial.shape[1])
+    total = jnp.take(chunks, me, axis=0).astype(jnp.float32)
+    for shift in range(1, count):
+        sent = jnp.take(chunks, (me + shift) % count, axis=0)
+        pairs = [(j, (j + shift) % count) for j in range(count)]
+        total = total + lax.ppermute(sent, axis, pairs).astype(jnp.float32)
+    reduced = total.astype(jnp.bfloat16)
+    pieces = [reduced]
+    for shift in range(1, count):
+        pairs = [(j, (j + shift) % count) for j in range(count)]
+        pieces.append(lax.ppermute(reduced, axis, pairs))
+    order = (me - jnp.arange(count, dtype=jnp.int32)) % count
+    return jnp.take(jnp.stack(pieces), order, axis=0).reshape(partial.shape)
+
+
 def per_device(
     queries,
     key_cache,
@@ -106,7 +124,7 @@
         jnp.stack([w_gate, w_up, w_down]), "req", axis=1, tiled=True
     )
     attended = attend(queries, key_cache, value_cache, decode_len, stretch_start, page_table)
-    projected = lax.psum(
+    projected = ring_sum(
         jnp.dot(attended, o_weight, preferred_element_type=jnp.float32).astype(jnp.bfloat16), "mlp"
     ).astype(jnp.float32)
     resid = hidden_in.astype(jnp.float32) + rms(projected, attn_gain)

time: 262 us -> 225 us (0.86)
  waiting for transfers between devices: 141 us -> 91.3 us
  starting transfers between devices: 0.09 us -> 10.3 us
  local copies, waits for them, and re-layouts: 18.1 us -> 23.6 us
  matrix products: 61.5 us -> 57.5 us
    psum x1 -> x0, waiting for transfers between devices: 66.2 us -> none  [per_device(): lax.psum(jnp.dot(attended, o_weight, preferred_element_type=jnp.float32)....]
    ppermute x0 -> x6, waiting for transfers between devices: none -> 53 us  [the longest x3 26.7 us: ring_sum(): pieces.append(lax.ppermute(reduced, axis, pairs))]
    all_gather x1, waiting for transfers between devices: 39.7 us -> 0.01 us  [per_device(): lax.all_gather(jnp.stack([w_gate, w_up, w_down]), 'req', axis=1, tiled=True)]
    ppermute x0 -> x6, starting transfers between devices: none -> 10.3 us  [the longest x3 6.02 us: ring_sum(): total = total + lax.ppermute(sent, axis, pairs).astype(jnp.float32)]
    gather x0 -> x2, local copies, waits for them, and re-layouts: none -> 4.12 us  [ring_sum(): return jnp.take(jnp.stack(pieces), order, axis=0).reshape(partial.shape)]
    dot_general x1, matrix products: 10.5 us -> 6.71 us  [attend(): jnp.einsum('rghd,tgd->rght', pre_q, pre_keys, preferred_element_type=jnp....]
    unnamed x4 -> x3, waiting for transfers between devices: 34.9 us -> 38.4 us
    dot_general x1, matrix products: 9.56 us -> 6.16 us  [attend(): jnp.einsum('rght,tgd->rghd', pre_weight.astype(jnp.bfloat16), pre_vals, p...]
  transfers between devices with their start and end apart: 3 -> 8, of which waited for: 3 -> 5; matrix products, arithmetic and copies ran while one was open for 4% -> 24% of each run, Pallas kernels for 0% -> 0%
where the time goes in v4:
time: 225 us; the launch traced here: 223 us
  waiting for transfers between devices  91.3 us (41%)
  matrix products  57.5 us (26%)
  local copies, waits for them, and re-layouts  23.6 us (10%)
  other arithmetic  19.5 us (9%)
  between operations  14.4 us (6%)
  starting transfers between devices  10.3 us (5%)
  blocking collectives  6.57 us (3%)
    unnamed x3, waiting for transfers between devices  38.4 us
    ppermute x3, waiting for transfers between devices, ring_sum(): pieces.append(lax.ppermute(reduced, axis, pairs))  26.7 us
    ppermute x3, waiting for transfers between devices, ring_sum(): total = total + lax.ppermute(sent, axis, pairs).astype(jnp.float32)  26.2 us
    dot_general x1, matrix products, per_device(): lax.dot_general(act, weights[2], (((1,), (1,)), ((), ())), preferred_elem...  22 us
    dot_general x1, matrix products, per_device(): gate = jnp.dot(normed, weights[0], preferred_element_type=jnp.float32)  12.7 us
    reduce_sum x2, other arithmetic, rms(): jnp.mean(values * values, axis=-1, keepdims=True) + EPS  6.75 us
    dot_general x1, matrix products, attend(): jnp.einsum('rghd,tgd->rght', pre_q, pre_keys, preferred_element_type=jnp....  6.71 us
    psum x1, blocking collectives, per_device(): square = lax.psum(jnp.sum(total * total, axis=-1, keepdims=True), 'mlp')  6.57 us
  transfers between devices with their start and end apart: 8, of which 5 were waited for; matrix products, arithmetic and copies ran while one was open for 24% of the time, Pallas kernels for 0%

profile of v4, /device:TPU:1, one launch (start us, length us, event | category | flops | bytes accessed | tf_op | source)
XLA Modules:
  0.0 223.2 jit_solution(8581690460030437519)
XLA Ops:
  6.5 2.4 %pad_maximum_fusion.1 = bf16[3,72,2304]{2,1,0:T(8,128)(2,1)} fusion(bf16[1,72,2304]{2,1,0:T(8,128)(2,1)} %bitcast.151, bf16[1,72,2304]{2,1,0:T(8,128)(2,1)} %bitcast.152, bf16[1,72,2304]{2,1,0:T(8,128)(2,1)} %bitcast.153), kind=kLoop, calls=%fused_computation.52 | loop fusion | flops 995328 | bytes 1990656 | tf_op jit(solution)/shard_map/stack | solution.py:124
  8.9 0.0 all-gather.2.cloned.1.call-update
  9.0 0.0 reduce-scatter.4.cloned.1.call-start
  9.1 1.1 slice.25
  10.8 0.2 copy.43
  11.1 4.5 %gather_fusion.1 = bf16[32,128,256]{2,1,0:T(8,128)(2,1)} fusion(bf16[80,128,256]{2,1,0:T(8,128)(2,1)} %param.17, s32[1024]{0:T(1024)S(1)} %pad_clamp_fusion.1), kind=kCustom, calls=%fused_computation.1 | custom fusion | bytes 4194432 | tf_op jit(solution)/shard_map/gather | solution.py:39
  15.6 4.5 %gather_fusion = bf16[32,128,256]{2,1,0:T(8,128)(2,1)} fusion(bf16[80,128,256]{2,1,0:T(8,128)(2,1)} %param.18, s32[1024]{0:T(1024)S(1)} %pad_clamp_fusion.1), kind=kCustom, calls=%fused_computation | custom fusion | bytes 4194432 | tf_op jit(solution)/shard_map/gather | solution.py:40
  20.1 0.1 broadcast_compare_fusion
  20.1 0.2 select_reduce_fusion
  20.4 0.2 add.168
  20.6 0.3 fusion.39
  20.9 4.9 %fusion.52 = (f32[16,2]{0,1:T(2,128)S(1)}, bf16[16,1,2,10240]{3,0,2,1:T(8,128)(2,1)S(1)}) fusion(bf16[10240,256,1]{1,0,2:T(8,128)(2,1)} %bitcast.140, bf16[2,2,8,256]{3,2,1,0:T(8,128)(2,1)S(1)} %bitcast.149, pred[16,10240]{1,0:T(8,128)(4,1)S(1)} %fusion.39), kind=kOutput, calls=%fused_computation.93 | convolution fusion | flops 169410528 | bytes 6078592 | tf_op jit(solution)/shard_map/rghd,tgd->rght/dot_general | solution.py:71
  25.8 2.1 fusion.33
  28.0 1.7 iota_compare_fusion
  29.7 6.7 %fusion = (f32[512,2]{0,1:T(2,128)S(1)}, f32[4096,512,2]{1,0,2:T(8,128)S(1)}) fusion(pred[512,4096]{0,1:T(8,128)(4,1)S(1)} %iota_compare_fusion, bf16[4096,256,1]{1,0,2:T(8,128)(2,1)S(1)} %bitcast.139, bf16[512,2,256]{0,2,1:T(8,128)(2,1)S(1)} %bitcast.150), kind=kOutput, calls=%fused_computation.4 | convolution fusion | flops 2164259840 | bytes 21499904 | tf_op jit(solution)/shard_map/rghd,tgd->rght/dot_general | solution.py:43
  36.4 6.2 %fusion.36 = bf16[512,1,2,256]{0,3,2,1:T(8,128)(2,1)S(1)} fusion(bf16[4096,256,1]{1,0,2:T(8,128)(2,1)S(1)} %bitcast.138, f32[4096,512,2]{1,0,2:T(8,128)S(1)} %get-tuple-element.25, pred[512,4096]{0,1:T(8,128)(4,1)S(1)} %iota_compare_fusion, f32[512,2]{0,1:T(2,128)S(1)} %get-tuple-element.24), kind=kOutput, calls=%fused_computation.53 | convolution fusion | flops 2164785152 | bytes 21499904 | tf_op jit(solution)/shard_map/rght,tgd->rghd/dot_general | solution.py:49
  42.6 0.1 pad_maximum_fusion.2
  42.7 2.9 %convolution_convert_fusion = bf16[528,2304]{1,0:T(8,128)(2,1)} fusion(bf16[528,512]{0,1:T(8,128)(2,1)S(1)} %bitcast.145, bf16[512,2304]{1,0:T(8,128)(2,1)S(1)} %copy-done), kind=kOutput, calls=%fused_computation.37 | convolution fusion | flops 1246924800 | bytes 5332992 | tf_op jit(solution)/shard_map/dot_general | solution.py:128
  45.6 1.9 reshape.297
  47.5 1.3 select_bitcast_fusion.2
  48.8 2.3 %collective-permute-start = (bf16[132,2304]{1,0:T(8,128)(2,1)}, bf16[132,2304]{1,0:T(8,128)(2,1)S(1)}, u32[]{:S(2)}, u32[]{:S(2)}) collective-permute-start(bf16[132,2304]{1,0:T(8,128)(2,1)} %get-tuple-element.19), channel_id=1, source_target_pairs={{0,1},{1,2},{2,3},{3,0},{4,5},{5,6},{6,7},{7,4},{8,9},{9,10},{10,1... | collective-permute-start | bytes 1824776 | tf_op jit(solution)/shard_map/ppermute | solution.py:97
  51.2 2.6 %collective-permute-start.1 = (bf16[132,2304]{1,0:T(8,128)(2,1)}, bf16[132,2304]{1,0:T(8,128)(2,1)}, u32[]{:S(2)}, u32[]{:S(2)}) collective-permute-start(bf16[132,2304]{1,0:T(8,128)(2,1)} %get-tuple-element.21), channel_id=1, source_target_pairs={{0,2},{1,3},{2,0},{3,1},{4,6},{5,7},{6,4},{7,5},{8,10},{9,11},{10,... | collective-permute-start | bytes 1824776 | tf_op jit(solution)/shard_map/ppermute | solution.py:97
  53.8 1.1 collective-permute-start.2
  54.9 11.8 %collective-permute-done = bf16[132,2304]{1,0:T(8,128)(2,1)S(1)} collective-permute-done((bf16[132,2304]{1,0:T(8,128)(2,1)}, bf16[132,2304]{1,0:T(8,128)(2,1)S(1)}, u32[]{:S(2)}, u32[]{:S(2)}) %collective-permute-start) | collective-permute-done | bytes 608288 | tf_op jit(solution)/shard_map/ppermute | solution.py:97
  66.6 14.5 %collective-permute-done.1 = bf16[132,2304]{1,0:T(8,128)(2,1)} collective-permute-done((bf16[132,2304]{1,0:T(8,128)(2,1)}, bf16[132,2304]{1,0:T(8,128)(2,1)}, u32[]{:S(2)}, u32[]{:S(2)}) %collective-permute-start.1) | collective-permute-done | bytes 608288 | tf_op jit(solution)/shard_map/ppermute | solution.py:97
  81.1 1.8 add_convert_fusion
  82.9 1.1 collective-permute-start.3
  84.0 2.9 %collective-permute-start.4 = (bf16[132,2304]{1,0:T(8,128)(2,1)S(1)}, bf16[132,2304]{1,0:T(8,128)(2,1)S(1)}, u32[]{:S(2)}, u32[]{:S(2)}) collective-permute-start(bf16[132,2304]{1,0:T(8,128)(2,1)S(1)} %add_convert_fusion), channel_id=1, source_target_pairs={{0,2},{1,3},{2,0},{3,1},{4,6},{5,7},{6,4},{7,5},{8,10},{9,11},{10,... | collective-permute-start | bytes 1824776 | tf_op jit(solution)/shard_map/ppermute | solution.py:102
  87.0 0.2 collective-permute-start.5
  87.2 0.1 broadcast_in_dim.87
  87.3 0.1 broadcast_in_dim.88
  87.4 11.4 %collective-permute-done.3 = bf16[132,2304]{1,0:T(8,128)(2,1)S(1)} collective-permute-done((bf16[132,2304]{1,0:T(8,128)(2,1)S(1)}, bf16[132,2304]{1,0:T(8,128)(2,1)S(1)}, u32[]{:S(2)}, u32[]{:S(2)}) %collective-permute-start.3) | collective-permute-done | bytes 608288 | tf_op jit(solution)/shard_map/ppermute | solution.py:102
  98.7 15.4 %collective-permute-done.4 = bf16[132,2304]{1,0:T(8,128)(2,1)S(1)} collective-permute-done((bf16[132,2304]{1,0:T(8,128)(2,1)S(1)}, bf16[132,2304]{1,0:T(8,128)(2,1)S(1)}, u32[]{:S(2)}, u32[]{:S(2)}) %collective-permute-start.4) | collective-permute-done | bytes 608288 | tf_op jit(solution)/shard_map/ppermute | solution.py:102
  114.1 1.8 pad_maximum_fusion
  115.9 2.4 %gather_fusion.2 = bf16[4,132,2304]{2,1,0:T(8,128)(2,1)S(1)} fusion(bf16[4,132,2304]{2,1,0:T(8,128)(2,1)} %pad_maximum_fusion, s32[1024]{0:T(1024)S(1)} %pad_clamp_fusion), kind=kCustom, calls=%fused_computation.2 | custom fusion | bytes 4866064 | tf_op jit(solution)/shard_map/jit(_take)/gather | solution.py:104
  118.3 1.7 gather.18
  120.0 0.8 multiply_reduce_fusion
  120.8 0.1 rsqrt.23
  120.9 5.9 %multiply_reduce_fusion.1 = (f32[528]{0:T(1024)S(1)}, f32[528,2304]{1,0:T(8,128)}) fusion(f32[2304]{0:T(1024)S(1)} %copy-done.5, f32[528]{0:T(1024)S(1)} %rsqrt.23, bf16[528,2304]{1,0:T(8,128)(2,1)} %gather.18, pred[528]{0:T(1024)(128)(4,1)S(1)} %broadcast_in_dim.88, bf16[528,2304]{1,0:T(8,128)(2,1)} %param.22), kind=kLoop, calls=%fused_computation.33 | loop fusion | flops 9731568 | bytes 9746064 | tf_op jit(solution)/shard_map/reduce_sum | solution.py:19
  126.9 12.7 %fusion.21 = f32[528,2304]{1,0:T(8,128)} fusion(bf16[3,2304,2304]{2,1,0:T(8,128)(2,1)} %all-gather.2.cloned.1.call-done, f32[528,2304]{1,0:T(8,128)} %get-tuple-element.18, f32[2304]{0:T(1024)S(1)} %copy-done.8, f32[528]{0:T(1024)S(1)} %add_rsqrt_fusion), kind=kOutput, calls=%fused_computation.31 | convolution fusion | flops 5619068928 | bytes 20360256 | tf_op jit(solution)/shard_map/dot_general | solution.py:132
  139.6 22.0 %fusion.23 = bf16[528,2304]{1,0:T(8,128)(2,1)} fusion(bf16[3,2304,2304]{2,1,0:T(8,128)(2,1)} %all-gather.2.cloned.1.call-done, f32[528,2304]{1,0:T(8,128)} %fusion.21, f32[528,2304]{1,0:T(8,128)} %get-tuple-element.18, f32[2304]{0:T(1024)S(1)} %copy-done.8, f32[528]{0:T(1024)S(1)} %add_rsqrt_fusion), kind=kOutput, calls=%fused_computation.36 | convolution fusion | flops 11218673664 | bytes 33410112 | tf_op jit(solution)/shard_map/dot_general | solution.py:135
  161.6 4.6 %copy.41 = bf16[528,2304]{0,1:T(8,128)(2,1)} copy(bf16[528,2304]{1,0:T(8,128)(2,1)} %fusion.23) | data formatting | bytes 4866048
  166.2 0.8 dynamic_slice.7
  167.0 38.3 %reduce-scatter.4.cloned.1.call-done = bf16[576,528]{1,0:T(8,128)(2,1)} async-done(((bf16[2304,528]{1,0:T(8,128)(2,1)}), bf16[576,528]{1,0:T(8,128)(2,1)}) %reduce-scatter.4.cloned.1.call-update) | async-done | bytes 608272
  205.3 1.4 copy.42
  206.8 0.2 fusion.27
  207.0 6.6 %psum.7 = f32[528,1]{0,1:T(1,128)S(1)} all-reduce(f32[528,1]{0,1:T(1,128)S(1)} %broadcast_in_dim.99), channel_id=1, replica_groups=mesh['req'=32,'mlp'=4] {'mlp'}, use_global_device_ids=true, to_apply=%region_7.9 | all-reduce | flops 528 | bytes 4224 | tf_op jit(solution)/shard_map/psum | solution.py:143
  213.6 2.8 %fusion.30 = bf16[528,576]{1,0:T(8,128)(2,1)} fusion(bf16[528,576]{1,0:T(8,128)(2,1)S(1)} %copy.42, f32[528,2304]{1,0:T(8,128)} %get-tuple-element.18, s32[]{:T(128)S(6)} %select_n.102, f32[576]{0:T(1024)S(1)} %dynamic_slice.7, f32[528]{0:T(1024)S(1)} %rsqrt_reduce_fusion), kind=kLoop, calls=%fused_computation.45 | loop fusion | flops 1520640 | bytes 2437444 | tf_op jit(solution)/shard_map/convert_element_type | solution.py:147
  (43 shorter events, 0.2 us)
Async XLA Ops:
  6.5 36.1 %copy-start = (bf16[512,2304]{1,0:T(8,128)(2,1)S(1)}, bf16[512,2304]{1,0:T(8,128)(2,1)}, u32[]{:S(2)}) copy-start(bf16[512,2304]{1,0:T(8,128)(2,1)} %param.23) | copy-start | bytes 7077892
  6.5 4.5 %copy-start.6 = (s32[17,32]{1,0:T(8,128)S(1)}, s32[17,32]{1,0:T(8,128)}, u32[]{:S(2)}) copy-start(s32[17,32]{1,0:T(8,128)} %param.21) | copy-start | bytes 6532
  6.5 120.3 %all-gather.2.cloned.1.call-start = ((), (), s32[]{:S(2)}) async-start(), calls=%async_computation.1 | async-start | bytes 32845824 | tf_op jit(solution)/shard_map/all_gather | solution.py:123
  9.0 196.4 %reduce-scatter.4.cloned.1.call-start = ((), (), s32[]{:S(2)}) async-start(), calls=%async_computation.2 | async-start | bytes 3686400
  10.1 9.9 %copy-start.7 = (s32[16]{0:T(128)S(1)}, s32[16]{0:T(128)}, u32[]{:S(2)}) copy-start(s32[16]{0:T(128)} %param.19) | copy-start | bytes 196
  11.1 9.8 %slice-start.2 = ((bf16[528,512]{1,0:T(8,128)(2,1)}), bf16[16,512]{1,0:T(8,128)(2,1)S(1)}, s32[]{:S(2)}) async-start(bf16[528,512]{1,0:T(8,128)(2,1)} %param.16), calls=%async_computation.5 | async-start | bytes 32768 | tf_op jit(solution)/shard_map/slice | solution.py:36
  20.6 5.2 %slice-start = ((s8[5242880]{0:T(1024)(128)(4,1)}), s8[4194304]{0:T(1024)(128)(4,1)S(1)}, s32[]{:S(2)}) async-start(s8[5242880]{0:T(1024)(128)(4,1)} %bitcast.141), calls=%async_computation.3 | async-start | bytes 8388608
  20.9 4.9 %slice-start.1 = ((s8[5242880]{0:T(1024)(128)(4,1)}), s8[1048576]{0:T(1024)(128)(4,1)S(1)}, s32[]{:S(2)}) async-start(s8[5242880]{0:T(1024)(128)(4,1)} %bitcast.141), calls=%async_computation.4 | async-start | bytes 2097152
  25.8 3.9 %copy-start.3 = (bf16[32,128,256]{2,1,0:T(8,128)(2,1)S(1)}, bf16[32,128,256]{2,1,0:T(8,128)(2,1)}, u32[]{:S(2)}) copy-start(bf16[32,128,256]{2,1,0:T(8,128)(2,1)} %gather_fusion.1) | copy-start | bytes 6291460
  29.7 6.7 %copy-start.2 = (bf16[32,128,256]{2,1,0:T(8,128)(2,1)S(1)}, bf16[32,128,256]{2,1,0:T(8,128)(2,1)}, u32[]{:S(2)}) copy-start(bf16[32,128,256]{2,1,0:T(8,128)(2,1)} %gather_fusion) | copy-start | bytes 6291460
  48.8 17.8 %collective-permute-start = (bf16[132,2304]{1,0:T(8,128)(2,1)}, bf16[132,2304]{1,0:T(8,128)(2,1)S(1)}, u32[]{:S(2)}, u32[]{:S(2)}) collective-permute-start(bf16[132,2304]{1,0:T(8,128)(2,1)} %get-tuple-element.19), channel_id=1, source_target_pairs={{0,1},{1,2},{2,3},{3,0},{4,5},{5,6},{6,7},{7,4},{8,9},{9,10},{10,1... | collective-permute-start | bytes 1824776 | tf_op jit(solution)/shard_map/ppermute | solution.py:97
  51.2 29.9 %collective-permute-start.1 = (bf16[132,2304]{1,0:T(8,128)(2,1)}, bf16[132,2304]{1,0:T(8,128)(2,1)}, u32[]{:S(2)}, u32[]{:S(2)}) collective-permute-start(bf16[132,2304]{1,0:T(8,128)(2,1)} %get-tuple-element.21), channel_id=1, source_target_pairs={{0,2},{1,3},{2,0},{3,1},{4,6},{5,7},{6,4},{7,5},{8,10},{9,11},{10,... | collective-permute-start | bytes 1824776 | tf_op jit(solution)/shard_map/ppermute | solution.py:97
  53.8 27.3 %collective-permute-start.2 = (bf16[132,2304]{1,0:T(8,128)(2,1)}, bf16[132,2304]{1,0:T(8,128)(2,1)}, u32[]{:S(2)}, u32[]{:S(2)}) collective-permute-start(bf16[132,2304]{1,0:T(8,128)(2,1)} %get-tuple-element.20), channel_id=1, source_target_pairs={{0,3},{1,0},{2,1},{3,2},{4,7},{5,4},{6,5},{7,6},{8,11},{9,8},{10,9... | collective-permute-start | bytes 1824776 | tf_op jit(solution)/shard_map/ppermute | solution.py:97
  66.6 14.5 %copy-start.4 = (bf16[132,2304]{1,0:T(8,128)(2,1)}, bf16[132,2304]{1,0:T(8,128)(2,1)S(1)}, u32[]{:S(2)}) copy-start(bf16[132,2304]{1,0:T(8,128)(2,1)S(1)} %collective-permute-done) | copy-start | bytes 1824772
  82.9 15.8 %collective-permute-start.3 = (bf16[132,2304]{1,0:T(8,128)(2,1)S(1)}, bf16[132,2304]{1,0:T(8,128)(2,1)S(1)}, u32[]{:S(2)}, u32[]{:S(2)}) collective-permute-start(bf16[132,2304]{1,0:T(8,128)(2,1)S(1)} %add_convert_fusion), channel_id=1, source_target_pairs={{0,1},{1,2},{2,3},{3,0},{4,5},{5,6},{6,7},{7,4},{8,9},{9,10},{10,1... | collective-permute-start | bytes 1824776 | tf_op jit(solution)/shard_map/ppermute | solution.py:102
  84.0 30.1 %collective-permute-start.4 = (bf16[132,2304]{1,0:T(8,128)(2,1)S(1)}, bf16[132,2304]{1,0:T(8,128)(2,1)S(1)}, u32[]{:S(2)}, u32[]{:S(2)}) collective-permute-start(bf16[132,2304]{1,0:T(8,128)(2,1)S(1)} %add_convert_fusion), channel_id=1, source_target_pairs={{0,2},{1,3},{2,0},{3,1},{4,6},{5,7},{6,4},{7,5},{8,10},{9,11},{10,... | collective-permute-start | bytes 1824776 | tf_op jit(solution)/shard_map/ppermute | solution.py:102
  87.0 27.1 %collective-permute-start.5 = (bf16[132,2304]{1,0:T(8,128)(2,1)S(1)}, bf16[132,2304]{1,0:T(8,128)(2,1)S(1)}, u32[]{:S(2)}, u32[]{:S(2)}) collective-permute-start(bf16[132,2304]{1,0:T(8,128)(2,1)S(1)} %add_convert_fusion), channel_id=1, source_target_pairs={{0,3},{1,0},{2,1},{3,2},{4,7},{5,4},{6,5},{7,6},{8,11},{9,8},{10,9... | collective-permute-start | bytes 1824776 | tf_op jit(solution)/shard_map/ppermute | solution.py:102
  118.3 2.6 %copy-start.5 = (f32[2304]{0:T(1024)S(1)}, f32[2304]{0:T(1024)}, u32[]{:S(2)}) copy-start(f32[2304]{0:T(1024)} %param.24) | copy-start | bytes 27652
  120.9 6.0 %copy-start.8 = (f32[2304]{0:T(1024)S(1)}, f32[2304]{0:T(1024)}, u32[]{:S(2)}) copy-start(f32[2304]{0:T(1024)} %param.25) | copy-start | bytes 27652
  161.6 54.8 %copy-start.1 = (bf16[512,2304]{1,0:T(8,128)(2,1)S(1)}, bf16[512,2304]{1,0:T(8,128)(2,1)}, u32[]{:S(2)}) copy-start(bf16[512,2304]{1,0:T(8,128)(2,1)} %param.23) | copy-start | bytes 7077892
Sparse Core Ops, SparseCore 0:
  9.7 112.9 all-gather.1
  166.3 38.9 reduce-scatter.3

commit v5 on v4

--- a/solution.py
+++ b/solution.py
@@ -104,6 +104,18 @@
     return jnp.take(jnp.stack(pieces), order, axis=0).reshape(partial.shape)
 
 
+def ring_scatter(partial, axis):
+    count = lax.axis_size(axis)
+    me = lax.axis_index(axis)
+    width = partial.shape[1] // count
+    total = lax.dynamic_slice_in_dim(partial, me * width, width, 1).astype(jnp.float32)
+    for shift in range(1, count):
+        sent = lax.dynamic_slice_in_dim(partial, ((me + shift) % count) * width, width, 1)
+        pairs = [(j, (j + shift) % count) for j in range(count)]
+        total = total + lax.ppermute(sent, axis, pairs).astype(jnp.float32)
+    return total
+
+
 def per_device(
     queries,
     key_cache,
@@ -135,9 +147,7 @@
     partial_out = lax.dot_general(
         act, weights[2], (((1,), (1,)), ((), ())), preferred_element_type=jnp.float32
     )
-    total = lax.psum_scatter(
-        partial_out.astype(jnp.bfloat16), "mlp", scatter_dimension=1, tiled=True
-    ).astype(jnp.float32)
+    total = ring_scatter(partial_out.astype(jnp.bfloat16), "mlp")
     width = total.shape[1]
     first = lax.axis_index("mlp") * width
     square = lax.psum(jnp.sum(total * total, axis=-1, keepdims=True), "mlp")

time: 225 us -> 220 us (0.978)
  waiting for transfers between devices: 91.3 us -> 81.2 us
  local copies, waits for them, and re-layouts: 23.6 us -> 19.4 us
  starting transfers between devices: 10.3 us -> 14.3 us
  other arithmetic: 19.5 us -> 23.1 us
  blocking collectives: 6.57 us -> 9.02 us
    unnamed x3 -> x1, waiting for transfers between devices: 38.4 us -> 0.02 us
    ppermute x0 -> x3, waiting for transfers between devices: none -> 28.3 us  [ring_scatter(): total = total + lax.ppermute(sent, axis, pairs).astype(jnp.float32)]
    unnamed x25 -> x23, local copies, waits for them, and re-layouts: 6.32 us -> 0.27 us
    ppermute x0 -> x3, starting transfers between devices: none -> 3.98 us  [ring_scatter(): total = total + lax.ppermute(sent, axis, pairs).astype(jnp.float32)]
    dynamic_slice x0 -> x1, local copies, waits for them, and re-layouts: none -> 2.64 us  [ring_scatter(): lax.dynamic_slice_in_dim(partial, (me + shift) % count * width, width, 1)]
    psum x1, blocking collectives: 6.57 us -> 9.02 us  [per_device(): square = lax.psum(jnp.sum(total * total, axis=-1, keepdims=True), 'mlp')]
  transfers between devices with their start and end apart: 8 -> 10, of which waited for: 5 -> 6; matrix products, arithmetic and copies ran while one was open for 24% -> 24% of each run, Pallas kernels for 0% -> 0%
where the time goes in v5:
time: 220 us; the launch traced here: 219 us
  waiting for transfers between devices  81.2 us (37%)
  matrix products  57 us (26%)
  other arithmetic  23.1 us (10%)
  local copies, waits for them, and re-layouts  19.4 us (9%)
  between operations  14.4 us (7%)
  starting transfers between devices  14.3 us (6%)
  blocking collectives  9.02 us (4%)
    ppermute x3, waiting for transfers between devices, ring_scatter(): total = total + lax.ppermute(sent, axis, pairs).astype(jnp.float32)  28.3 us
    ppermute x3, waiting for transfers between devices, ring_sum(): pieces.append(lax.ppermute(reduced, axis, pairs))  26.8 us
    ppermute x3, waiting for transfers between devices, ring_sum(): total = total + lax.ppermute(sent, axis, pairs).astype(jnp.float32)  26.1 us
    dot_general x1, matrix products, per_device(): lax.dot_general(act, weights[2], (((1,), (1,)), ((), ())), preferred_elem...  22 us
    dot_general x1, matrix products, per_device(): gate = jnp.dot(normed, weights[0], preferred_element_type=jnp.float32)  12.7 us
    psum x1, blocking collectives, per_device(): square = lax.psum(jnp.sum(total * total, axis=-1, keepdims=True), 'mlp')  9.02 us
    reduce_sum x2, other arithmetic, rms(): jnp.mean(values * values, axis=-1, keepdims=True) + EPS  7.08 us
    dot_general x1, matrix products, attend(): jnp.einsum('rghd,tgd->rght', pre_q, pre_keys, preferred_element_type=jnp....  6.71 us
  transfers between devices with their start and end apart: 10, of which 6 were waited for; matrix products, arithmetic and copies ran while one was open for 24% of the time, Pallas kernels for 0%

profile of v5, /device:TPU:1, one launch (start us, length us, event | category | flops | bytes accessed | tf_op | source)
XLA Modules:
  0.0 218.6 jit_solution(10714796012083237218)
XLA Ops:
  6.5 2.4 %pad_maximum_fusion.1 = bf16[3,72,2304]{2,1,0:T(8,128)(2,1)} fusion(bf16[1,72,2304]{2,1,0:T(8,128)(2,1)} %bitcast.147, bf16[1,72,2304]{2,1,0:T(8,128)(2,1)} %bitcast.148, bf16[1,72,2304]{2,1,0:T(8,128)(2,1)} %bitcast.149), kind=kLoop, calls=%fused_computation.49 | loop fusion | flops 995328 | bytes 1990656 | tf_op jit(solution)/shard_map/stack | solution.py:136
  8.9 0.0 all-gather.2.cloned.1.call-update
  9.7 0.2 copy.35
  10.0 4.5 %gather_fusion.1 = bf16[32,128,256]{2,1,0:T(8,128)(2,1)} fusion(bf16[80,128,256]{2,1,0:T(8,128)(2,1)} %param.17, s32[1024]{0:T(1024)S(1)} %pad_clamp_fusion.1), kind=kCustom, calls=%fused_computation.1 | custom fusion | bytes 4194432 | tf_op jit(solution)/shard_map/gather | solution.py:39
  14.4 4.5 %gather_fusion = bf16[32,128,256]{2,1,0:T(8,128)(2,1)} fusion(bf16[80,128,256]{2,1,0:T(8,128)(2,1)} %param.18, s32[1024]{0:T(1024)S(1)} %pad_clamp_fusion.1), kind=kCustom, calls=%fused_computation | custom fusion | bytes 4194432 | tf_op jit(solution)/shard_map/gather | solution.py:40
  18.9 0.1 broadcast_compare_fusion
  19.0 0.2 select_reduce_fusion
  19.3 0.2 add.191
  19.5 0.3 fusion.35
  19.8 4.4 %fusion.48 = (f32[16,2]{0,1:T(2,128)S(1)}, bf16[16,1,2,10240]{3,0,2,1:T(8,128)(2,1)S(1)}) fusion(bf16[10240,256,1]{1,0,2:T(8,128)(2,1)} %bitcast.138, bf16[2,2,8,256]{3,2,1,0:T(8,128)(2,1)S(1)} %bitcast.137, pred[16,10240]{1,0:T(8,128)(4,1)S(1)} %fusion.35), kind=kOutput, calls=%fused_computation.93 | convolution fusion | flops 169410528 | bytes 6078592 | tf_op jit(solution)/shard_map/rghd,tgd->rght/dot_general | solution.py:71
  24.2 2.1 fusion.29
  26.4 1.7 iota_compare_fusion
  28.1 6.7 %fusion = (f32[512,2]{0,1:T(2,128)S(1)}, f32[4096,512,2]{1,0,2:T(8,128)S(1)}) fusion(pred[512,4096]{0,1:T(8,128)(4,1)S(1)} %iota_compare_fusion, bf16[4096,256,1]{1,0,2:T(8,128)(2,1)S(1)} %bitcast.136, bf16[512,2,256]{0,2,1:T(8,128)(2,1)S(1)} %bitcast.146), kind=kOutput, calls=%fused_computation.4 | convolution fusion | flops 2164259840 | bytes 21499904 | tf_op jit(solution)/shard_map/rghd,tgd->rght/dot_general | solution.py:43
  34.9 6.2 %fusion.32 = bf16[512,1,2,256]{0,3,2,1:T(8,128)(2,1)S(1)} fusion(bf16[4096,256,1]{1,0,2:T(8,128)(2,1)S(1)} %bitcast.135, f32[4096,512,2]{1,0,2:T(8,128)S(1)} %get-tuple-element.28, pred[512,4096]{0,1:T(8,128)(4,1)S(1)} %iota_compare_fusion, f32[512,2]{0,1:T(2,128)S(1)} %get-tuple-element.27), kind=kOutput, calls=%fused_computation.50 | convolution fusion | flops 2164785152 | bytes 21499904 | tf_op jit(solution)/shard_map/rght,tgd->rghd/dot_general | solution.py:49
  41.0 0.1 pad_maximum_fusion.2
  41.1 2.9 %convolution_convert_fusion = bf16[528,2304]{1,0:T(8,128)(2,1)} fusion(bf16[528,512]{0,1:T(8,128)(2,1)S(1)} %bitcast.142, bf16[512,2304]{1,0:T(8,128)(2,1)S(1)} %copy-done), kind=kOutput, calls=%fused_computation.37 | convolution fusion | flops 1246924800 | bytes 5332992 | tf_op jit(solution)/shard_map/dot_general | solution.py:140
  44.0 1.9 reshape.297
  45.9 1.3 select_bitcast_fusion.2
  47.3 2.3 %collective-permute-start = (bf16[132,2304]{1,0:T(8,128)(2,1)}, bf16[132,2304]{1,0:T(8,128)(2,1)S(1)}, u32[]{:S(2)}, u32[]{:S(2)}) collective-permute-start(bf16[132,2304]{1,0:T(8,128)(2,1)} %get-tuple-element.19), channel_id=1, source_target_pairs={{0,1},{1,2},{2,3},{3,0},{4,5},{5,6},{6,7},{7,4},{8,9},{9,10},{10,1... | collective-permute-start | bytes 1824776 | tf_op jit(solution)/shard_map/ppermute | solution.py:97
  49.6 2.7 %collective-permute-start.1 = (bf16[132,2304]{1,0:T(8,128)(2,1)}, bf16[132,2304]{1,0:T(8,128)(2,1)}, u32[]{:S(2)}, u32[]{:S(2)}) collective-permute-start(bf16[132,2304]{1,0:T(8,128)(2,1)} %get-tuple-element.21), channel_id=1, source_target_pairs={{0,2},{1,3},{2,0},{3,1},{4,6},{5,7},{6,4},{7,5},{8,10},{9,11},{10,... | collective-permute-start | bytes 1824776 | tf_op jit(solution)/shard_map/ppermute | solution.py:97
  52.3 1.1 collective-permute-start.2
  53.3 11.7 %collective-permute-done = bf16[132,2304]{1,0:T(8,128)(2,1)S(1)} collective-permute-done((bf16[132,2304]{1,0:T(8,128)(2,1)}, bf16[132,2304]{1,0:T(8,128)(2,1)S(1)}, u32[]{:S(2)}, u32[]{:S(2)}) %collective-permute-start) | collective-permute-done | bytes 608288 | tf_op jit(solution)/shard_map/ppermute | solution.py:97
  65.1 14.3 %collective-permute-done.1 = bf16[132,2304]{1,0:T(8,128)(2,1)} collective-permute-done((bf16[132,2304]{1,0:T(8,128)(2,1)}, bf16[132,2304]{1,0:T(8,128)(2,1)}, u32[]{:S(2)}, u32[]{:S(2)}) %collective-permute-start.1) | collective-permute-done | bytes 608288 | tf_op jit(solution)/shard_map/ppermute | solution.py:97
  79.4 1.8 add_convert_fusion.1
  81.2 1.4 collective-permute-start.3
  82.6 2.9 %collective-permute-start.4 = (bf16[132,2304]{1,0:T(8,128)(2,1)S(1)}, bf16[132,2304]{1,0:T(8,128)(2,1)S(1)}, u32[]{:S(2)}, u32[]{:S(2)}) collective-permute-start(bf16[132,2304]{1,0:T(8,128)(2,1)S(1)} %add_convert_fusion.1), channel_id=1, source_target_pairs={{0,2},{1,3},{2,0},{3,1},{4,6},{5,7},{6,4},{7,5},{8,10},{9,11},{10,... | collective-permute-start | bytes 1824776 | tf_op jit(solution)/shard_map/ppermute | solution.py:102
  85.5 0.1 collective-permute-start.5
  85.5 0.1 broadcast_in_dim.87
  85.6 0.1 broadcast_in_dim.88
  85.7 11.5 %collective-permute-done.3 = bf16[132,2304]{1,0:T(8,128)(2,1)S(1)} collective-permute-done((bf16[132,2304]{1,0:T(8,128)(2,1)S(1)}, bf16[132,2304]{1,0:T(8,128)(2,1)S(1)}, u32[]{:S(2)}, u32[]{:S(2)}) %collective-permute-start.3) | collective-permute-done | bytes 608288 | tf_op jit(solution)/shard_map/ppermute | solution.py:102
  97.3 15.3 %collective-permute-done.4 = bf16[132,2304]{1,0:T(8,128)(2,1)S(1)} collective-permute-done((bf16[132,2304]{1,0:T(8,128)(2,1)S(1)}, bf16[132,2304]{1,0:T(8,128)(2,1)S(1)}, u32[]{:S(2)}, u32[]{:S(2)}) %collective-permute-start.4) | collective-permute-done | bytes 608288 | tf_op jit(solution)/shard_map/ppermute | solution.py:102
  112.6 1.7 pad_maximum_fusion
  114.3 2.7 %gather_fusion.2 = bf16[4,132,2304]{2,1,0:T(8,128)(2,1)S(1)} fusion(bf16[4,132,2304]{2,1,0:T(8,128)(2,1)} %pad_maximum_fusion, s32[1024]{0:T(1024)S(1)} %pad_clamp_fusion), kind=kCustom, calls=%fused_computation.2 | custom fusion | bytes 4866064 | tf_op jit(solution)/shard_map/jit(_take)/gather | solution.py:104
  117.1 1.7 gather.18
  118.7 0.8 multiply_reduce_fusion
  119.6 0.1 rsqrt.23
  119.7 6.3 %multiply_reduce_fusion.1 = (f32[528]{0:T(1024)S(1)}, f32[528,2304]{1,0:T(8,128)}) fusion(f32[2304]{0:T(1024)S(1)} %copy-done.5, f32[528]{0:T(1024)S(1)} %rsqrt.23, bf16[528,2304]{1,0:T(8,128)(2,1)} %gather.18, pred[528]{0:T(1024)(128)(4,1)S(1)} %broadcast_in_dim.88, bf16[528,2304]{1,0:T(8,128)(2,1)} %param.22), kind=kLoop, calls=%fused_computation.33 | loop fusion | flops 9731568 | bytes 9746064 | tf_op jit(solution)/shard_map/reduce_sum | solution.py:19
  126.0 12.7 %fusion.21 = f32[528,2304]{1,0:T(8,128)} fusion(bf16[3,2304,2304]{2,1,0:T(8,128)(2,1)} %all-gather.2.cloned.1.call-done, f32[528,2304]{1,0:T(8,128)} %get-tuple-element.18, f32[2304]{0:T(1024)S(1)} %copy-done.8, f32[528]{0:T(1024)S(1)} %add_rsqrt_fusion), kind=kOutput, calls=%fused_computation.31 | convolution fusion | flops 5619068928 | bytes 20360256 | tf_op jit(solution)/shard_map/dot_general | solution.py:144
  138.6 22.0 %fusion.23 = bf16[528,2304]{1,0:T(8,128)(2,1)} fusion(bf16[3,2304,2304]{2,1,0:T(8,128)(2,1)} %all-gather.2.cloned.1.call-done, f32[528,2304]{1,0:T(8,128)} %fusion.21, f32[528,2304]{1,0:T(8,128)} %get-tuple-element.18, f32[2304]{0:T(1024)S(1)} %copy-done.8, f32[528]{0:T(1024)S(1)} %add_rsqrt_fusion), kind=kOutput, calls=%fused_computation.36 | convolution fusion | flops 11218673664 | bytes 33410112 | tf_op jit(solution)/shard_map/dot_general | solution.py:147
  160.7 2.6 %constant_dynamic-slice_fusion.2 = (bf16[528,576]{1,0:T(8,128)(2,1)S(1)}, bf16[528,576]{1,0:T(8,128)(2,1)S(1)}, bf16[528,576]{1,0:T(8,128)(2,1)S(1)}) fusion(bf16[528,2304]{1,0:T(8,128)(2,1)} %fusion.23, s32[]{:T(128)S(6)} %select_n.119, s32[]{:T(128)S(6)} %select_n.121, s32[]{:T(128)S(6)} %select_n.120), kind=kLoop, calls=%fused_computation.76 | loop fusion | bytes 3649548 | tf_op jit(solution)/shard_map/dynamic_slice | solution.py:113
  163.3 1.5 collective-permute-start.6
  164.8 2.5 %collective-permute-start.7 = (bf16[528,576]{1,0:T(8,128)(2,1)S(1)}, bf16[528,576]{1,0:T(8,128)(2,1)}, u32[]{:S(2)}, u32[]{:S(2)}) collective-permute-start(bf16[528,576]{1,0:T(8,128)(2,1)S(1)} %get-tuple-element.24), channel_id=1, source_target_pairs={{0,2},{1,3},{2,0},{3,1},{4,6},{5,7},{6,4},{7,5},{8,10},{9,11},{10,... | collective-permute-start | bytes 1824776 | tf_op jit(solution)/shard_map/ppermute | solution.py:115
  167.3 0.8 dynamic_slice.23
  168.1 12.5 %collective-permute-done.6 = bf16[528,576]{1,0:T(8,128)(2,1)S(1)} collective-permute-done((bf16[528,576]{1,0:T(8,128)(2,1)S(1)}, bf16[528,576]{1,0:T(8,128)(2,1)S(1)}, u32[]{:S(2)}, u32[]{:S(2)}) %collective-permute-start.6) | collective-permute-done | bytes 608288 | tf_op jit(solution)/shard_map/ppermute | solution.py:115
  180.5 15.8 %collective-permute-done.7 = bf16[528,576]{1,0:T(8,128)(2,1)} collective-permute-done((bf16[528,576]{1,0:T(8,128)(2,1)S(1)}, bf16[528,576]{1,0:T(8,128)(2,1)}, u32[]{:S(2)}, u32[]{:S(2)}) %collective-permute-start.7) | collective-permute-done | bytes 608288 | tf_op jit(solution)/shard_map/ppermute | solution.py:115
  196.4 2.4 %multiply_reduce_fusion.2 = f32[528]{0:T(1024)S(1)} fusion(bf16[528,576]{1,0:T(8,128)(2,1)} %collective-permute-done.8, bf16[528,576]{1,0:T(8,128)(2,1)} %collective-permute-done.7, bf16[528,576]{1,0:T(8,128)(2,1)S(1)} %collective-permute-done.6, bf16[528,2304]{1,0:T(8,128)(2,1)} %fusion.23, s32[]{:T(128)S(6)} %select_n.118), kind=kLoop, calls=%fused_computation.41 | loop fusion | flops 2736624 | bytes 2435140 | tf_op jit(solution)/shard_map/reduce_sum | solution.py:153
  198.7 9.0 %psum.7 = f32[528,1]{0,1:T(1,128)S(1)} all-reduce(f32[528,1]{0,1:T(1,128)S(1)} %broadcast_in_dim.99), channel_id=1, replica_groups=mesh['req'=32,'mlp'=4] {'mlp'}, use_global_device_ids=true, to_apply=%region_6.8 | all-reduce | flops 528 | bytes 4224 | tf_op jit(solution)/shard_map/psum | solution.py:153
  207.8 3.9 %add_convert_fusion = bf16[528,576]{1,0:T(8,128)(2,1)} fusion(f32[528,2304]{1,0:T(8,128)} %get-tuple-element.18, s32[]{:T(128)S(6)} %select_n.118, f32[576]{0:T(1024)S(1)} %dynamic_slice.23, f32[528]{0:T(1024)S(1)} %rsqrt_reduce_fusion, bf16[528,576]{1,0:T(8,128)(2,1)} %collective-permute-done.8, bf16[528,576]{1,0:T(8,128)(2,1)} %collective-permute-done.7, ...), kind=kLoop, calls=%fused_computation.40 | loop fusion | flops 3345408 | bytes 4262212 | tf_op jit(solution)/shard_map/convert_element_type | solution.py:157
  (46 shorter events, 0.2 us)
Async XLA Ops:
  6.5 34.6 %copy-start = (bf16[512,2304]{1,0:T(8,128)(2,1)S(1)}, bf16[512,2304]{1,0:T(8,128)(2,1)}, u32[]{:S(2)}) copy-start(bf16[512,2304]{1,0:T(8,128)(2,1)} %param.23) | copy-start | bytes 7077892
  6.5 3.1 %slice-start = ((bf16[528,512]{1,0:T(8,128)(2,1)}), bf16[512,512]{1,0:T(8,128)(2,1)S(1)}, s32[]{:S(2)}) async-start(bf16[528,512]{1,0:T(8,128)(2,1)} %param.16), calls=%async_computation.1 | async-start | bytes 1048576 | tf_op jit(solution)/shard_map/slice | solution.py:35
  6.5 119.4 %all-gather.2.cloned.1.call-start = ((), (), s32[]{:S(2)}) async-start(), calls=%async_computation | async-start | bytes 32845824 | tf_op jit(solution)/shard_map/all_gather | solution.py:135
  6.5 3.4 %copy-start.6 = (s32[17,32]{1,0:T(8,128)S(1)}, s32[17,32]{1,0:T(8,128)}, u32[]{:S(2)}) copy-start(s32[17,32]{1,0:T(8,128)} %param.21) | copy-start | bytes 6532
  14.4 4.5 %copy-start.7 = (s32[16]{0:T(128)S(1)}, s32[16]{0:T(128)}, u32[]{:S(2)}) copy-start(s32[16]{0:T(128)} %param.19) | copy-start | bytes 196
  14.4 5.3 %slice-start.1 = ((bf16[528,512]{1,0:T(8,128)(2,1)}), bf16[16,512]{1,0:T(8,128)(2,1)S(1)}, s32[]{:S(2)}) async-start(bf16[528,512]{1,0:T(8,128)(2,1)} %param.16), calls=%async_computation.2 | async-start | bytes 32768 | tf_op jit(solution)/shard_map/slice | solution.py:36
  19.5 4.7 %slice-start.2 = ((s8[5242880]{0:T(1024)(128)(4,1)}), s8[4194304]{0:T(1024)(128)(4,1)S(1)}, s32[]{:S(2)}) async-start(s8[5242880]{0:T(1024)(128)(4,1)} %bitcast.139), calls=%async_computation.3 | async-start | bytes 8388608
  19.8 4.5 %slice-start.3 = ((s8[5242880]{0:T(1024)(128)(4,1)}), s8[1048576]{0:T(1024)(128)(4,1)S(1)}, s32[]{:S(2)}) async-start(s8[5242880]{0:T(1024)(128)(4,1)} %bitcast.139), calls=%async_computation.4 | async-start | bytes 2097152
  24.2 3.9 %copy-start.3 = (bf16[32,128,256]{2,1,0:T(8,128)(2,1)S(1)}, bf16[32,128,256]{2,1,0:T(8,128)(2,1)}, u32[]{:S(2)}) copy-start(bf16[32,128,256]{2,1,0:T(8,128)(2,1)} %gather_fusion.1) | copy-start | bytes 6291460
  28.1 6.7 %copy-start.2 = (bf16[32,128,256]{2,1,0:T(8,128)(2,1)S(1)}, bf16[32,128,256]{2,1,0:T(8,128)(2,1)}, u32[]{:S(2)}) copy-start(bf16[32,128,256]{2,1,0:T(8,128)(2,1)} %gather_fusion) | copy-start | bytes 6291460
  47.3 17.8 %collective-permute-start = (bf16[132,2304]{1,0:T(8,128)(2,1)}, bf16[132,2304]{1,0:T(8,128)(2,1)S(1)}, u32[]{:S(2)}, u32[]{:S(2)}) collective-permute-start(bf16[132,2304]{1,0:T(8,128)(2,1)} %get-tuple-element.19), channel_id=1, source_target_pairs={{0,1},{1,2},{2,3},{3,0},{4,5},{5,6},{6,7},{7,4},{8,9},{9,10},{10,1... | collective-permute-start | bytes 1824776 | tf_op jit(solution)/shard_map/ppermute | solution.py:97
  49.6 29.8 %collective-permute-start.1 = (bf16[132,2304]{1,0:T(8,128)(2,1)}, bf16[132,2304]{1,0:T(8,128)(2,1)}, u32[]{:S(2)}, u32[]{:S(2)}) collective-permute-start(bf16[132,2304]{1,0:T(8,128)(2,1)} %get-tuple-element.21), channel_id=1, source_target_pairs={{0,2},{1,3},{2,0},{3,1},{4,6},{5,7},{6,4},{7,5},{8,10},{9,11},{10,... | collective-permute-start | bytes 1824776 | tf_op jit(solution)/shard_map/ppermute | solution.py:97
  52.3 27.1 %collective-permute-start.2 = (bf16[132,2304]{1,0:T(8,128)(2,1)}, bf16[132,2304]{1,0:T(8,128)(2,1)}, u32[]{:S(2)}, u32[]{:S(2)}) collective-permute-start(bf16[132,2304]{1,0:T(8,128)(2,1)} %get-tuple-element.20), channel_id=1, source_target_pairs={{0,3},{1,0},{2,1},{3,2},{4,7},{5,4},{6,5},{7,6},{8,11},{9,8},{10,9... | collective-permute-start | bytes 1824776 | tf_op jit(solution)/shard_map/ppermute | solution.py:97
  65.1 14.3 %copy-start.4 = (bf16[132,2304]{1,0:T(8,128)(2,1)}, bf16[132,2304]{1,0:T(8,128)(2,1)S(1)}, u32[]{:S(2)}) copy-start(bf16[132,2304]{1,0:T(8,128)(2,1)S(1)} %collective-permute-done) | copy-start | bytes 1824772
  81.2 16.0 %collective-permute-start.3 = (bf16[132,2304]{1,0:T(8,128)(2,1)S(1)}, bf16[132,2304]{1,0:T(8,128)(2,1)S(1)}, u32[]{:S(2)}, u32[]{:S(2)}) collective-permute-start(bf16[132,2304]{1,0:T(8,128)(2,1)S(1)} %add_convert_fusion.1), channel_id=1, source_target_pairs={{0,1},{1,2},{2,3},{3,0},{4,5},{5,6},{6,7},{7,4},{8,9},{9,10},{10,1... | collective-permute-start | bytes 1824776 | tf_op jit(solution)/shard_map/ppermute | solution.py:102
  82.6 29.9 %collective-permute-start.4 = (bf16[132,2304]{1,0:T(8,128)(2,1)S(1)}, bf16[132,2304]{1,0:T(8,128)(2,1)S(1)}, u32[]{:S(2)}, u32[]{:S(2)}) collective-permute-start(bf16[132,2304]{1,0:T(8,128)(2,1)S(1)} %add_convert_fusion.1), channel_id=1, source_target_pairs={{0,2},{1,3},{2,0},{3,1},{4,6},{5,7},{6,4},{7,5},{8,10},{9,11},{10,... | collective-permute-start | bytes 1824776 | tf_op jit(solution)/shard_map/ppermute | solution.py:102
  85.5 27.1 %collective-permute-start.5 = (bf16[132,2304]{1,0:T(8,128)(2,1)S(1)}, bf16[132,2304]{1,0:T(8,128)(2,1)S(1)}, u32[]{:S(2)}, u32[]{:S(2)}) collective-permute-start(bf16[132,2304]{1,0:T(8,128)(2,1)S(1)} %add_convert_fusion.1), channel_id=1, source_target_pairs={{0,3},{1,0},{2,1},{3,2},{4,7},{5,4},{6,5},{7,6},{8,11},{9,8},{10,9... | collective-permute-start | bytes 1824776 | tf_op jit(solution)/shard_map/ppermute | solution.py:102
  117.1 2.6 %copy-start.5 = (f32[2304]{0:T(1024)S(1)}, f32[2304]{0:T(1024)}, u32[]{:S(2)}) copy-start(f32[2304]{0:T(1024)} %param.24) | copy-start | bytes 27652
  119.7 6.3 %copy-start.8 = (f32[2304]{0:T(1024)S(1)}, f32[2304]{0:T(1024)}, u32[]{:S(2)}) copy-start(f32[2304]{0:T(1024)} %param.25) | copy-start | bytes 27652
  163.3 17.2 %collective-permute-start.6 = (bf16[528,576]{1,0:T(8,128)(2,1)S(1)}, bf16[528,576]{1,0:T(8,128)(2,1)S(1)}, u32[]{:S(2)}, u32[]{:S(2)}) collective-permute-start(bf16[528,576]{1,0:T(8,128)(2,1)S(1)} %get-tuple-element.22), channel_id=1, source_target_pairs={{0,1},{1,2},{2,3},{3,0},{4,5},{5,6},{6,7},{7,4},{8,9},{9,10},{10,1... | collective-permute-start | bytes 1824776 | tf_op jit(solution)/shard_map/ppermute | solution.py:115
  164.8 31.6 %collective-permute-start.7 = (bf16[528,576]{1,0:T(8,128)(2,1)S(1)}, bf16[528,576]{1,0:T(8,128)(2,1)}, u32[]{:S(2)}, u32[]{:S(2)}) collective-permute-start(bf16[528,576]{1,0:T(8,128)(2,1)S(1)} %get-tuple-element.24), channel_id=1, source_target_pairs={{0,2},{1,3},{2,0},{3,1},{4,6},{5,7},{6,4},{7,5},{8,10},{9,11},{10,... | collective-permute-start | bytes 1824776 | tf_op jit(solution)/shard_map/ppermute | solution.py:115
  167.3 29.1 %collective-permute-start.8 = (bf16[528,576]{1,0:T(8,128)(2,1)S(1)}, bf16[528,576]{1,0:T(8,128)(2,1)}, u32[]{:S(2)}, u32[]{:S(2)}) collective-permute-start(bf16[528,576]{1,0:T(8,128)(2,1)S(1)} %get-tuple-element.23), channel_id=1, source_target_pairs={{0,3},{1,0},{2,1},{3,2},{4,7},{5,4},{6,5},{7,6},{8,11},{9,8},{10,9... | collective-permute-start | bytes 1824776 | tf_op jit(solution)/shard_map/ppermute | solution.py:115
  196.4 15.3 %copy-start.1 = (bf16[512,2304]{1,0:T(8,128)(2,1)S(1)}, bf16[512,2304]{1,0:T(8,128)(2,1)}, u32[]{:S(2)}) copy-start(bf16[512,2304]{1,0:T(8,128)(2,1)} %param.23) | copy-start | bytes 7077892
Sparse Core Ops, SparseCore 0:
  9.7 112.9 all-gather.1

commit v6 on v5

--- a/solution.py
+++ b/solution.py
@@ -116,6 +116,15 @@
     return total
 
 
+def ring_total(value, axis):
+    count = lax.axis_size(axis)
+    total = value
+    for shift in range(1, count):
+        pairs = [(j, (j + shift) % count) for j in range(count)]
+        total = total + lax.ppermute(value, axis, pairs)
+    return total
+
+
 def per_device(
     queries,
     key_cache,
@@ -150,7 +159,7 @@
     total = ring_scatter(partial_out.astype(jnp.bfloat16), "mlp")
     width = total.shape[1]
     first = lax.axis_index("mlp") * width
-    square = lax.psum(jnp.sum(total * total, axis=-1, keepdims=True), "mlp")
+    square = ring_total(jnp.sum(total * total, axis=-1), "mlp")[:, None]
     scale = lax.rsqrt(square / hidden_in.shape[1] + EPS)
     gain = lax.dynamic_slice_in_dim(ffn_out_gain, first, width, 0)
     kept = lax.dynamic_slice_in_dim(resid, first, width, 1)

time: 220 us -> 219 us (level)
  blocking collectives: 9.02 us -> 0 us
  starting transfers between devices: 14.3 us -> 18.5 us
  waiting for transfers between devices: 81.2 us -> 84.9 us
    psum x1 -> x0, blocking collectives: 9.02 us -> none  [per_device(): square = lax.psum(jnp.sum(total * total, axis=-1, keepdims=True), 'mlp')]
    ppermute x0 -> x3, starting transfers between devices: none -> 4.24 us  [ring_total(): total = total + lax.ppermute(value, axis, pairs)]
    ppermute x0 -> x3, waiting for transfers between devices: none -> 2.89 us  [ring_total(): total = total + lax.ppermute(value, axis, pairs)]
  transfers between devices with their start and end apart: 10 -> 13, of which waited for: 6 -> 7; matrix products, arithmetic and copies ran while one was open for 24% -> 25% of each run, Pallas kernels for 0% -> 0%
where the time goes in v6:
time: 219 us; the launch traced here: 217 us
  waiting for transfers between devices  84.9 us (39%)
  matrix products  57.1 us (26%)
  other arithmetic  23 us (11%)
  local copies, waits for them, and re-layouts  19.5 us (9%)
  starting transfers between devices  18.5 us (8%)
  between operations  14.4 us (7%)
    ppermute x3, waiting for transfers between devices, ring_scatter(): total = total + lax.ppermute(sent, axis, pairs).astype(jnp.float32)  29 us
    ppermute x3, waiting for transfers between devices, ring_sum(): pieces.append(lax.ppermute(reduced, axis, pairs))  26.9 us
    ppermute x3, waiting for transfers between devices, ring_sum(): total = total + lax.ppermute(sent, axis, pairs).astype(jnp.float32)  26.1 us
    dot_general x1, matrix products, per_device(): lax.dot_general(act, weights[2], (((1,), (1,)), ((), ())), preferred_elem...  22.1 us
    dot_general x1, matrix products, per_device(): gate = jnp.dot(normed, weights[0], preferred_element_type=jnp.float32)  12.6 us
    reduce_sum x2, other arithmetic, rms(): jnp.mean(values * values, axis=-1, keepdims=True) + EPS  7.04 us
    dot_general x1, matrix products, attend(): jnp.einsum('rghd,tgd->rght', pre_q, pre_keys, preferred_element_type=jnp....  6.71 us
    dot_general x1, matrix products, attend(): jnp.einsum('rght,tgd->rghd', pre_weight.astype(jnp.bfloat16), pre_vals, p...  6.16 us
  transfers between devices with their start and end apart: 13, of which 7 were waited for; matrix products, arithmetic and copies ran while one was open for 25% of the time, Pallas kernels for 0%

profile of v6, /device:TPU:1, one launch (start us, length us, event | category | flops | bytes accessed | tf_op | source)
XLA Modules:
  0.0 217.3 jit_solution(16446759053537097979)
XLA Ops:
  6.5 2.4 %pad_maximum_fusion.1 = bf16[3,72,2304]{2,1,0:T(8,128)(2,1)} fusion(bf16[1,72,2304]{2,1,0:T(8,128)(2,1)} %bitcast.147, bf16[1,72,2304]{2,1,0:T(8,128)(2,1)} %bitcast.148, bf16[1,72,2304]{2,1,0:T(8,128)(2,1)} %bitcast.149), kind=kLoop, calls=%fused_computation.49 | loop fusion | flops 995328 | bytes 1990656 | tf_op jit(solution)/shard_map/stack | solution.py:145
  9.7 0.2 copy.35
  10.0 4.5 %gather_fusion.1 = bf16[32,128,256]{2,1,0:T(8,128)(2,1)} fusion(bf16[80,128,256]{2,1,0:T(8,128)(2,1)} %param.17, s32[1024]{0:T(1024)S(1)} %pad_clamp_fusion.1), kind=kCustom, calls=%fused_computation.1 | custom fusion | bytes 4194432 | tf_op jit(solution)/shard_map/gather | solution.py:39
  14.5 4.5 %gather_fusion = bf16[32,128,256]{2,1,0:T(8,128)(2,1)} fusion(bf16[80,128,256]{2,1,0:T(8,128)(2,1)} %param.18, s32[1024]{0:T(1024)S(1)} %pad_clamp_fusion.1), kind=kCustom, calls=%fused_computation | custom fusion | bytes 4194432 | tf_op jit(solution)/shard_map/gather | solution.py:40
  19.0 0.1 broadcast_compare_fusion
  19.1 0.2 select_reduce_fusion
  19.3 0.2 add.199
  19.6 0.3 fusion.35
  19.9 4.5 %fusion.48 = (f32[16,2]{0,1:T(2,128)S(1)}, bf16[16,1,2,10240]{3,0,2,1:T(8,128)(2,1)S(1)}) fusion(bf16[10240,256,1]{1,0,2:T(8,128)(2,1)} %bitcast.138, bf16[2,2,8,256]{3,2,1,0:T(8,128)(2,1)S(1)} %bitcast.137, pred[16,10240]{1,0:T(8,128)(4,1)S(1)} %fusion.35), kind=kOutput, calls=%fused_computation.93 | convolution fusion | flops 169410528 | bytes 6078592 | tf_op jit(solution)/shard_map/rghd,tgd->rght/dot_general | solution.py:71
  24.3 2.1 fusion.29
  26.5 1.7 iota_compare_fusion
  28.2 6.7 %fusion = (f32[512,2]{0,1:T(2,128)S(1)}, f32[4096,512,2]{1,0,2:T(8,128)S(1)}) fusion(pred[512,4096]{0,1:T(8,128)(4,1)S(1)} %iota_compare_fusion, bf16[4096,256,1]{1,0,2:T(8,128)(2,1)S(1)} %bitcast.136, bf16[512,2,256]{0,2,1:T(8,128)(2,1)S(1)} %bitcast.146), kind=kOutput, calls=%fused_computation.4 | convolution fusion | flops 2164259840 | bytes 21499904 | tf_op jit(solution)/shard_map/rghd,tgd->rght/dot_general | solution.py:43
  35.0 6.2 %fusion.32 = bf16[512,1,2,256]{0,3,2,1:T(8,128)(2,1)S(1)} fusion(bf16[4096,256,1]{1,0,2:T(8,128)(2,1)S(1)} %bitcast.135, f32[4096,512,2]{1,0,2:T(8,128)S(1)} %get-tuple-element.28, pred[512,4096]{0,1:T(8,128)(4,1)S(1)} %iota_compare_fusion, f32[512,2]{0,1:T(2,128)S(1)} %get-tuple-element.27), kind=kOutput, calls=%fused_computation.50 | convolution fusion | flops 2164785152 | bytes 21499904 | tf_op jit(solution)/shard_map/rght,tgd->rghd/dot_general | solution.py:49
  41.1 0.1 pad_maximum_fusion.2
  41.2 2.9 %convolution_convert_fusion = bf16[528,2304]{1,0:T(8,128)(2,1)} fusion(bf16[528,512]{0,1:T(8,128)(2,1)S(1)} %bitcast.142, bf16[512,2304]{1,0:T(8,128)(2,1)S(1)} %copy-done), kind=kOutput, calls=%fused_computation.37 | convolution fusion | flops 1246924800 | bytes 5332992 | tf_op jit(solution)/shard_map/dot_general | solution.py:149
  44.1 1.9 reshape.301
  46.0 1.3 select_bitcast_fusion.2
  47.3 2.4 %collective-permute-start = (bf16[132,2304]{1,0:T(8,128)(2,1)}, bf16[132,2304]{1,0:T(8,128)(2,1)S(1)}, u32[]{:S(2)}, u32[]{:S(2)}) collective-permute-start(bf16[132,2304]{1,0:T(8,128)(2,1)} %get-tuple-element.19), channel_id=1, source_target_pairs={{0,1},{1,2},{2,3},{3,0},{4,5},{5,6},{6,7},{7,4},{8,9},{9,10},{10,1... | collective-permute-start | bytes 1824776 | tf_op jit(solution)/shard_map/ppermute | solution.py:97
  49.7 2.7 %collective-permute-start.1 = (bf16[132,2304]{1,0:T(8,128)(2,1)}, bf16[132,2304]{1,0:T(8,128)(2,1)}, u32[]{:S(2)}, u32[]{:S(2)}) collective-permute-start(bf16[132,2304]{1,0:T(8,128)(2,1)} %get-tuple-element.21), channel_id=1, source_target_pairs={{0,2},{1,3},{2,0},{3,1},{4,6},{5,7},{6,4},{7,5},{8,10},{9,11},{10,... | collective-permute-start | bytes 1824776 | tf_op jit(solution)/shard_map/ppermute | solution.py:97
  52.4 1.0 collective-permute-start.2
  53.4 11.8 %collective-permute-done = bf16[132,2304]{1,0:T(8,128)(2,1)S(1)} collective-permute-done((bf16[132,2304]{1,0:T(8,128)(2,1)}, bf16[132,2304]{1,0:T(8,128)(2,1)S(1)}, u32[]{:S(2)}, u32[]{:S(2)}) %collective-permute-start) | collective-permute-done | bytes 608288 | tf_op jit(solution)/shard_map/ppermute | solution.py:97
  65.2 14.3 %collective-permute-done.1 = bf16[132,2304]{1,0:T(8,128)(2,1)} collective-permute-done((bf16[132,2304]{1,0:T(8,128)(2,1)}, bf16[132,2304]{1,0:T(8,128)(2,1)}, u32[]{:S(2)}, u32[]{:S(2)}) %collective-permute-start.1) | collective-permute-done | bytes 608288 | tf_op jit(solution)/shard_map/ppermute | solution.py:97
  79.5 1.8 add_convert_fusion.1
  81.3 1.4 collective-permute-start.3
  82.7 2.8 %collective-permute-start.4 = (bf16[132,2304]{1,0:T(8,128)(2,1)S(1)}, bf16[132,2304]{1,0:T(8,128)(2,1)S(1)}, u32[]{:S(2)}, u32[]{:S(2)}) collective-permute-start(bf16[132,2304]{1,0:T(8,128)(2,1)S(1)} %add_convert_fusion.1), channel_id=1, source_target_pairs={{0,2},{1,3},{2,0},{3,1},{4,6},{5,7},{6,4},{7,5},{8,10},{9,11},{10,... | collective-permute-start | bytes 1824776 | tf_op jit(solution)/shard_map/ppermute | solution.py:102
  85.6 0.1 broadcast_in_dim.85
  85.7 0.1 broadcast_in_dim.86
  85.8 11.6 %collective-permute-done.3 = bf16[132,2304]{1,0:T(8,128)(2,1)S(1)} collective-permute-done((bf16[132,2304]{1,0:T(8,128)(2,1)S(1)}, bf16[132,2304]{1,0:T(8,128)(2,1)S(1)}, u32[]{:S(2)}, u32[]{:S(2)}) %collective-permute-start.3) | collective-permute-done | bytes 608288 | tf_op jit(solution)/shard_map/ppermute | solution.py:102
  97.4 15.3 %collective-permute-done.4 = bf16[132,2304]{1,0:T(8,128)(2,1)S(1)} collective-permute-done((bf16[132,2304]{1,0:T(8,128)(2,1)S(1)}, bf16[132,2304]{1,0:T(8,128)(2,1)S(1)}, u32[]{:S(2)}, u32[]{:S(2)}) %collective-permute-start.4) | collective-permute-done | bytes 608288 | tf_op jit(solution)/shard_map/ppermute | solution.py:102
  112.7 1.7 pad_maximum_fusion
  114.4 2.7 %gather_fusion.2 = bf16[4,132,2304]{2,1,0:T(8,128)(2,1)S(1)} fusion(bf16[4,132,2304]{2,1,0:T(8,128)(2,1)} %pad_maximum_fusion, s32[1024]{0:T(1024)S(1)} %pad_clamp_fusion), kind=kCustom, calls=%fused_computation.2 | custom fusion | bytes 4866064 | tf_op jit(solution)/shard_map/jit(_take)/gather | solution.py:104
  117.2 1.7 gather.18
  118.8 0.8 multiply_reduce_fusion
  119.7 0.1 rsqrt.24
  119.8 6.2 %multiply_reduce_fusion.1 = (f32[528]{0:T(1024)S(1)}, f32[528,2304]{1,0:T(8,128)}) fusion(f32[2304]{0:T(1024)S(1)} %copy-done.5, f32[528]{0:T(1024)S(1)} %rsqrt.24, bf16[528,2304]{1,0:T(8,128)(2,1)} %gather.18, pred[528]{0:T(1024)(128)(4,1)S(1)} %broadcast_in_dim.86, bf16[528,2304]{1,0:T(8,128)(2,1)} %param.22), kind=kLoop, calls=%fused_computation.33 | loop fusion | flops 9731568 | bytes 9746064 | tf_op jit(solution)/shard_map/reduce_sum | solution.py:19
  126.0 12.6 %fusion.21 = f32[528,2304]{1,0:T(8,128)} fusion(bf16[3,2304,2304]{2,1,0:T(8,128)(2,1)} %all-gather.2.cloned.1.call-done, f32[528,2304]{1,0:T(8,128)} %get-tuple-element.18, f32[2304]{0:T(1024)S(1)} %copy-done.8, f32[528]{0:T(1024)S(1)} %add_rsqrt_fusion.1), kind=kOutput, calls=%fused_computation.31 | convolution fusion | flops 5619068928 | bytes 20360256 | tf_op jit(solution)/shard_map/dot_general | solution.py:153
  138.6 22.1 %fusion.23 = bf16[528,2304]{1,0:T(8,128)(2,1)} fusion(bf16[3,2304,2304]{2,1,0:T(8,128)(2,1)} %all-gather.2.cloned.1.call-done, f32[528,2304]{1,0:T(8,128)} %fusion.21, f32[528,2304]{1,0:T(8,128)} %get-tuple-element.18, f32[2304]{0:T(1024)S(1)} %copy-done.8, f32[528]{0:T(1024)S(1)} %add_rsqrt_fusion.1), kind=kOutput, calls=%fused_computation.36 | convolution fusion | flops 11218673664 | bytes 33410112 | tf_op jit(solution)/shard_map/dot_general | solution.py:156
  160.7 2.7 %constant_dynamic-slice_fusion.2 = (bf16[528,576]{1,0:T(8,128)(2,1)S(1)}, bf16[528,576]{1,0:T(8,128)(2,1)S(1)}, bf16[528,576]{1,0:T(8,128)(2,1)S(1)}) fusion(bf16[528,2304]{1,0:T(8,128)(2,1)} %fusion.23, s32[]{:T(128)S(6)} %select_n.119, s32[]{:T(128)S(6)} %select_n.121, s32[]{:T(128)S(6)} %select_n.120), kind=kLoop, calls=%fused_computation.76 | loop fusion | bytes 3649548 | tf_op jit(solution)/shard_map/dynamic_slice | solution.py:113
  163.4 1.4 collective-permute-start.6
  164.8 2.5 %collective-permute-start.7 = (bf16[528,576]{1,0:T(8,128)(2,1)S(1)}, bf16[528,576]{1,0:T(8,128)(2,1)}, u32[]{:S(2)}, u32[]{:S(2)}) collective-permute-start(bf16[528,576]{1,0:T(8,128)(2,1)S(1)} %get-tuple-element.24), channel_id=1, source_target_pairs={{0,2},{1,3},{2,0},{3,1},{4,6},{5,7},{6,4},{7,5},{8,10},{9,11},{10,... | collective-permute-start | bytes 1824776 | tf_op jit(solution)/shard_map/ppermute | solution.py:115
  167.3 13.4 %collective-permute-done.6 = bf16[528,576]{1,0:T(8,128)(2,1)S(1)} collective-permute-done((bf16[528,576]{1,0:T(8,128)(2,1)S(1)}, bf16[528,576]{1,0:T(8,128)(2,1)S(1)}, u32[]{:S(2)}, u32[]{:S(2)}) %collective-permute-start.6) | collective-permute-done | bytes 608288 | tf_op jit(solution)/shard_map/ppermute | solution.py:115
  180.7 15.6 %collective-permute-done.7 = bf16[528,576]{1,0:T(8,128)(2,1)} collective-permute-done((bf16[528,576]{1,0:T(8,128)(2,1)S(1)}, bf16[528,576]{1,0:T(8,128)(2,1)}, u32[]{:S(2)}, u32[]{:S(2)}) %collective-permute-start.7) | collective-permute-done | bytes 608288 | tf_op jit(solution)/shard_map/ppermute | solution.py:115
  196.3 2.4 %multiply_reduce_fusion.2 = f32[528]{0:T(1024)S(1)} fusion(bf16[528,576]{1,0:T(8,128)(2,1)} %collective-permute-done.8, bf16[528,576]{1,0:T(8,128)(2,1)} %collective-permute-done.7, bf16[528,576]{1,0:T(8,128)(2,1)S(1)} %collective-permute-done.6, bf16[528,2304]{1,0:T(8,128)(2,1)} %fusion.23, s32[]{:T(128)S(6)} %select_n.118), kind=kLoop, calls=%fused_computation.41 | loop fusion | flops 2736624 | bytes 2435140 | tf_op jit(solution)/shard_map/reduce_sum | solution.py:162
  198.7 1.3 collective-permute-start.10
  200.0 2.9 %collective-permute-start.11 = (f32[528]{0:T(1024)S(1)}, f32[528]{0:T(1024)S(1)}, u32[]{:S(2)}, u32[]{:S(2)}) collective-permute-start(f32[528]{0:T(1024)S(1)} %multiply_reduce_fusion.2), channel_id=1, source_target_pairs={{0,3},{1,0},{2,1},{3,2},{4,7},{5,4},{6,5},{7,6},{8,11},{9,8},{10,9... | collective-permute-start | bytes 6344 | tf_op jit(solution)/shard_map/ppermute | solution.py:124
  202.9 0.8 dynamic_slice.23
  203.7 2.9 %collective-permute-done.9 = f32[528]{0:T(1024)S(1)} collective-permute-done((f32[528]{0:T(1024)S(1)}, f32[528]{0:T(1024)S(1)}, u32[]{:S(2)}, u32[]{:S(2)}) %collective-permute-start.9) | collective-permute-done | bytes 2144 | tf_op jit(solution)/shard_map/ppermute | solution.py:124
  206.6 3.9 %add_convert_fusion = bf16[528,576]{1,0:T(8,128)(2,1)} fusion(f32[528,2304]{1,0:T(8,128)} %get-tuple-element.18, s32[]{:T(128)S(6)} %select_n.118, f32[576]{0:T(1024)S(1)} %dynamic_slice.23, f32[528]{0:T(1024)S(1)} %add_rsqrt_fusion, bf16[528,576]{1,0:T(8,128)(2,1)} %collective-permute-done.8, bf16[528,576]{1,0:T(8,128)(2,1)} %collective-permute-done.7, ...), kind=kLoop, calls=%fused_computation.40 | loop fusion | flops 3345408 | bytes 4262212 | tf_op jit(solution)/shard_map/convert_element_type | solution.py:166
  (50 shorter events, 0.2 us)
Async XLA Ops:
  6.5 34.7 %copy-start = (bf16[512,2304]{1,0:T(8,128)(2,1)S(1)}, bf16[512,2304]{1,0:T(8,128)(2,1)}, u32[]{:S(2)}) copy-start(bf16[512,2304]{1,0:T(8,128)(2,1)} %param.23) | copy-start | bytes 7077892
  6.5 3.2 %slice-start = ((bf16[528,512]{1,0:T(8,128)(2,1)}), bf16[512,512]{1,0:T(8,128)(2,1)S(1)}, s32[]{:S(2)}) async-start(bf16[528,512]{1,0:T(8,128)(2,1)} %param.16), calls=%async_computation.1 | async-start | bytes 1048576 | tf_op jit(solution)/shard_map/slice | solution.py:35
  6.5 119.5 %all-gather.2.cloned.1.call-start = ((), (), s32[]{:S(2)}) async-start(), calls=%async_computation | async-start | bytes 32845824 | tf_op jit(solution)/shard_map/all_gather | solution.py:144
  6.5 3.4 %copy-start.6 = (s32[17,32]{1,0:T(8,128)S(1)}, s32[17,32]{1,0:T(8,128)}, u32[]{:S(2)}) copy-start(s32[17,32]{1,0:T(8,128)} %param.21) | copy-start | bytes 6532
  14.5 4.5 %copy-start.7 = (s32[16]{0:T(128)S(1)}, s32[16]{0:T(128)}, u32[]{:S(2)}) copy-start(s32[16]{0:T(128)} %param.19) | copy-start | bytes 196
  14.5 5.4 %slice-start.1 = ((bf16[528,512]{1,0:T(8,128)(2,1)}), bf16[16,512]{1,0:T(8,128)(2,1)S(1)}, s32[]{:S(2)}) async-start(bf16[528,512]{1,0:T(8,128)(2,1)} %param.16), calls=%async_computation.2 | async-start | bytes 32768 | tf_op jit(solution)/shard_map/slice | solution.py:36
  19.6 4.8 %slice-start.2 = ((s8[5242880]{0:T(1024)(128)(4,1)}), s8[4194304]{0:T(1024)(128)(4,1)S(1)}, s32[]{:S(2)}) async-start(s8[5242880]{0:T(1024)(128)(4,1)} %bitcast.139), calls=%async_computation.3 | async-start | bytes 8388608
  19.8 4.5 %slice-start.3 = ((s8[5242880]{0:T(1024)(128)(4,1)}), s8[1048576]{0:T(1024)(128)(4,1)S(1)}, s32[]{:S(2)}) async-start(s8[5242880]{0:T(1024)(128)(4,1)} %bitcast.139), calls=%async_computation.4 | async-start | bytes 2097152
  24.3 3.9 %copy-start.3 = (bf16[32,128,256]{2,1,0:T(8,128)(2,1)S(1)}, bf16[32,128,256]{2,1,0:T(8,128)(2,1)}, u32[]{:S(2)}) copy-start(bf16[32,128,256]{2,1,0:T(8,128)(2,1)} %gather_fusion.1) | copy-start | bytes 6291460
  28.2 6.7 %copy-start.2 = (bf16[32,128,256]{2,1,0:T(8,128)(2,1)S(1)}, bf16[32,128,256]{2,1,0:T(8,128)(2,1)}, u32[]{:S(2)}) copy-start(bf16[32,128,256]{2,1,0:T(8,128)(2,1)} %gather_fusion) | copy-start | bytes 6291460
  47.3 17.8 %collective-permute-start = (bf16[132,2304]{1,0:T(8,128)(2,1)}, bf16[132,2304]{1,0:T(8,128)(2,1)S(1)}, u32[]{:S(2)}, u32[]{:S(2)}) collective-permute-start(bf16[132,2304]{1,0:T(8,128)(2,1)} %get-tuple-element.19), channel_id=1, source_target_pairs={{0,1},{1,2},{2,3},{3,0},{4,5},{5,6},{6,7},{7,4},{8,9},{9,10},{10,1... | collective-permute-start | bytes 1824776 | tf_op jit(solution)/shard_map/ppermute | solution.py:97
  49.7 29.8 %collective-permute-start.1 = (bf16[132,2304]{1,0:T(8,128)(2,1)}, bf16[132,2304]{1,0:T(8,128)(2,1)}, u32[]{:S(2)}, u32[]{:S(2)}) collective-permute-start(bf16[132,2304]{1,0:T(8,128)(2,1)} %get-tuple-element.21), channel_id=1, source_target_pairs={{0,2},{1,3},{2,0},{3,1},{4,6},{5,7},{6,4},{7,5},{8,10},{9,11},{10,... | collective-permute-start | bytes 1824776 | tf_op jit(solution)/shard_map/ppermute | solution.py:97
  52.4 27.1 %collective-permute-start.2 = (bf16[132,2304]{1,0:T(8,128)(2,1)}, bf16[132,2304]{1,0:T(8,128)(2,1)}, u32[]{:S(2)}, u32[]{:S(2)}) collective-permute-start(bf16[132,2304]{1,0:T(8,128)(2,1)} %get-tuple-element.20), channel_id=1, source_target_pairs={{0,3},{1,0},{2,1},{3,2},{4,7},{5,4},{6,5},{7,6},{8,11},{9,8},{10,9... | collective-permute-start | bytes 1824776 | tf_op jit(solution)/shard_map/ppermute | solution.py:97
  65.2 14.3 %copy-start.4 = (bf16[132,2304]{1,0:T(8,128)(2,1)}, bf16[132,2304]{1,0:T(8,128)(2,1)S(1)}, u32[]{:S(2)}) copy-start(bf16[132,2304]{1,0:T(8,128)(2,1)S(1)} %collective-permute-done) | copy-start | bytes 1824772
  81.3 16.0 %collective-permute-start.3 = (bf16[132,2304]{1,0:T(8,128)(2,1)S(1)}, bf16[132,2304]{1,0:T(8,128)(2,1)S(1)}, u32[]{:S(2)}, u32[]{:S(2)}) collective-permute-start(bf16[132,2304]{1,0:T(8,128)(2,1)S(1)} %add_convert_fusion.1), channel_id=1, source_target_pairs={{0,1},{1,2},{2,3},{3,0},{4,5},{5,6},{6,7},{7,4},{8,9},{9,10},{10,1... | collective-permute-start | bytes 1824776 | tf_op jit(solution)/shard_map/ppermute | solution.py:102
  82.7 29.9 %collective-permute-start.4 = (bf16[132,2304]{1,0:T(8,128)(2,1)S(1)}, bf16[132,2304]{1,0:T(8,128)(2,1)S(1)}, u32[]{:S(2)}, u32[]{:S(2)}) collective-permute-start(bf16[132,2304]{1,0:T(8,128)(2,1)S(1)} %add_convert_fusion.1), channel_id=1, source_target_pairs={{0,2},{1,3},{2,0},{3,1},{4,6},{5,7},{6,4},{7,5},{8,10},{9,11},{10,... | collective-permute-start | bytes 1824776 | tf_op jit(solution)/shard_map/ppermute | solution.py:102
  85.6 27.1 %collective-permute-start.5 = (bf16[132,2304]{1,0:T(8,128)(2,1)S(1)}, bf16[132,2304]{1,0:T(8,128)(2,1)S(1)}, u32[]{:S(2)}, u32[]{:S(2)}) collective-permute-start(bf16[132,2304]{1,0:T(8,128)(2,1)S(1)} %add_convert_fusion.1), channel_id=1, source_target_pairs={{0,3},{1,0},{2,1},{3,2},{4,7},{5,4},{6,5},{7,6},{8,11},{9,8},{10,9... | collective-permute-start | bytes 1824776 | tf_op jit(solution)/shard_map/ppermute | solution.py:102
  117.2 2.6 %copy-start.5 = (f32[2304]{0:T(1024)S(1)}, f32[2304]{0:T(1024)}, u32[]{:S(2)}) copy-start(f32[2304]{0:T(1024)} %param.24) | copy-start | bytes 27652
  119.7 6.3 %copy-start.8 = (f32[2304]{0:T(1024)S(1)}, f32[2304]{0:T(1024)}, u32[]{:S(2)}) copy-start(f32[2304]{0:T(1024)} %param.25) | copy-start | bytes 27652
  163.4 17.3 %collective-permute-start.6 = (bf16[528,576]{1,0:T(8,128)(2,1)S(1)}, bf16[528,576]{1,0:T(8,128)(2,1)S(1)}, u32[]{:S(2)}, u32[]{:S(2)}) collective-permute-start(bf16[528,576]{1,0:T(8,128)(2,1)S(1)} %get-tuple-element.22), channel_id=1, source_target_pairs={{0,1},{1,2},{2,3},{3,0},{4,5},{5,6},{6,7},{7,4},{8,9},{9,10},{10,1... | collective-permute-start | bytes 1824776 | tf_op jit(solution)/shard_map/ppermute | solution.py:115
  164.8 31.5 %collective-permute-start.7 = (bf16[528,576]{1,0:T(8,128)(2,1)S(1)}, bf16[528,576]{1,0:T(8,128)(2,1)}, u32[]{:S(2)}, u32[]{:S(2)}) collective-permute-start(bf16[528,576]{1,0:T(8,128)(2,1)S(1)} %get-tuple-element.24), channel_id=1, source_target_pairs={{0,2},{1,3},{2,0},{3,1},{4,6},{5,7},{6,4},{7,5},{8,10},{9,11},{10,... | collective-permute-start | bytes 1824776 | tf_op jit(solution)/shard_map/ppermute | solution.py:115
  167.3 29.0 %collective-permute-start.8 = (bf16[528,576]{1,0:T(8,128)(2,1)S(1)}, bf16[528,576]{1,0:T(8,128)(2,1)}, u32[]{:S(2)}, u32[]{:S(2)}) collective-permute-start(bf16[528,576]{1,0:T(8,128)(2,1)S(1)} %get-tuple-element.23), channel_id=1, source_target_pairs={{0,3},{1,0},{2,1},{3,2},{4,7},{5,4},{6,5},{7,6},{8,11},{9,8},{10,9... | collective-permute-start | bytes 1824776 | tf_op jit(solution)/shard_map/ppermute | solution.py:115
  196.3 14.2 %copy-start.1 = (bf16[512,2304]{1,0:T(8,128)(2,1)S(1)}, bf16[512,2304]{1,0:T(8,128)(2,1)}, u32[]{:S(2)}) copy-start(bf16[512,2304]{1,0:T(8,128)(2,1)} %param.23) | copy-start | bytes 7077892
  198.7 5.0 %collective-permute-start.10 = (f32[528]{0:T(1024)S(1)}, f32[528]{0:T(1024)S(1)}, u32[]{:S(2)}, u32[]{:S(2)}) collective-permute-start(f32[528]{0:T(1024)S(1)} %multiply_reduce_fusion.2), channel_id=1, source_target_pairs={{0,2},{1,3},{2,0},{3,1},{4,6},{5,7},{6,4},{7,5},{8,10},{9,11},{10,... | collective-permute-start | bytes 6344 | tf_op jit(solution)/shard_map/ppermute | solution.py:124
  200.0 3.7 %collective-permute-start.11 = (f32[528]{0:T(1024)S(1)}, f32[528]{0:T(1024)S(1)}, u32[]{:S(2)}, u32[]{:S(2)}) collective-permute-start(f32[528]{0:T(1024)S(1)} %multiply_reduce_fusion.2), channel_id=1, source_target_pairs={{0,3},{1,0},{2,1},{3,2},{4,7},{5,4},{6,5},{7,6},{8,11},{9,8},{10,9... | collective-permute-start | bytes 6344 | tf_op jit(solution)/shard_map/ppermute | solution.py:124
  202.9 3.7 %collective-permute-start.9 = (f32[528]{0:T(1024)S(1)}, f32[528]{0:T(1024)S(1)}, u32[]{:S(2)}, u32[]{:S(2)}) collective-permute-start(f32[528]{0:T(1024)S(1)} %multiply_reduce_fusion.2), channel_id=1, source_target_pairs={{0,1},{1,2},{2,3},{3,0},{4,5},{5,6},{6,7},{7,4},{8,9},{9,10},{10,1... | collective-permute-start | bytes 6344 | tf_op jit(solution)/shard_map/ppermute | solution.py:124
Sparse Core Ops, SparseCore 0:
  9.7 112.9 all-gather.1

commit v7 on v6

--- a/solution.py
+++ b/solution.py
@@ -104,18 +104,6 @@
     return jnp.take(jnp.stack(pieces), order, axis=0).reshape(partial.shape)
 
 
-def ring_scatter(partial, axis):
-    count = lax.axis_size(axis)
-    me = lax.axis_index(axis)
-    width = partial.shape[1] // count
-    total = lax.dynamic_slice_in_dim(partial, me * width, width, 1).astype(jnp.float32)
-    for shift in range(1, count):
-        sent = lax.dynamic_slice_in_dim(partial, ((me + shift) % count) * width, width, 1)
-        pairs = [(j, (j + shift) % count) for j in range(count)]
-        total = total + lax.ppermute(sent, axis, pairs).astype(jnp.float32)
-    return total
-
-
 def ring_total(value, axis):
     count = lax.axis_size(axis)
     total = value
@@ -123,6 +111,26 @@
         pairs = [(j, (j + shift) % count) for j in range(count)]
         total = total + lax.ppermute(value, axis, pairs)
     return total
+
+
+def down_scatter(act, down, axis):
+    count = lax.axis_size(axis)
+    me = lax.axis_index(axis)
+    width = down.shape[0] // count
+
+    def block(index):
+        rows = lax.dynamic_slice_in_dim(down, index * width, width, 0)
+        return lax.dot_general(
+            act, rows, (((1,), (1,)), ((), ())), preferred_element_type=jnp.float32
+        )
+
+    total = None
+    for shift in range(1, count):
+        sent = block((me + shift) % count).astype(jnp.bfloat16)
+        pairs = [(j, (j + shift) % count) for j in range(count)]
+        received = lax.ppermute(sent, axis, pairs).astype(jnp.float32)
+        total = received if total is None else total + received
+    return total + block(me).astype(jnp.bfloat16).astype(jnp.float32)
 
 
 def per_device(
@@ -153,10 +161,8 @@
     gate = jnp.dot(normed, weights[0], preferred_element_type=jnp.float32)
     up_part = jnp.dot(normed, weights[1], preferred_element_type=jnp.float32)
     act = (jax.nn.gelu(gate, approximate=True) * up_part).astype(jnp.bfloat16)
-    partial_out = lax.dot_general(
-        act, weights[2], (((1,), (1,)), ((), ())), preferred_element_type=jnp.float32
-    )
-    total = ring_scatter(partial_out.astype(jnp.bfloat16), "mlp")
+    act = lax.optimization_barrier(act)
+    total = down_scatter(act, weights[2], "mlp")
     width = total.shape[1]
     first = lax.axis_index("mlp") * width
     square = ring_total(jnp.sum(total * total, axis=-1), "mlp")[:, None]

time: 219 us -> 216 us (0.986)
  local copies, waits for them, and re-layouts: 19.5 us -> 23.2 us
  waiting for transfers between devices: 84.9 us -> 82 us
  other arithmetic: 23 us -> 20.4 us
    slice x0 -> x1, local copies, waits for them, and re-layouts: none -> 6.38 us  [per_device(): total = down_scatter(act, weights[2], 'mlp')]
    ppermute x3, waiting for transfers between devices: 29 us -> 26.1 us  [down_scatter(): received = lax.ppermute(sent, axis, pairs).astype(jnp.float32)]
    dynamic_slice x1 -> x0, local copies, waits for them, and re-layouts: 2.66 us -> none  [ring_scatter(): lax.dynamic_slice_in_dim(partial, (me + shift) % count * width, width, 1)]
    reduce_sum x1 -> x0, other arithmetic: 2.36 us -> none  [per_device(): square = ring_total(jnp.sum(total * total, axis=-1), 'mlp')[:, None]]
    dot_general x1 -> x5, matrix products: 22.1 us -> 23.3 us  [the longest x4 12.9 us: block(): lax.dot_general(act, rows, (((1,), (1,)), ((), ())), preferred_element_ty...]
  transfers between devices with their start and end apart: 13 -> 13, of which waited for: 7 -> 9; matrix products, arithmetic and copies ran while one was open for 25% -> 28% of each run, Pallas kernels for 0% -> 0%
where the time goes in v7:
time: 216 us; the launch traced here: 215 us
  waiting for transfers between devices  82 us (38%)
  matrix products  56.3 us (26%)
  local copies, waits for them, and re-layouts  23.2 us (11%)
  other arithmetic  20.4 us (9%)
  starting transfers between devices  18.3 us (8%)
  between operations  14.5 us (7%)
    ppermute x3, waiting for transfers between devices, ring_sum(): pieces.append(lax.ppermute(reduced, axis, pairs))  26.9 us
    ppermute x3, waiting for transfers between devices, ring_sum(): total = total + lax.ppermute(sent, axis, pairs).astype(jnp.float32)  26.1 us
    ppermute x3, waiting for transfers between devices, down_scatter(): received = lax.ppermute(sent, axis, pairs).astype(jnp.float32)  26.1 us
    dot_general x4, matrix products, block(): lax.dot_general(act, rows, (((1,), (1,)), ((), ())), preferred_element_ty...  12.9 us
    dot_general x1, matrix products, per_device(): gate = jnp.dot(normed, weights[0], preferred_element_type=jnp.float32)  10.6 us
    dot_general x1, matrix products, per_device(): up_part = jnp.dot(normed, weights[1], preferred_element_type=jnp.float32)  10.4 us
    reduce_sum x2, other arithmetic, rms(): jnp.mean(values * values, axis=-1, keepdims=True) + EPS  7.13 us
    dot_general x1, matrix products, attend(): jnp.einsum('rghd,tgd->rght', pre_q, pre_keys, preferred_element_type=jnp....  6.71 us
  transfers between devices with their start and end apart: 13, of which 9 were waited for; matrix products, arithmetic and copies ran while one was open for 28% of the time, Pallas kernels for 0%

profile of v7, /device:TPU:1, one launch (start us, length us, event | category | flops | bytes accessed | tf_op | source)
XLA Modules:
  0.0 214.6 jit_solution(12423699526512979317)
XLA Ops:
  6.5 2.4 %pad_maximum_fusion.1 = bf16[3,72,2304]{2,1,0:T(8,128)(2,1)} fusion(bf16[1,72,2304]{2,1,0:T(8,128)(2,1)} %bitcast.166, bf16[1,72,2304]{2,1,0:T(8,128)(2,1)} %bitcast.167, bf16[1,72,2304]{2,1,0:T(8,128)(2,1)} %bitcast.168), kind=kLoop, calls=%fused_computation.63 | loop fusion | flops 995328 | bytes 1990656 | tf_op jit(solution)/shard_map/stack | solution.py:153
  9.7 0.2 copy.35
  10.0 4.5 %gather_fusion.1 = bf16[32,128,256]{2,1,0:T(8,128)(2,1)} fusion(bf16[80,128,256]{2,1,0:T(8,128)(2,1)} %param.17, s32[1024]{0:T(1024)S(1)} %pad_clamp_fusion.1), kind=kCustom, calls=%fused_computation.1 | custom fusion | bytes 4194432 | tf_op jit(solution)/shard_map/gather | solution.py:39
  14.5 4.5 %gather_fusion = bf16[32,128,256]{2,1,0:T(8,128)(2,1)} fusion(bf16[80,128,256]{2,1,0:T(8,128)(2,1)} %param.18, s32[1024]{0:T(1024)S(1)} %pad_clamp_fusion.1), kind=kCustom, calls=%fused_computation | custom fusion | bytes 4194432 | tf_op jit(solution)/shard_map/gather | solution.py:40
  19.1 0.2 select_reduce_fusion
  19.3 0.2 add.199
  19.6 0.3 fusion.60
  19.8 4.5 %fusion.77 = (f32[16,2]{0,1:T(2,128)S(1)}, bf16[16,1,2,10240]{3,0,2,1:T(8,128)(2,1)S(1)}) fusion(bf16[10240,256,1]{1,0,2:T(8,128)(2,1)} %bitcast.157, bf16[2,2,8,256]{3,2,1,0:T(8,128)(2,1)S(1)} %bitcast.156, pred[16,10240]{1,0:T(8,128)(4,1)S(1)} %fusion.60), kind=kOutput, calls=%fused_computation.108 | convolution fusion | flops 169410528 | bytes 6078592 | tf_op jit(solution)/shard_map/rghd,tgd->rght/dot_general | solution.py:71
  24.3 2.1 fusion.54
  26.5 1.7 iota_compare_fusion
  28.2 6.7 %fusion = (f32[512,2]{0,1:T(2,128)S(1)}, f32[4096,512,2]{1,0,2:T(8,128)S(1)}) fusion(pred[512,4096]{0,1:T(8,128)(4,1)S(1)} %iota_compare_fusion, bf16[4096,256,1]{1,0,2:T(8,128)(2,1)S(1)} %bitcast.155, bf16[512,2,256]{0,2,1:T(8,128)(2,1)S(1)} %bitcast.165), kind=kOutput, calls=%fused_computation.4 | convolution fusion | flops 2164259840 | bytes 21499904 | tf_op jit(solution)/shard_map/rghd,tgd->rght/dot_general | solution.py:43
  34.9 6.2 %fusion.57 = bf16[512,1,2,256]{0,3,2,1:T(8,128)(2,1)S(1)} fusion(bf16[4096,256,1]{1,0,2:T(8,128)(2,1)S(1)} %bitcast.154, f32[4096,512,2]{1,0,2:T(8,128)S(1)} %get-tuple-element.25, pred[512,4096]{0,1:T(8,128)(4,1)S(1)} %iota_compare_fusion, f32[512,2]{0,1:T(2,128)S(1)} %get-tuple-element.24), kind=kOutput, calls=%fused_computation.64 | convolution fusion | flops 2164785152 | bytes 21499904 | tf_op jit(solution)/shard_map/rght,tgd->rghd/dot_general | solution.py:49
  41.2 2.9 %convolution_convert_fusion = bf16[528,2304]{1,0:T(8,128)(2,1)} fusion(bf16[528,512]{0,1:T(8,128)(2,1)S(1)} %bitcast.161, bf16[512,2304]{1,0:T(8,128)(2,1)S(1)} %copy-done), kind=kOutput, calls=%fused_computation.34 | convolution fusion | flops 1246924800 | bytes 5332992 | tf_op jit(solution)/shard_map/dot_general | solution.py:157
  44.1 1.9 reshape.305
  46.0 1.3 select_bitcast_fusion.2
  47.3 2.4 %collective-permute-start = (bf16[132,2304]{1,0:T(8,128)(2,1)}, bf16[132,2304]{1,0:T(8,128)(2,1)S(1)}, u32[]{:S(2)}, u32[]{:S(2)}) collective-permute-start(bf16[132,2304]{1,0:T(8,128)(2,1)} %get-tuple-element.19), channel_id=1, source_target_pairs={{0,1},{1,2},{2,3},{3,0},{4,5},{5,6},{6,7},{7,4},{8,9},{9,10},{10,1... | collective-permute-start | bytes 1824776 | tf_op jit(solution)/shard_map/ppermute | solution.py:97
  49.7 2.7 %collective-permute-start.1 = (bf16[132,2304]{1,0:T(8,128)(2,1)}, bf16[132,2304]{1,0:T(8,128)(2,1)}, u32[]{:S(2)}, u32[]{:S(2)}) collective-permute-start(bf16[132,2304]{1,0:T(8,128)(2,1)} %get-tuple-element.21), channel_id=1, source_target_pairs={{0,2},{1,3},{2,0},{3,1},{4,6},{5,7},{6,4},{7,5},{8,10},{9,11},{10,... | collective-permute-start | bytes 1824776 | tf_op jit(solution)/shard_map/ppermute | solution.py:97
  52.4 1.0 collective-permute-start.2
  53.4 11.8 %collective-permute-done = bf16[132,2304]{1,0:T(8,128)(2,1)S(1)} collective-permute-done((bf16[132,2304]{1,0:T(8,128)(2,1)}, bf16[132,2304]{1,0:T(8,128)(2,1)S(1)}, u32[]{:S(2)}, u32[]{:S(2)}) %collective-permute-start) | collective-permute-done | bytes 608288 | tf_op jit(solution)/shard_map/ppermute | solution.py:97
  65.2 14.3 %collective-permute-done.1 = bf16[132,2304]{1,0:T(8,128)(2,1)} collective-permute-done((bf16[132,2304]{1,0:T(8,128)(2,1)}, bf16[132,2304]{1,0:T(8,128)(2,1)}, u32[]{:S(2)}, u32[]{:S(2)}) %collective-permute-start.1) | collective-permute-done | bytes 608288 | tf_op jit(solution)/shard_map/ppermute | solution.py:97
  79.5 1.8 add_convert_fusion.1
  81.3 1.4 collective-permute-start.3
  82.7 2.8 %collective-permute-start.4 = (bf16[132,2304]{1,0:T(8,128)(2,1)S(1)}, bf16[132,2304]{1,0:T(8,128)(2,1)S(1)}, u32[]{:S(2)}, u32[]{:S(2)}) collective-permute-start(bf16[132,2304]{1,0:T(8,128)(2,1)S(1)} %add_convert_fusion.1), channel_id=1, source_target_pairs={{0,2},{1,3},{2,0},{3,1},{4,6},{5,7},{6,4},{7,5},{8,10},{9,11},{10,... | collective-permute-start | bytes 1824776 | tf_op jit(solution)/shard_map/ppermute | solution.py:102
  85.8 11.6 %collective-permute-done.3 = bf16[132,2304]{1,0:T(8,128)(2,1)S(1)} collective-permute-done((bf16[132,2304]{1,0:T(8,128)(2,1)S(1)}, bf16[132,2304]{1,0:T(8,128)(2,1)S(1)}, u32[]{:S(2)}, u32[]{:S(2)}) %collective-permute-start.3) | collective-permute-done | bytes 608288 | tf_op jit(solution)/shard_map/ppermute | solution.py:102
  97.3 15.3 %collective-permute-done.4 = bf16[132,2304]{1,0:T(8,128)(2,1)S(1)} collective-permute-done((bf16[132,2304]{1,0:T(8,128)(2,1)S(1)}, bf16[132,2304]{1,0:T(8,128)(2,1)S(1)}, u32[]{:S(2)}, u32[]{:S(2)}) %collective-permute-start.4) | collective-permute-done | bytes 608288 | tf_op jit(solution)/shard_map/ppermute | solution.py:102
  112.7 1.8 pad_maximum_fusion
  114.4 2.7 %gather_fusion.2 = bf16[4,132,2304]{2,1,0:T(8,128)(2,1)S(1)} fusion(bf16[4,132,2304]{2,1,0:T(8,128)(2,1)} %pad_maximum_fusion, s32[1024]{0:T(1024)S(1)} %pad_clamp_fusion), kind=kCustom, calls=%fused_computation.2 | custom fusion | bytes 4866064 | tf_op jit(solution)/shard_map/jit(_take)/gather | solution.py:104
  117.2 1.7 gather.18
  118.9 0.8 multiply_reduce_fusion
  119.8 6.3 %multiply_reduce_fusion.1 = (f32[528]{0:T(1024)S(1)}, f32[528,2304]{1,0:T(8,128)}) fusion(f32[2304]{0:T(1024)S(1)} %copy-done.9, f32[528]{0:T(1024)S(1)} %rsqrt.24, bf16[528,2304]{1,0:T(8,128)(2,1)} %gather.18, pred[528]{0:T(1024)(128)(4,1)S(1)} %broadcast_in_dim.86, bf16[528,2304]{1,0:T(8,128)(2,1)} %param.22), kind=kLoop, calls=%fused_computation.31 | loop fusion | flops 9731568 | bytes 9746064 | tf_op jit(solution)/shard_map/reduce_sum | solution.py:19
  126.1 10.6 %fusion.20 = f32[528,2304]{1,0:T(8,128)S(1)} fusion(bf16[3,2304,2304]{2,1,0:T(8,128)(2,1)} %all-gather.2.cloned.1.call-done, f32[528,2304]{1,0:T(8,128)} %get-tuple-element.18, f32[2304]{0:T(1024)S(1)} %copy-done.12, f32[528]{0:T(1024)S(1)} %add_rsqrt_fusion.1), kind=kOutput, calls=%fused_computation.29 | convolution fusion | flops 5619068928 | bytes 20360256 | tf_op jit(solution)/shard_map/dot_general | solution.py:161
  136.8 10.4 %fusion.21 = bf16[528,2304]{1,0:T(8,128)(2,1)S(1)} fusion(f32[528,2304]{1,0:T(8,128)S(1)} %fusion.20, bf16[3,2304,2304]{2,1,0:T(8,128)(2,1)} %all-gather.2.cloned.1.call-done, f32[528,2304]{1,0:T(8,128)S(1)} %copy-done.3, f32[2304]{0:T(1024)S(1)} %copy-done.12, f32[528]{0:T(1024)S(1)} %add_rsqrt_fusion.1), kind=kOutput, calls=%fused_computation.33 | convolution fusion | flops 5611769856 | bytes 22793280 | tf_op jit(solution)/shard_map/dot_general | solution.py:162
  147.2 6.4 %slice.48 = bf16[1,2304,2304]{2,1,0:T(8,128)(2,1)S(1)} slice(bf16[3,2304,2304]{2,1,0:T(8,128)(2,1)} %all-gather.2.cloned.1.call-done), slice={[2:3], [0:2304], [0:2304]} | slice | bytes 21233664 | tf_op jit(solution)/shard_map/slice | solution.py:165
  153.6 2.1 fusion.37
  155.6 1.2 collective-permute-start.6
  156.9 2.9 %fusion.40 = bf16[528,576]{1,0:T(8,128)(2,1)} fusion(bf16[528,2304]{1,0:T(8,128)(2,1)S(1)} %fusion.21, bf16[1,2304,2304]{2,1,0:T(8,128)(2,1)S(1)} %slice.48, s32[]{:T(128)S(6)} %select_n.120), kind=kOutput, calls=%fused_computation.50 | convolution fusion | flops 1401725952 | bytes 5695492 | tf_op jit(solution)/shard_map/dot_general | solution.py:123
  159.8 2.5 %collective-permute-start.7 = (bf16[528,576]{1,0:T(8,128)(2,1)}, bf16[528,576]{1,0:T(8,128)(2,1)S(1)}, u32[]{:S(2)}, u32[]{:S(2)}) collective-permute-start(bf16[528,576]{1,0:T(8,128)(2,1)} %fusion.40), channel_id=1, source_target_pairs={{0,2},{1,3},{2,0},{3,1},{4,6},{5,7},{6,4},{7,5},{8,10},{9,11},{10,... | collective-permute-start | bytes 1824776 | tf_op jit(solution)/shard_map/ppermute | solution.py:131
  162.3 2.9 %fusion.43 = bf16[528,576]{1,0:T(8,128)(2,1)} fusion(bf16[528,2304]{1,0:T(8,128)(2,1)S(1)} %fusion.21, bf16[1,2304,2304]{2,1,0:T(8,128)(2,1)S(1)} %slice.48, s32[]{:T(128)S(6)} %select_n.121), kind=kOutput, calls=%fused_computation.51 | convolution fusion | flops 1401725952 | bytes 5695492 | tf_op jit(solution)/shard_map/dot_general | solution.py:123
  165.2 7.5 %collective-permute-done.6 = bf16[528,576]{1,0:T(8,128)(2,1)S(1)} collective-permute-done((bf16[528,576]{1,0:T(8,128)(2,1)S(1)}, bf16[528,576]{1,0:T(8,128)(2,1)S(1)}, u32[]{:S(2)}, u32[]{:S(2)}) %collective-permute-start.6) | collective-permute-done | bytes 608288 | tf_op jit(solution)/shard_map/ppermute | solution.py:131
  172.8 15.5 %collective-permute-done.7 = bf16[528,576]{1,0:T(8,128)(2,1)S(1)} collective-permute-done((bf16[528,576]{1,0:T(8,128)(2,1)}, bf16[528,576]{1,0:T(8,128)(2,1)S(1)}, u32[]{:S(2)}, u32[]{:S(2)}) %collective-permute-start.7) | collective-permute-done | bytes 608288 | tf_op jit(solution)/shard_map/ppermute | solution.py:131
  188.3 3.1 %collective-permute-done.8 = bf16[528,576]{1,0:T(8,128)(2,1)S(1)} collective-permute-done((bf16[528,576]{1,0:T(8,128)(2,1)}, bf16[528,576]{1,0:T(8,128)(2,1)S(1)}, u32[]{:S(2)}, u32[]{:S(2)}) %collective-permute-start.8) | collective-permute-done | bytes 608288 | tf_op jit(solution)/shard_map/ppermute | solution.py:131
  191.3 5.0 %multiply_reduce_fusion.2 = (f32[528]{0:T(1024)S(1)}, f32[528,576]{1,0:T(8,128)S(1)}) fusion(bf16[528,576]{1,0:T(8,128)(2,1)S(1)} %collective-permute-done.8, bf16[528,576]{1,0:T(8,128)(2,1)S(1)} %collective-permute-done.7, bf16[528,576]{1,0:T(8,128)(2,1)S(1)} %collective-permute-done.6, bf16[528,2304]{1,0:T(8,128)(2,1)} %copy-done.13, ...), kind=kOutput, calls=%fused_computation.55 | convolution fusion | flops 1404462592 | bytes 8130628 | tf_op jit(solution)/shard_map/dot_general | solution.py:123
  196.3 1.6 collective-permute-start.10
  197.9 2.7 %collective-permute-start.11 = (f32[528]{0:T(1024)S(1)}, f32[528]{0:T(1024)S(1)}, u32[]{:S(2)}, u32[]{:S(2)}) collective-permute-start(f32[528]{0:T(1024)S(1)} %get-tuple-element.26), channel_id=1, source_target_pairs={{0,3},{1,0},{2,1},{3,2},{4,7},{5,4},{6,5},{7,6},{8,11},{9,8},{10,9... | collective-permute-start | bytes 6344 | tf_op jit(solution)/shard_map/ppermute | solution.py:112
  200.6 0.8 dynamic_slice.35
  201.4 0.2 collective-permute-done.11
  201.6 2.7 %collective-permute-done.9 = f32[528]{0:T(1024)S(1)} collective-permute-done((f32[528]{0:T(1024)S(1)}, f32[528]{0:T(1024)S(1)}, u32[]{:S(2)}, u32[]{:S(2)}) %collective-permute-start.9) | collective-permute-done | bytes 2144 | tf_op jit(solution)/shard_map/ppermute | solution.py:112
  204.3 3.5 %add_convert_fusion = bf16[528,576]{1,0:T(8,128)(2,1)} fusion(f32[528,2304]{1,0:T(8,128)} %get-tuple-element.18, s32[]{:T(128)S(6)} %select_n.118, f32[576]{0:T(1024)S(1)} %dynamic_slice.35, f32[528]{0:T(1024)S(1)} %add_rsqrt_fusion, f32[528,576]{1,0:T(8,128)S(1)} %get-tuple-element.27, bf16[528,576]{1,0:T(8,128)(2,1)} %copy-done.7, ...), kind=kLoop, calls=%fused_computation.54 | loop fusion | flops 3041280 | bytes 4870468 | tf_op jit(solution)/shard_map/convert_element_type | solution.py:172
  (63 shorter events, 0.6 us)
Async XLA Ops:
  6.5 34.6 %copy-start = (bf16[512,2304]{1,0:T(8,128)(2,1)S(1)}, bf16[512,2304]{1,0:T(8,128)(2,1)}, u32[]{:S(2)}) copy-start(bf16[512,2304]{1,0:T(8,128)(2,1)} %param.23) | copy-start | bytes 7077892
  6.5 3.2 %slice-start = ((bf16[528,512]{1,0:T(8,128)(2,1)}), bf16[512,512]{1,0:T(8,128)(2,1)S(1)}, s32[]{:S(2)}) async-start(bf16[528,512]{1,0:T(8,128)(2,1)} %param.16), calls=%async_computation.1 | async-start | bytes 1048576 | tf_op jit(solution)/shard_map/slice | solution.py:35
  6.5 119.6 %all-gather.2.cloned.1.call-start = ((), (), s32[]{:S(2)}) async-start(), calls=%async_computation | async-start | bytes 32845824 | tf_op jit(solution)/shard_map/all_gather | solution.py:152
  6.5 3.4 %copy-start.10 = (s32[17,32]{1,0:T(8,128)S(1)}, s32[17,32]{1,0:T(8,128)}, u32[]{:S(2)}) copy-start(s32[17,32]{1,0:T(8,128)} %param.21) | copy-start | bytes 6532
  14.5 4.5 %copy-start.11 = (s32[16]{0:T(128)S(1)}, s32[16]{0:T(128)}, u32[]{:S(2)}) copy-start(s32[16]{0:T(128)} %param.19) | copy-start | bytes 196
  14.5 5.3 %slice-start.1 = ((bf16[528,512]{1,0:T(8,128)(2,1)}), bf16[16,512]{1,0:T(8,128)(2,1)S(1)}, s32[]{:S(2)}) async-start(bf16[528,512]{1,0:T(8,128)(2,1)} %param.16), calls=%async_computation.2 | async-start | bytes 32768 | tf_op jit(solution)/shard_map/slice | solution.py:36
  19.5 4.8 %slice-start.2 = ((s8[5242880]{0:T(1024)(128)(4,1)}), s8[4194304]{0:T(1024)(128)(4,1)S(1)}, s32[]{:S(2)}) async-start(s8[5242880]{0:T(1024)(128)(4,1)} %bitcast.158), calls=%async_computation.3 | async-start | bytes 8388608
  19.8 4.5 %slice-start.3 = ((s8[5242880]{0:T(1024)(128)(4,1)}), s8[1048576]{0:T(1024)(128)(4,1)S(1)}, s32[]{:S(2)}) async-start(s8[5242880]{0:T(1024)(128)(4,1)} %bitcast.158), calls=%async_computation.4 | async-start | bytes 2097152
  24.3 3.9 %copy-start.5 = (bf16[32,128,256]{2,1,0:T(8,128)(2,1)S(1)}, bf16[32,128,256]{2,1,0:T(8,128)(2,1)}, u32[]{:S(2)}) copy-start(bf16[32,128,256]{2,1,0:T(8,128)(2,1)} %gather_fusion.1) | copy-start | bytes 6291460
  28.2 6.7 %copy-start.4 = (bf16[32,128,256]{2,1,0:T(8,128)(2,1)S(1)}, bf16[32,128,256]{2,1,0:T(8,128)(2,1)}, u32[]{:S(2)}) copy-start(bf16[32,128,256]{2,1,0:T(8,128)(2,1)} %gather_fusion) | copy-start | bytes 6291460
  47.3 17.9 %collective-permute-start = (bf16[132,2304]{1,0:T(8,128)(2,1)}, bf16[132,2304]{1,0:T(8,128)(2,1)S(1)}, u32[]{:S(2)}, u32[]{:S(2)}) collective-permute-start(bf16[132,2304]{1,0:T(8,128)(2,1)} %get-tuple-element.19), channel_id=1, source_target_pairs={{0,1},{1,2},{2,3},{3,0},{4,5},{5,6},{6,7},{7,4},{8,9},{9,10},{10,1... | collective-permute-start | bytes 1824776 | tf_op jit(solution)/shard_map/ppermute | solution.py:97
  49.7 29.8 %collective-permute-start.1 = (bf16[132,2304]{1,0:T(8,128)(2,1)}, bf16[132,2304]{1,0:T(8,128)(2,1)}, u32[]{:S(2)}, u32[]{:S(2)}) collective-permute-start(bf16[132,2304]{1,0:T(8,128)(2,1)} %get-tuple-element.21), channel_id=1, source_target_pairs={{0,2},{1,3},{2,0},{3,1},{4,6},{5,7},{6,4},{7,5},{8,10},{9,11},{10,... | collective-permute-start | bytes 1824776 | tf_op jit(solution)/shard_map/ppermute | solution.py:97
  52.4 27.1 %collective-permute-start.2 = (bf16[132,2304]{1,0:T(8,128)(2,1)}, bf16[132,2304]{1,0:T(8,128)(2,1)}, u32[]{:S(2)}, u32[]{:S(2)}) collective-permute-start(bf16[132,2304]{1,0:T(8,128)(2,1)} %get-tuple-element.20), channel_id=1, source_target_pairs={{0,3},{1,0},{2,1},{3,2},{4,7},{5,4},{6,5},{7,6},{8,11},{9,8},{10,9... | collective-permute-start | bytes 1824776 | tf_op jit(solution)/shard_map/ppermute | solution.py:97
  65.2 14.3 %copy-start.8 = (bf16[132,2304]{1,0:T(8,128)(2,1)}, bf16[132,2304]{1,0:T(8,128)(2,1)S(1)}, u32[]{:S(2)}) copy-start(bf16[132,2304]{1,0:T(8,128)(2,1)S(1)} %collective-permute-done) | copy-start | bytes 1824772
  81.3 16.0 %collective-permute-start.3 = (bf16[132,2304]{1,0:T(8,128)(2,1)S(1)}, bf16[132,2304]{1,0:T(8,128)(2,1)S(1)}, u32[]{:S(2)}, u32[]{:S(2)}) collective-permute-start(bf16[132,2304]{1,0:T(8,128)(2,1)S(1)} %add_convert_fusion.1), channel_id=1, source_target_pairs={{0,1},{1,2},{2,3},{3,0},{4,5},{5,6},{6,7},{7,4},{8,9},{9,10},{10,1... | collective-permute-start | bytes 1824776 | tf_op jit(solution)/shard_map/ppermute | solution.py:102
  82.7 29.9 %collective-permute-start.4 = (bf16[132,2304]{1,0:T(8,128)(2,1)S(1)}, bf16[132,2304]{1,0:T(8,128)(2,1)S(1)}, u32[]{:S(2)}, u32[]{:S(2)}) collective-permute-start(bf16[132,2304]{1,0:T(8,128)(2,1)S(1)} %add_convert_fusion.1), channel_id=1, source_target_pairs={{0,2},{1,3},{2,0},{3,1},{4,6},{5,7},{6,4},{7,5},{8,10},{9,11},{10,... | collective-permute-start | bytes 1824776 | tf_op jit(solution)/shard_map/ppermute | solution.py:102
  85.6 27.1 %collective-permute-start.5 = (bf16[132,2304]{1,0:T(8,128)(2,1)S(1)}, bf16[132,2304]{1,0:T(8,128)(2,1)S(1)}, u32[]{:S(2)}, u32[]{:S(2)}) collective-permute-start(bf16[132,2304]{1,0:T(8,128)(2,1)S(1)} %add_convert_fusion.1), channel_id=1, source_target_pairs={{0,3},{1,0},{2,1},{3,2},{4,7},{5,4},{6,5},{7,6},{8,11},{9,8},{10,9... | collective-permute-start | bytes 1824776 | tf_op jit(solution)/shard_map/ppermute | solution.py:102
  117.2 2.6 %copy-start.9 = (f32[2304]{0:T(1024)S(1)}, f32[2304]{0:T(1024)}, u32[]{:S(2)}) copy-start(f32[2304]{0:T(1024)} %param.24) | copy-start | bytes 27652
  119.8 6.3 %copy-start.12 = (f32[2304]{0:T(1024)S(1)}, f32[2304]{0:T(1024)}, u32[]{:S(2)}) copy-start(f32[2304]{0:T(1024)} %param.25) | copy-start | bytes 27652
  126.1 10.6 %copy-start.3 = (f32[528,2304]{1,0:T(8,128)S(1)}, f32[528,2304]{1,0:T(8,128)}, u32[]{:S(2)}) copy-start(f32[528,2304]{1,0:T(8,128)} %get-tuple-element.18) | copy-start | bytes 14598148
  147.1 15.2 %copy-start.13 = (bf16[528,2304]{1,0:T(8,128)(2,1)}, bf16[528,2304]{1,0:T(8,128)(2,1)S(1)}, u32[]{:S(2)}) copy-start(bf16[528,2304]{1,0:T(8,128)(2,1)S(1)} %fusion.21) | copy-start | bytes 7299076
  153.5 8.8 %copy-start.2 = (bf16[1,2304,2304]{2,1,0:T(8,128)(2,1)}, bf16[1,2304,2304]{2,1,0:T(8,128)(2,1)S(1)}, u32[]{:S(2)}) copy-start(bf16[1,2304,2304]{2,1,0:T(8,128)(2,1)S(1)} %slice.48) | copy-start | bytes 31850500
  155.6 17.1 %collective-permute-start.6 = (bf16[528,576]{1,0:T(8,128)(2,1)S(1)}, bf16[528,576]{1,0:T(8,128)(2,1)S(1)}, u32[]{:S(2)}, u32[]{:S(2)}) collective-permute-start(bf16[528,576]{1,0:T(8,128)(2,1)S(1)} %fusion.37), channel_id=1, source_target_pairs={{0,1},{1,2},{2,3},{3,0},{4,5},{5,6},{6,7},{7,4},{8,9},{9,10},{10,1... | collective-permute-start | bytes 1824776 | tf_op jit(solution)/shard_map/ppermute | solution.py:131
  159.8 28.4 %collective-permute-start.7 = (bf16[528,576]{1,0:T(8,128)(2,1)}, bf16[528,576]{1,0:T(8,128)(2,1)S(1)}, u32[]{:S(2)}, u32[]{:S(2)}) collective-permute-start(bf16[528,576]{1,0:T(8,128)(2,1)} %fusion.40), channel_id=1, source_target_pairs={{0,2},{1,3},{2,0},{3,1},{4,6},{5,7},{6,4},{7,5},{8,10},{9,11},{10,... | collective-permute-start | bytes 1824776 | tf_op jit(solution)/shard_map/ppermute | solution.py:131
  165.2 26.1 %collective-permute-start.8 = (bf16[528,576]{1,0:T(8,128)(2,1)}, bf16[528,576]{1,0:T(8,128)(2,1)S(1)}, u32[]{:S(2)}, u32[]{:S(2)}) collective-permute-start(bf16[528,576]{1,0:T(8,128)(2,1)} %fusion.43), channel_id=1, source_target_pairs={{0,3},{1,0},{2,1},{3,2},{4,7},{5,4},{6,5},{7,6},{8,11},{9,8},{10,9... | collective-permute-start | bytes 1824776 | tf_op jit(solution)/shard_map/ppermute | solution.py:131
  188.3 8.0 %copy-start.6 = (bf16[528,576]{1,0:T(8,128)(2,1)}, bf16[528,576]{1,0:T(8,128)(2,1)S(1)}, u32[]{:S(2)}) copy-start(bf16[528,576]{1,0:T(8,128)(2,1)S(1)} %collective-permute-done.7) | copy-start | bytes 1824772
  191.3 5.0 %copy-start.7 = (bf16[528,576]{1,0:T(8,128)(2,1)}, bf16[528,576]{1,0:T(8,128)(2,1)S(1)}, u32[]{:S(2)}) copy-start(bf16[528,576]{1,0:T(8,128)(2,1)S(1)} %collective-permute-done.8) | copy-start | bytes 1824772
  196.3 5.1 %collective-permute-start.10 = (f32[528]{0:T(1024)S(1)}, f32[528]{0:T(1024)S(1)}, u32[]{:S(2)}, u32[]{:S(2)}) collective-permute-start(f32[528]{0:T(1024)S(1)} %get-tuple-element.26), channel_id=1, source_target_pairs={{0,2},{1,3},{2,0},{3,1},{4,6},{5,7},{6,4},{7,5},{8,10},{9,11},{10,... | collective-permute-start | bytes 6344 | tf_op jit(solution)/shard_map/ppermute | solution.py:112
  197.9 3.7 %collective-permute-start.11 = (f32[528]{0:T(1024)S(1)}, f32[528]{0:T(1024)S(1)}, u32[]{:S(2)}, u32[]{:S(2)}) collective-permute-start(f32[528]{0:T(1024)S(1)} %get-tuple-element.26), channel_id=1, source_target_pairs={{0,3},{1,0},{2,1},{3,2},{4,7},{5,4},{6,5},{7,6},{8,11},{9,8},{10,9... | collective-permute-start | bytes 6344 | tf_op jit(solution)/shard_map/ppermute | solution.py:112
  200.6 3.7 %collective-permute-start.9 = (f32[528]{0:T(1024)S(1)}, f32[528]{0:T(1024)S(1)}, u32[]{:S(2)}, u32[]{:S(2)}) collective-permute-start(f32[528]{0:T(1024)S(1)} %get-tuple-element.26), channel_id=1, source_target_pairs={{0,1},{1,2},{2,3},{3,0},{4,5},{5,6},{6,7},{7,4},{8,9},{9,10},{10,1... | collective-permute-start | bytes 6344 | tf_op jit(solution)/shard_map/ppermute | solution.py:112
  204.3 3.5 %copy-start.1 = (bf16[512,2304]{1,0:T(8,128)(2,1)S(1)}, bf16[512,2304]{1,0:T(8,128)(2,1)}, u32[]{:S(2)}) copy-start(bf16[512,2304]{1,0:T(8,128)(2,1)} %param.23) | copy-start | bytes 7077892
Sparse Core Ops, SparseCore 0:
  9.7 112.9 all-gather.1

commit v8 on v7

--- a/solution.py
+++ b/solution.py
@@ -116,10 +116,10 @@
 def down_scatter(act, down, axis):
     count = lax.axis_size(axis)
     me = lax.axis_index(axis)
-    width = down.shape[0] // count
+    width = down.shape[1] // count
 
     def block(index):
-        rows = lax.dynamic_slice_in_dim(down, index * width, width, 0)
+        rows = lax.dynamic_slice(down, (2, index * width, 0), (1, width, down.shape[2]))[0]
         return lax.dot_general(
             act, rows, (((1,), (1,)), ((), ())), preferred_element_type=jnp.float32
         )
@@ -157,12 +157,12 @@
         jnp.dot(attended, o_weight, preferred_element_type=jnp.float32).astype(jnp.bfloat16), "mlp"
     ).astype(jnp.float32)
     resid = hidden_in.astype(jnp.float32) + rms(projected, attn_gain)
-    normed = rms(resid, ffn_in_gain).astype(jnp.bfloat16)
+    normed = lax.optimization_barrier(rms(resid, ffn_in_gain).astype(jnp.bfloat16))
     gate = jnp.dot(normed, weights[0], preferred_element_type=jnp.float32)
     up_part = jnp.dot(normed, weights[1], preferred_element_type=jnp.float32)
     act = (jax.nn.gelu(gate, approximate=True) * up_part).astype(jnp.bfloat16)
     act = lax.optimization_barrier(act)
-    total = down_scatter(act, weights[2], "mlp")
+    total = down_scatter(act, weights, "mlp")
     width = total.shape[1]
     first = lax.axis_index("mlp") * width
     square = ring_total(jnp.sum(total * total, axis=-1), "mlp")[:, None]

time: 216 us -> 223 us (1.032)
  matrix products: 56.3 us -> 62 us
    slice x1 -> x0, local copies, waits for them, and re-layouts: 6.38 us -> none  [per_device(): total = down_scatter(act, weights[2], 'mlp')]
    dot_general x4, matrix products: 12.9 us -> 19.1 us  [block(): lax.dot_general(act, rows, (((1,), (1,)), ((), ())), preferred_element_ty...]
    gather x2, local copies, waits for them, and re-layouts: 4.39 us -> 6.91 us  [ring_sum(): return jnp.take(jnp.stack(pieces), order, axis=0).reshape(partial.shape)]
    unnamed x33 -> x31, local copies, waits for them, and re-layouts: 0.29 us -> 2.53 us
  transfers between devices with their start and end apart: 13 -> 13, of which waited for: 9 -> 9; matrix products, arithmetic and copies ran while one was open for 28% -> 31% of each run, Pallas kernels for 0% -> 0%
where the time goes in v8:
time: 223 us; the launch traced here: 221 us
  waiting for transfers between devices  80.4 us (36%)
  matrix products  62 us (28%)
  local copies, waits for them, and re-layouts  22.7 us (10%)
  other arithmetic  22.6 us (10%)
  starting transfers between devices  18.5 us (8%)
  between operations  14.4 us (6%)
    ppermute x3, waiting for transfers between devices, ring_sum(): pieces.append(lax.ppermute(reduced, axis, pairs))  27.2 us
    ppermute x3, waiting for transfers between devices, ring_sum(): total = total + lax.ppermute(sent, axis, pairs).astype(jnp.float32)  26 us
    ppermute x3, waiting for transfers between devices, down_scatter(): received = lax.ppermute(sent, axis, pairs).astype(jnp.float32)  24.2 us
    dot_general x4, matrix products, block(): lax.dot_general(act, rows, (((1,), (1,)), ((), ())), preferred_element_ty...  19.1 us
    dot_general x1, matrix products, per_device(): gate = jnp.dot(normed, weights[0], preferred_element_type=jnp.float32)  10.4 us
    dot_general x1, matrix products, per_device(): up_part = jnp.dot(normed, weights[1], preferred_element_type=jnp.float32)  10.2 us
    gather x2, local copies, waits for them, and re-layouts, ring_sum(): return jnp.take(jnp.stack(pieces), order, axis=0).reshape(partial.shape)  6.91 us
    dot_general x1, matrix products, attend(): jnp.einsum('rghd,tgd->rght', pre_q, pre_keys, preferred_element_type=jnp....  6.7 us
  transfers between devices with their start and end apart: 13, of which 9 were waited for; matrix products, arithmetic and copies ran while one was open for 31% of the time, Pallas kernels for 0%

profile of v8, /device:TPU:1, one launch (start us, length us, event | category | flops | bytes accessed | tf_op | source)
XLA Modules:
  0.0 220.6 jit_solution(6198298556023993276)
XLA Ops:
  6.5 2.4 %pad_maximum_fusion.1 = bf16[3,72,2304]{2,1,0:T(8,128)(2,1)} fusion(bf16[1,72,2304]{2,1,0:T(8,128)(2,1)} %bitcast.168, bf16[1,72,2304]{2,1,0:T(8,128)(2,1)} %bitcast.169, bf16[1,72,2304]{2,1,0:T(8,128)(2,1)} %bitcast.170), kind=kLoop, calls=%fused_computation.63 | loop fusion | flops 995328 | bytes 1990656 | tf_op jit(solution)/shard_map/stack | solution.py:153
  10.0 4.5 %gather_fusion.1 = bf16[32,128,256]{2,1,0:T(8,128)(2,1)} fusion(bf16[80,128,256]{2,1,0:T(8,128)(2,1)} %param.17, s32[1024]{0:T(1024)S(1)} %pad_clamp_fusion.1), kind=kCustom, calls=%fused_computation.1 | custom fusion | bytes 4194432 | tf_op jit(solution)/shard_map/gather | solution.py:39
  14.5 4.5 %gather_fusion = bf16[32,128,256]{2,1,0:T(8,128)(2,1)} fusion(bf16[80,128,256]{2,1,0:T(8,128)(2,1)} %param.18, s32[1024]{0:T(1024)S(1)} %pad_clamp_fusion.1), kind=kCustom, calls=%fused_computation | custom fusion | bytes 4194432 | tf_op jit(solution)/shard_map/gather | solution.py:40
  19.1 0.2 select_reduce_fusion
  19.3 0.2 add.199
  19.6 0.3 fusion.60
  19.9 4.5 %fusion.81 = (f32[16,2]{0,1:T(2,128)S(1)}, bf16[16,1,2,10240]{3,0,2,1:T(8,128)(2,1)S(1)}) fusion(bf16[10240,256,1]{1,0,2:T(8,128)(2,1)} %bitcast.159, bf16[2,2,8,256]{3,2,1,0:T(8,128)(2,1)S(1)} %bitcast.158, pred[16,10240]{1,0:T(8,128)(4,1)S(1)} %fusion.60), kind=kOutput, calls=%fused_computation.112 | convolution fusion | flops 169410528 | bytes 6078592 | tf_op jit(solution)/shard_map/rghd,tgd->rght/dot_general | solution.py:71
  24.4 2.1 fusion.54
  26.5 1.7 iota_compare_fusion
  28.2 6.7 %fusion = (f32[512,2]{0,1:T(2,128)S(1)}, f32[4096,512,2]{1,0,2:T(8,128)S(1)}) fusion(pred[512,4096]{0,1:T(8,128)(4,1)S(1)} %iota_compare_fusion, bf16[4096,256,1]{1,0,2:T(8,128)(2,1)S(1)} %bitcast.157, bf16[512,2,256]{0,2,1:T(8,128)(2,1)S(1)} %bitcast.167), kind=kOutput, calls=%fused_computation.4 | convolution fusion | flops 2164259840 | bytes 21499904 | tf_op jit(solution)/shard_map/rghd,tgd->rght/dot_general | solution.py:43
  35.0 6.2 %fusion.57 = bf16[512,1,2,256]{0,3,2,1:T(8,128)(2,1)S(1)} fusion(bf16[4096,256,1]{1,0,2:T(8,128)(2,1)S(1)} %bitcast.156, f32[4096,512,2]{1,0,2:T(8,128)S(1)} %get-tuple-element.25, pred[512,4096]{0,1:T(8,128)(4,1)S(1)} %iota_compare_fusion, f32[512,2]{0,1:T(2,128)S(1)} %get-tuple-element.24), kind=kOutput, calls=%fused_computation.64 | convolution fusion | flops 2164785152 | bytes 21499904 | tf_op jit(solution)/shard_map/rght,tgd->rghd/dot_general | solution.py:49
  41.2 3.0 %convolution_convert_fusion = bf16[528,2304]{1,0:T(8,128)(2,1)} fusion(bf16[528,512]{0,1:T(8,128)(2,1)S(1)} %bitcast.163, bf16[512,2304]{1,0:T(8,128)(2,1)S(1)} %copy-done), kind=kOutput, calls=%fused_computation.34 | convolution fusion | flops 1246924800 | bytes 5332992 | tf_op jit(solution)/shard_map/dot_general | solution.py:157
  44.2 3.0 %reshape.301 = bf16[4,132,2304]{2,1,0:T(8,128)(2,1)} reshape(bf16[528,2304]{1,0:T(8,128)(2,1)} %convolution_convert_fusion) | data formatting | bytes 4866048 | tf_op jit(solution)/shard_map/reshape | solution.py:92
  47.2 2.7 %select_bitcast_fusion.2 = (bf16[132,2304]{1,0:T(8,128)(2,1)}, bf16[132,2304]{1,0:T(8,128)(2,1)S(1)}, bf16[132,2304]{1,0:T(8,128)(2,1)}) fusion(bf16[4,132,2304]{2,1,0:T(8,128)(2,1)} %reshape.301, s32[]{:T(128)S(6)} %select_n.134, pred[]{:T(512)S(6)} %and.74, s32[]{:T(128)S(6)} %select_n.138, pred[]{:T(512)S(6)} %and.76, s32[]{:T(128)S(6)} %select_n.136, ...), kind=kLoop, calls=%fused_computation.72 | loop fusion | flops 912384 | bytes 3649551 | tf_op jit(solution)/shard_map/jit(_take)/select_n | solution.py:95
  49.8 2.4 %collective-permute-start = (bf16[132,2304]{1,0:T(8,128)(2,1)}, bf16[132,2304]{1,0:T(8,128)(2,1)S(1)}, u32[]{:S(2)}, u32[]{:S(2)}) collective-permute-start(bf16[132,2304]{1,0:T(8,128)(2,1)} %get-tuple-element.19), channel_id=1, source_target_pairs={{0,1},{1,2},{2,3},{3,0},{4,5},{5,6},{6,7},{7,4},{8,9},{9,10},{10,1... | collective-permute-start | bytes 1824776 | tf_op jit(solution)/shard_map/ppermute | solution.py:97
  52.2 2.7 %collective-permute-start.1 = (bf16[132,2304]{1,0:T(8,128)(2,1)}, bf16[132,2304]{1,0:T(8,128)(2,1)S(1)}, u32[]{:S(2)}, u32[]{:S(2)}) collective-permute-start(bf16[132,2304]{1,0:T(8,128)(2,1)} %get-tuple-element.21), channel_id=1, source_target_pairs={{0,2},{1,3},{2,0},{3,1},{4,6},{5,7},{6,4},{7,5},{8,10},{9,11},{10,... | collective-permute-start | bytes 1824776 | tf_op jit(solution)/shard_map/ppermute | solution.py:97
  54.9 1.0 collective-permute-start.2
  55.9 11.8 %collective-permute-done = bf16[132,2304]{1,0:T(8,128)(2,1)S(1)} collective-permute-done((bf16[132,2304]{1,0:T(8,128)(2,1)}, bf16[132,2304]{1,0:T(8,128)(2,1)S(1)}, u32[]{:S(2)}, u32[]{:S(2)}) %collective-permute-start) | collective-permute-done | bytes 608288 | tf_op jit(solution)/shard_map/ppermute | solution.py:97
  67.7 14.2 %collective-permute-done.1 = bf16[132,2304]{1,0:T(8,128)(2,1)S(1)} collective-permute-done((bf16[132,2304]{1,0:T(8,128)(2,1)}, bf16[132,2304]{1,0:T(8,128)(2,1)S(1)}, u32[]{:S(2)}, u32[]{:S(2)}) %collective-permute-start.1) | collective-permute-done | bytes 608288 | tf_op jit(solution)/shard_map/ppermute | solution.py:97
  81.9 1.5 add_convert_fusion.1
  83.4 1.1 collective-permute-start.3
  84.4 3.5 %collective-permute-start.4 = (bf16[132,2304]{1,0:T(8,128)(2,1)S(1)}, bf16[132,2304]{1,0:T(8,128)(2,1)S(1)}, u32[]{:S(2)}, u32[]{:S(2)}) collective-permute-start(bf16[132,2304]{1,0:T(8,128)(2,1)S(1)} %add_convert_fusion.1), channel_id=1, source_target_pairs={{0,2},{1,3},{2,0},{3,1},{4,6},{5,7},{6,4},{7,5},{8,10},{9,11},{10,... | collective-permute-start | bytes 1824776 | tf_op jit(solution)/shard_map/ppermute | solution.py:102
  88.1 11.7 %collective-permute-done.3 = bf16[132,2304]{1,0:T(8,128)(2,1)S(1)} collective-permute-done((bf16[132,2304]{1,0:T(8,128)(2,1)S(1)}, bf16[132,2304]{1,0:T(8,128)(2,1)S(1)}, u32[]{:S(2)}, u32[]{:S(2)}) %collective-permute-start.3) | collective-permute-done | bytes 608288 | tf_op jit(solution)/shard_map/ppermute | solution.py:102
  99.8 15.6 %collective-permute-done.4 = bf16[132,2304]{1,0:T(8,128)(2,1)S(1)} collective-permute-done((bf16[132,2304]{1,0:T(8,128)(2,1)S(1)}, bf16[132,2304]{1,0:T(8,128)(2,1)S(1)}, u32[]{:S(2)}, u32[]{:S(2)}) %collective-permute-start.4) | collective-permute-done | bytes 608288 | tf_op jit(solution)/shard_map/ppermute | solution.py:102
  115.3 1.8 pad_maximum_fusion
  117.2 3.9 %gather_fusion.2 = bf16[4,132,2304]{2,1,0:T(8,128)(2,1)} fusion(bf16[4,132,2304]{2,1,0:T(8,128)(2,1)} %pad_maximum_fusion, s32[1024]{0:T(1024)S(1)} %pad_clamp_fusion), kind=kCustom, calls=%fused_computation.2 | custom fusion | bytes 4866064 | tf_op jit(solution)/shard_map/jit(_take)/gather | solution.py:104
  121.0 3.0 %gather.18 = bf16[528,2304]{1,0:T(8,128)(2,1)} reshape(bf16[4,132,2304]{2,1,0:T(8,128)(2,1)} %gather_fusion.2) | data formatting | bytes 4866048 | tf_op jit(solution)/shard_map/jit(_take)/gather | solution.py:104
  124.1 2.5 %multiply_reduce_fusion = f32[4,132]{1,0:T(4,128)S(1)} fusion(bf16[4,132,2304]{2,1,0:T(8,128)(2,1)} %gather_fusion.2, pred[4]{0:T(512)(128)(4,1)S(1)} %compare_and_fusion), kind=kLoop, calls=%fused_computation.21 | loop fusion | flops 4865520 | bytes 2435140 | tf_op jit(solution)/shard_map/reduce_sum | solution.py:19
  126.7 3.9 %multiply_reduce_fusion.1 = (f32[528]{0:T(1024)S(1)}, f32[528,2304]{1,0:T(8,128)S(1)}) fusion(f32[2304]{0:T(1024)S(1)} %copy-done.8, f32[528]{0:T(1024)S(1)} %rsqrt.24, bf16[528,2304]{1,0:T(8,128)(2,1)} %gather.18, pred[528]{0:T(1024)(128)(4,1)S(1)} %broadcast_in_dim.86, bf16[528,2304]{1,0:T(8,128)(2,1)} %param.22), kind=kLoop, calls=%fused_computation.31 | loop fusion | flops 9731568 | bytes 9746064 | tf_op jit(solution)/shard_map/reduce_sum | solution.py:19
  130.6 2.2 %copy-done.2 = f32[528,2304]{1,0:T(8,128)} copy-done((f32[528,2304]{1,0:T(8,128)}, f32[528,2304]{1,0:T(8,128)S(1)}, u32[]{:S(2)}) %copy-start.2) | copy-done | bytes 4866072
  132.9 1.9 multiply_convert_fusion
  134.8 10.4 %fusion.20 = f32[528,2304]{1,0:T(8,128)S(1)} fusion(bf16[528,2304]{1,0:T(8,128)(2,1)} %multiply_convert_fusion, bf16[3,2304,2304]{2,1,0:T(8,128)(2,1)} %all-gather.2.cloned.1.call-done), kind=kOutput, calls=%fused_computation.29 | convolution fusion | flops 5615419392 | bytes 17915904 | tf_op jit(solution)/shard_map/dot_general | solution.py:161
  145.2 10.2 %fusion.21 = bf16[528,2304]{1,0:T(8,128)(2,1)S(1)} fusion(f32[528,2304]{1,0:T(8,128)S(1)} %fusion.20, bf16[528,2304]{1,0:T(8,128)(2,1)S(1)} %copy-done.3, bf16[3,2304,2304]{2,1,0:T(8,128)(2,1)} %all-gather.2.cloned.1.call-done), kind=kOutput, calls=%fused_computation.33 | convolution fusion | flops 5608120320 | bytes 20348928 | tf_op jit(solution)/shard_map/dot_general | solution.py:162
  155.3 4.7 %fusion.37 = bf16[528,576]{1,0:T(8,128)(2,1)S(1)} fusion(bf16[528,2304]{1,0:T(8,128)(2,1)S(1)} %fusion.21, bf16[3,2304,2304]{2,1,0:T(8,128)(2,1)} %all-gather.2.cloned.1.call-done, s32[]{:T(128)S(6)} %select_n.119), kind=kOutput, calls=%fused_computation.49 | convolution fusion | flops 1401725952 | bytes 5695492 | tf_op jit(solution)/shard_map/dot_general | solution.py:123
  160.1 1.0 collective-permute-start.6
  161.1 4.7 %fusion.40 = bf16[528,576]{1,0:T(8,128)(2,1)} fusion(bf16[528,2304]{1,0:T(8,128)(2,1)S(1)} %fusion.21, bf16[3,2304,2304]{2,1,0:T(8,128)(2,1)} %all-gather.2.cloned.1.call-done, s32[]{:T(128)S(6)} %select_n.120), kind=kOutput, calls=%fused_computation.50 | convolution fusion | flops 1401725952 | bytes 5695492 | tf_op jit(solution)/shard_map/dot_general | solution.py:123
  165.8 2.7 %collective-permute-start.7 = (bf16[528,576]{1,0:T(8,128)(2,1)}, bf16[528,576]{1,0:T(8,128)(2,1)S(1)}, u32[]{:S(2)}, u32[]{:S(2)}) collective-permute-start(bf16[528,576]{1,0:T(8,128)(2,1)} %fusion.40), channel_id=1, source_target_pairs={{0,2},{1,3},{2,0},{3,1},{4,6},{5,7},{6,4},{7,5},{8,10},{9,11},{10,... | collective-permute-start | bytes 1824776 | tf_op jit(solution)/shard_map/ppermute | solution.py:131
  168.6 4.7 %fusion.43 = bf16[528,576]{1,0:T(8,128)(2,1)} fusion(bf16[528,2304]{1,0:T(8,128)(2,1)S(1)} %fusion.21, bf16[3,2304,2304]{2,1,0:T(8,128)(2,1)} %all-gather.2.cloned.1.call-done, s32[]{:T(128)S(6)} %select_n.121), kind=kOutput, calls=%fused_computation.51 | convolution fusion | flops 1401725952 | bytes 5695492 | tf_op jit(solution)/shard_map/dot_general | solution.py:123
  173.2 3.8 %collective-permute-done.6 = bf16[528,576]{1,0:T(8,128)(2,1)S(1)} collective-permute-done((bf16[528,576]{1,0:T(8,128)(2,1)S(1)}, bf16[528,576]{1,0:T(8,128)(2,1)S(1)}, u32[]{:S(2)}, u32[]{:S(2)}) %collective-permute-start.6) | collective-permute-done | bytes 608288 | tf_op jit(solution)/shard_map/ppermute | solution.py:131
  177.0 16.2 %collective-permute-done.7 = bf16[528,576]{1,0:T(8,128)(2,1)S(1)} collective-permute-done((bf16[528,576]{1,0:T(8,128)(2,1)}, bf16[528,576]{1,0:T(8,128)(2,1)S(1)}, u32[]{:S(2)}, u32[]{:S(2)}) %collective-permute-start.7) | collective-permute-done | bytes 608288 | tf_op jit(solution)/shard_map/ppermute | solution.py:131
  193.2 4.3 %collective-permute-done.8 = bf16[528,576]{1,0:T(8,128)(2,1)S(1)} collective-permute-done((bf16[528,576]{1,0:T(8,128)(2,1)}, bf16[528,576]{1,0:T(8,128)(2,1)S(1)}, u32[]{:S(2)}, u32[]{:S(2)}) %collective-permute-start.8) | collective-permute-done | bytes 608288 | tf_op jit(solution)/shard_map/ppermute | solution.py:131
  197.5 5.0 %multiply_reduce_fusion.2 = (f32[528]{0:T(1024)S(1)}, f32[528,576]{1,0:T(8,128)S(1)}) fusion(bf16[528,576]{1,0:T(8,128)(2,1)S(1)} %collective-permute-done.8, bf16[528,576]{1,0:T(8,128)(2,1)S(1)} %collective-permute-done.7, bf16[528,576]{1,0:T(8,128)(2,1)S(1)} %collective-permute-done.6, bf16[528,2304]{1,0:T(8,128)(2,1)} %copy-done.12, ...), kind=kOutput, calls=%fused_computation.55 | convolution fusion | flops 1404462592 | bytes 8130628 | tf_op jit(solution)/shard_map/dot_general | solution.py:123
  202.5 1.4 collective-permute-start.10
  203.9 2.7 %collective-permute-start.11 = (f32[528]{0:T(1024)S(1)}, f32[528]{0:T(1024)S(1)}, u32[]{:S(2)}, u32[]{:S(2)}) collective-permute-start(f32[528]{0:T(1024)S(1)} %get-tuple-element.26), channel_id=1, source_target_pairs={{0,3},{1,0},{2,1},{3,2},{4,7},{5,4},{6,5},{7,6},{8,11},{9,8},{10,9... | collective-permute-start | bytes 6344 | tf_op jit(solution)/shard_map/ppermute | solution.py:112
  206.6 0.8 dynamic_slice.23
  207.4 0.4 collective-permute-done.11
  207.8 2.5 %collective-permute-done.9 = f32[528]{0:T(1024)S(1)} collective-permute-done((f32[528]{0:T(1024)S(1)}, f32[528]{0:T(1024)S(1)}, u32[]{:S(2)}, u32[]{:S(2)}) %collective-permute-start.9) | collective-permute-done | bytes 2144 | tf_op jit(solution)/shard_map/ppermute | solution.py:112
  210.3 3.5 %add_convert_fusion = bf16[528,576]{1,0:T(8,128)(2,1)} fusion(f32[528,2304]{1,0:T(8,128)} %copy-done.2, s32[]{:T(128)S(6)} %select_n.118, f32[576]{0:T(1024)S(1)} %dynamic_slice.23, f32[528]{0:T(1024)S(1)} %add_rsqrt_fusion, f32[528,576]{1,0:T(8,128)S(1)} %get-tuple-element.27, bf16[528,576]{1,0:T(8,128)(2,1)} %copy-done.7, bf16[528,576]{1,0:T(8,128)(2,1)} %copy-done.6, ...), kind=kLoop, calls=%fused_computation.54 | loop fusion | flops 3041280 | bytes 4870468 | tf_op jit(solution)/shard_map/convert_element_type | solution.py:172
  (61 shorter events, 0.8 us)
Async XLA Ops:
  6.5 34.7 %copy-start = (bf16[512,2304]{1,0:T(8,128)(2,1)S(1)}, bf16[512,2304]{1,0:T(8,128)(2,1)}, u32[]{:S(2)}) copy-start(bf16[512,2304]{1,0:T(8,128)(2,1)} %param.23) | copy-start | bytes 7077892
  6.5 3.2 %slice-start = ((bf16[528,512]{1,0:T(8,128)(2,1)}), bf16[512,512]{1,0:T(8,128)(2,1)S(1)}, s32[]{:S(2)}) async-start(bf16[528,512]{1,0:T(8,128)(2,1)} %param.16), calls=%async_computation.1 | async-start | bytes 1048576 | tf_op jit(solution)/shard_map/slice | solution.py:35
  6.5 128.2 %all-gather.2.cloned.1.call-start = ((), (), s32[]{:S(2)}) async-start(), calls=%async_computation | async-start | bytes 32845824 | tf_op jit(solution)/shard_map/all_gather | solution.py:152
  6.5 3.4 %copy-start.10 = (s32[17,32]{1,0:T(8,128)S(1)}, s32[17,32]{1,0:T(8,128)}, u32[]{:S(2)}) copy-start(s32[17,32]{1,0:T(8,128)} %param.21) | copy-start | bytes 6532
  14.5 4.5 %copy-start.11 = (s32[16]{0:T(128)S(1)}, s32[16]{0:T(128)}, u32[]{:S(2)}) copy-start(s32[16]{0:T(128)} %param.19) | copy-start | bytes 196
  14.5 5.3 %slice-start.1 = ((bf16[528,512]{1,0:T(8,128)(2,1)}), bf16[16,512]{1,0:T(8,128)(2,1)S(1)}, s32[]{:S(2)}) async-start(bf16[528,512]{1,0:T(8,128)(2,1)} %param.16), calls=%async_computation.2 | async-start | bytes 32768 | tf_op jit(solution)/shard_map/slice | solution.py:36
  19.6 4.8 %slice-start.2 = ((s8[5242880]{0:T(1024)(128)(4,1)}), s8[4194304]{0:T(1024)(128)(4,1)S(1)}, s32[]{:S(2)}) async-start(s8[5242880]{0:T(1024)(128)(4,1)} %bitcast.160), calls=%async_computation.3 | async-start | bytes 8388608
  19.8 4.5 %slice-start.3 = ((s8[5242880]{0:T(1024)(128)(4,1)}), s8[1048576]{0:T(1024)(128)(4,1)S(1)}, s32[]{:S(2)}) async-start(s8[5242880]{0:T(1024)(128)(4,1)} %bitcast.160), calls=%async_computation.4 | async-start | bytes 2097152
  24.3 3.9 %copy-start.5 = (bf16[32,128,256]{2,1,0:T(8,128)(2,1)S(1)}, bf16[32,128,256]{2,1,0:T(8,128)(2,1)}, u32[]{:S(2)}) copy-start(bf16[32,128,256]{2,1,0:T(8,128)(2,1)} %gather_fusion.1) | copy-start | bytes 6291460
  28.2 6.7 %copy-start.4 = (bf16[32,128,256]{2,1,0:T(8,128)(2,1)S(1)}, bf16[32,128,256]{2,1,0:T(8,128)(2,1)}, u32[]{:S(2)}) copy-start(bf16[32,128,256]{2,1,0:T(8,128)(2,1)} %gather_fusion) | copy-start | bytes 6291460
  49.8 17.9 %collective-permute-start = (bf16[132,2304]{1,0:T(8,128)(2,1)}, bf16[132,2304]{1,0:T(8,128)(2,1)S(1)}, u32[]{:S(2)}, u32[]{:S(2)}) collective-permute-start(bf16[132,2304]{1,0:T(8,128)(2,1)} %get-tuple-element.19), channel_id=1, source_target_pairs={{0,1},{1,2},{2,3},{3,0},{4,5},{5,6},{6,7},{7,4},{8,9},{9,10},{10,1... | collective-permute-start | bytes 1824776 | tf_op jit(solution)/shard_map/ppermute | solution.py:97
  52.2 29.7 %collective-permute-start.1 = (bf16[132,2304]{1,0:T(8,128)(2,1)}, bf16[132,2304]{1,0:T(8,128)(2,1)S(1)}, u32[]{:S(2)}, u32[]{:S(2)}) collective-permute-start(bf16[132,2304]{1,0:T(8,128)(2,1)} %get-tuple-element.21), channel_id=1, source_target_pairs={{0,2},{1,3},{2,0},{3,1},{4,6},{5,7},{6,4},{7,5},{8,10},{9,11},{10,... | collective-permute-start | bytes 1824776 | tf_op jit(solution)/shard_map/ppermute | solution.py:97
  54.9 27.0 %collective-permute-start.2 = (bf16[132,2304]{1,0:T(8,128)(2,1)S(1)}, bf16[132,2304]{1,0:T(8,128)(2,1)S(1)}, u32[]{:S(2)}, u32[]{:S(2)}) collective-permute-start(bf16[132,2304]{1,0:T(8,128)(2,1)S(1)} %get-tuple-element.20), channel_id=1, source_target_pairs={{0,3},{1,0},{2,1},{3,2},{4,7},{5,4},{6,5},{7,6},{8,11},{9,8},{10,9... | collective-permute-start | bytes 1824776 | tf_op jit(solution)/shard_map/ppermute | solution.py:97
  83.4 16.4 %collective-permute-start.3 = (bf16[132,2304]{1,0:T(8,128)(2,1)S(1)}, bf16[132,2304]{1,0:T(8,128)(2,1)S(1)}, u32[]{:S(2)}, u32[]{:S(2)}) collective-permute-start(bf16[132,2304]{1,0:T(8,128)(2,1)S(1)} %add_convert_fusion.1), channel_id=1, source_target_pairs={{0,1},{1,2},{2,3},{3,0},{4,5},{5,6},{6,7},{7,4},{8,9},{9,10},{10,1... | collective-permute-start | bytes 1824776 | tf_op jit(solution)/shard_map/ppermute | solution.py:102
  84.4 30.9 %collective-permute-start.4 = (bf16[132,2304]{1,0:T(8,128)(2,1)S(1)}, bf16[132,2304]{1,0:T(8,128)(2,1)S(1)}, u32[]{:S(2)}, u32[]{:S(2)}) collective-permute-start(bf16[132,2304]{1,0:T(8,128)(2,1)S(1)} %add_convert_fusion.1), channel_id=1, source_target_pairs={{0,2},{1,3},{2,0},{3,1},{4,6},{5,7},{6,4},{7,5},{8,10},{9,11},{10,... | collective-permute-start | bytes 1824776 | tf_op jit(solution)/shard_map/ppermute | solution.py:102
  87.9 27.4 %collective-permute-start.5 = (bf16[132,2304]{1,0:T(8,128)(2,1)S(1)}, bf16[132,2304]{1,0:T(8,128)(2,1)S(1)}, u32[]{:S(2)}, u32[]{:S(2)}) collective-permute-start(bf16[132,2304]{1,0:T(8,128)(2,1)S(1)} %add_convert_fusion.1), channel_id=1, source_target_pairs={{0,3},{1,0},{2,1},{3,2},{4,7},{5,4},{6,5},{7,6},{8,11},{9,8},{10,9... | collective-permute-start | bytes 1824776 | tf_op jit(solution)/shard_map/ppermute | solution.py:102
  121.0 5.7 %copy-start.8 = (f32[2304]{0:T(1024)S(1)}, f32[2304]{0:T(1024)}, u32[]{:S(2)}) copy-start(f32[2304]{0:T(1024)} %param.24) | copy-start | bytes 27652
  126.7 6.2 %copy-start.9 = (f32[2304]{0:T(1024)S(1)}, f32[2304]{0:T(1024)}, u32[]{:S(2)}) copy-start(f32[2304]{0:T(1024)} %param.25) | copy-start | bytes 27652
  130.6 2.3 %copy-start.2 = (f32[528,2304]{1,0:T(8,128)}, f32[528,2304]{1,0:T(8,128)S(1)}, u32[]{:S(2)}) copy-start(f32[528,2304]{1,0:T(8,128)S(1)} %get-tuple-element.18) | copy-start | bytes 14598148
  134.8 10.4 %copy-start.3 = (bf16[528,2304]{1,0:T(8,128)(2,1)S(1)}, bf16[528,2304]{1,0:T(8,128)(2,1)}, u32[]{:S(2)}) copy-start(bf16[528,2304]{1,0:T(8,128)(2,1)} %multiply_convert_fusion) | copy-start | bytes 7299076
  155.3 13.2 %copy-start.12 = (bf16[528,2304]{1,0:T(8,128)(2,1)}, bf16[528,2304]{1,0:T(8,128)(2,1)S(1)}, u32[]{:S(2)}) copy-start(bf16[528,2304]{1,0:T(8,128)(2,1)S(1)} %fusion.21) | copy-start | bytes 7299076
  160.1 17.0 %collective-permute-start.6 = (bf16[528,576]{1,0:T(8,128)(2,1)S(1)}, bf16[528,576]{1,0:T(8,128)(2,1)S(1)}, u32[]{:S(2)}, u32[]{:S(2)}) collective-permute-start(bf16[528,576]{1,0:T(8,128)(2,1)S(1)} %fusion.37), channel_id=1, source_target_pairs={{0,1},{1,2},{2,3},{3,0},{4,5},{5,6},{6,7},{7,4},{8,9},{9,10},{10,1... | collective-permute-start | bytes 1824776 | tf_op jit(solution)/shard_map/ppermute | solution.py:131
  165.8 27.4 %collective-permute-start.7 = (bf16[528,576]{1,0:T(8,128)(2,1)}, bf16[528,576]{1,0:T(8,128)(2,1)S(1)}, u32[]{:S(2)}, u32[]{:S(2)}) collective-permute-start(bf16[528,576]{1,0:T(8,128)(2,1)} %fusion.40), channel_id=1, source_target_pairs={{0,2},{1,3},{2,0},{3,1},{4,6},{5,7},{6,4},{7,5},{8,10},{9,11},{10,... | collective-permute-start | bytes 1824776 | tf_op jit(solution)/shard_map/ppermute | solution.py:131
  173.2 24.2 %collective-permute-start.8 = (bf16[528,576]{1,0:T(8,128)(2,1)}, bf16[528,576]{1,0:T(8,128)(2,1)S(1)}, u32[]{:S(2)}, u32[]{:S(2)}) collective-permute-start(bf16[528,576]{1,0:T(8,128)(2,1)} %fusion.43), channel_id=1, source_target_pairs={{0,3},{1,0},{2,1},{3,2},{4,7},{5,4},{6,5},{7,6},{8,11},{9,8},{10,9... | collective-permute-start | bytes 1824776 | tf_op jit(solution)/shard_map/ppermute | solution.py:131
  193.2 9.2 %copy-start.6 = (bf16[528,576]{1,0:T(8,128)(2,1)}, bf16[528,576]{1,0:T(8,128)(2,1)S(1)}, u32[]{:S(2)}) copy-start(bf16[528,576]{1,0:T(8,128)(2,1)S(1)} %collective-permute-done.7) | copy-start | bytes 1824772
  197.5 5.0 %copy-start.7 = (bf16[528,576]{1,0:T(8,128)(2,1)}, bf16[528,576]{1,0:T(8,128)(2,1)S(1)}, u32[]{:S(2)}) copy-start(bf16[528,576]{1,0:T(8,128)(2,1)S(1)} %collective-permute-done.8) | copy-start | bytes 1824772
  202.5 4.9 %collective-permute-start.10 = (f32[528]{0:T(1024)S(1)}, f32[528]{0:T(1024)S(1)}, u32[]{:S(2)}, u32[]{:S(2)}) collective-permute-start(f32[528]{0:T(1024)S(1)} %get-tuple-element.26), channel_id=1, source_target_pairs={{0,2},{1,3},{2,0},{3,1},{4,6},{5,7},{6,4},{7,5},{8,10},{9,11},{10,... | collective-permute-start | bytes 6344 | tf_op jit(solution)/shard_map/ppermute | solution.py:112
  203.9 3.9 %collective-permute-start.11 = (f32[528]{0:T(1024)S(1)}, f32[528]{0:T(1024)S(1)}, u32[]{:S(2)}, u32[]{:S(2)}) collective-permute-start(f32[528]{0:T(1024)S(1)} %get-tuple-element.26), channel_id=1, source_target_pairs={{0,3},{1,0},{2,1},{3,2},{4,7},{5,4},{6,5},{7,6},{8,11},{9,8},{10,9... | collective-permute-start | bytes 6344 | tf_op jit(solution)/shard_map/ppermute | solution.py:112
  206.6 3.7 %collective-permute-start.9 = (f32[528]{0:T(1024)S(1)}, f32[528]{0:T(1024)S(1)}, u32[]{:S(2)}, u32[]{:S(2)}) collective-permute-start(f32[528]{0:T(1024)S(1)} %get-tuple-element.26), channel_id=1, source_target_pairs={{0,1},{1,2},{2,3},{3,0},{4,5},{5,6},{6,7},{7,4},{8,9},{9,10},{10,1... | collective-permute-start | bytes 6344 | tf_op jit(solution)/shard_map/ppermute | solution.py:112
  210.3 3.5 %copy-start.1 = (bf16[512,2304]{1,0:T(8,128)(2,1)S(1)}, bf16[512,2304]{1,0:T(8,128)(2,1)}, u32[]{:S(2)}) copy-start(bf16[512,2304]{1,0:T(8,128)(2,1)} %param.23) | copy-start | bytes 7077892
Sparse Core Ops, SparseCore 0:
  9.7 112.9 all-gather.1
